TPU v7x, 256 devices: a whole 4x4x8 slice. The times are simulated.
256 devices in a mesh: group: 8 (over y, core), tile: 32 (over z, x).
Axes of the slice: x: 4, y: 4, z: 8, core: 2. Of those that a mesh axis runs over, the one named last changes fastest.
Arguments:
- radiance: bfloat16 [224, 3072, 1024], P(None, 'tile', 'group'), may hold values from -200 to 200
- valid_mask: int32 [3072, 1024], P('tile', 'group'), may hold values 0 or 1
Outputs:
- whitened: bfloat16 [224, 3072, 1024], P(None, 'tile', 'group')
- whitened_cov: float32 [224, 224], replicated
All inputs are finite; a program needn't handle non-finite values. No bound on the sum of `valid_mask` on one device may be relied on, other than what follows from the above.
Results may differ from a plain program's by a relative error of at most 0.0058.
Values may be sent and summed in bfloat16 or wider, within the bound.
No kernel may reach another device: no remote copies, remote signals or barrier semaphores. Data moves between devices by JAX's collectives and lax.ppermute only.
A program may use at most 128 MiB of HBM per device.

v0:
```python
import jax
import jax.numpy as jnp
from jax import lax
from jax.experimental import pallas as pl
from jax.experimental.pallas import tpu as pltpu
from jax.sharding import PartitionSpec as P


def padded_2(block, sides, width):
    for axis, dim in sides:
        count = lax.axis_size(axis)
        forward = [(i, i + 1) for i in range(count - 1)]
        backward = [(target, source) for source, target in forward]
        low = lax.ppermute(
            lax.slice_in_dim(block, block.shape[dim] - width, None, axis=dim), axis, forward
        )
        high = lax.ppermute(lax.slice_in_dim(block, 0, width, axis=dim), axis, backward)
        block = jnp.concatenate([low, block, high], axis=dim)
    return block


def smooth_noise(padded, rows, cols):
    field = padded.astype(jnp.float32)
    row_smooth = (
        field[:, 0:rows]
        + 4.0 * field[:, 1 : rows + 1]
        + 6.0 * field[:, 2 : rows + 2]
        + 4.0 * field[:, 3 : rows + 3]
        + field[:, 4 : rows + 4]
    ) / 16.0
    smooth = (
        row_smooth[:, :, 0:cols]
        + 4.0 * row_smooth[:, :, 1 : cols + 1]
        + 6.0 * row_smooth[:, :, 2 : cols + 2]
        + 4.0 * row_smooth[:, :, 3 : cols + 3]
        + row_smooth[:, :, 4 : cols + 4]
    ) / 16.0
    centre = field[:, 2 : rows + 2, 2 : cols + 2]
    noise = centre - 0.5 * (
        field[:, 1 : rows + 1, 2 : cols + 2] + field[:, 3 : rows + 3, 2 : cols + 2]
    )
    return (smooth, noise)


def flat_pairs(sizes, move):
    y_size, z_size, x_size = sizes
    pairs = []
    for y in range(y_size):
        for core in range(2):
            for z in range(z_size):
                for x in range(x_size):
                    y2, core2, z2, x2 = move(y, core, z, x)
                    source = ((y * 2 + core) * z_size + z) * x_size + x
                    target = ((y2 * 2 + core2) * z_size + z2) * x_size + x2
                    pairs.append((source, target))
    return pairs


SIZES = (4, 8, 4)
CORE_SWAP = flat_pairs(SIZES, lambda y, c, z, x: (y, 1 - c, z, x))
STAGES = (
    [flat_pairs(SIZES, lambda y, c, z, x, k=k: (y, c, z, x ^ k)) for k in (1, 2, 3)],
    [flat_pairs(SIZES, lambda y, c, z, x, k=k: (y ^ k, c, z, x)) for k in (1, 2, 3)],
    [flat_pairs(SIZES, lambda y, c, z, x, k=k: (y, c, z ^ k, x)) for k in (1, 2, 3)],
    [flat_pairs(SIZES, lambda y, c, z, x: (y, c, 7 - z, x))],
)
AXES = ("group", "tile")


def total_of(value):
    half = value.shape[0] // 2
    core = lax.axis_index("group") % 2
    own = lax.dynamic_slice_in_dim(value, core * half, half, axis=0)
    other = lax.dynamic_slice_in_dim(value, (1 - core) * half, half, axis=0)
    own = own + lax.ppermute(other, AXES, CORE_SWAP)
    for stage in STAGES:
        parts = [lax.ppermute(own, AXES, pairs) for pairs in stage]
        if len(parts) == 1:
            own = own + parts[0]
        else:
            own = (own + parts[0]) + (parts[1] + parts[2])
    other = lax.ppermute(own, AXES, CORE_SWAP)
    first = core == 0
    return jnp.concatenate(
        [jnp.where(first, own, other), jnp.where(first, other, own)], axis=0
    )


def split_three(value):
    first = value.astype(jnp.bfloat16)
    rest = value - first.astype(jnp.float32)
    second = rest.astype(jnp.bfloat16)
    third = (rest - second.astype(jnp.float32)).astype(jnp.bfloat16)
    return (first, second, third)


def inverse_factor_kernel(cov_ref, out_ref, work_ref):
    size = cov_ref.shape[0]
    width = work_ref.shape[1]
    sub = lax.broadcasted_iota(jnp.int32, (8, 128), 0)
    lane = lax.broadcasted_iota(jnp.int32, (8, width), 1)
    sub_wide = lax.broadcasted_iota(jnp.int32, (8, width), 0)
    work_ref[...] = jnp.zeros_like(work_ref)
    work_ref[:, :size] = cov_ref[...]
    for block in range(size // 8):
        base, low = 8 * block, 8 * block + 8
        panel = work_ref[base:low, :]
        cols = [
            jnp.broadcast_to(panel[:, base + j : base + j + 1], (8, 128)) for j in range(8)
        ]
        eye = jnp.where(lane - base == sub_wide, 1.0, 0.0)
        rows = jnp.where((lane >= base) & (lane < low), eye, panel)
        scale = jnp.zeros((8, 128), jnp.float32)
        for j in range(8):
            root = lax.rsqrt(jnp.broadcast_to(cols[j][j : j + 1, :], (8, 128)))
            scale = jnp.where(sub == j, root, scale)
            if j < 7:
                ratio = jnp.where(sub > j, cols[j] * (root * root), 0.0)
                for i in range(j + 1, 8):
                    cols[i] = cols[i] - ratio * jnp.broadcast_to(cols[i][j : j + 1, :], (8, 128))
                ratio_wide = jnp.concatenate([ratio, ratio], axis=1)
                rows = rows - ratio_wide * jnp.broadcast_to(rows[j : j + 1, :], (8, width))
        rows = rows * jnp.concatenate([scale, scale], axis=1)
        work_ref[base:low, :] = jnp.where(lane < low, rows, 0.0)
        if low < size:
            one, two, three = split_three(rows)
            left = jnp.concatenate([one, one, two, two, one, three], axis=0)
            right = jnp.concatenate([one, two, one, two, three, one], axis=0)
            update = lax.dot_general(
                left, right, (((0,), (0,)), ((), ())), preferred_element_type=jnp.float32
            )
            rest = work_ref[low:size, :]
            rest_lane = lax.broadcasted_iota(jnp.int32, rest.shape, 1)
            rest = jnp.where((rest_lane >= base) & (rest_lane < low), 0.0, rest)
            work_ref[low:size, :] = rest - update[low:size, :]
    out_ref[...] = work_ref[:, :size]


def inverse_factor(cov):
    size = cov.shape[0]
    return pl.pallas_call(
        inverse_factor_kernel,
        out_shape=jax.ShapeDtypeStruct((size, size), jnp.float32),
        in_specs=[pl.BlockSpec(memory_space=pltpu.VMEM)],
        out_specs=pl.BlockSpec(memory_space=pltpu.VMEM),
        scratch_shapes=[pltpu.VMEM((size, 256), jnp.float32)],
        cost_estimate=pl.CostEstimate(
            flops=2 * size**3, bytes_accessed=8 * size**2, transcendentals=size
        ),
        name="inverse_factor",
    )(cov)


def finish(signal_moment, noise_moment, signal_first, noise_first, count):
    signal_cov = (signal_moment - jnp.outer(signal_first, signal_first) / count) / (count - 1.0)
    noise_cov = (noise_moment - jnp.outer(noise_first, noise_first) / count) / (count - 1.0)
    inverse_lower = inverse_factor(noise_cov)
    left = jnp.dot(inverse_lower, signal_cov, precision=lax.Precision.HIGHEST)
    whitened_cov = jnp.dot(left, inverse_lower.T, precision=lax.Precision.HIGHEST)
    return (inverse_lower, whitened_cov)


def body(radiance, valid_mask):
    bands, rows, cols = radiance.shape
    padded = padded_2(radiance, (("group", 2), ("tile", 1)), 2)
    smooth, noise = smooth_noise(padded, rows, cols)
    weight = valid_mask.astype(jnp.float32)[None]
    signal_masked = smooth * weight
    noise_masked = noise * weight
    signal_first = jnp.sum(signal_masked, axis=(1, 2))
    noise_first = jnp.sum(noise_masked, axis=(1, 2))
    count = jnp.sum(weight)
    signal_flat = signal_masked.astype(jnp.bfloat16).reshape(bands, rows * cols)
    noise_flat = noise_masked.astype(jnp.bfloat16).reshape(bands, rows * cols)
    dims = (((1,), (1,)), ((), ()))
    signal_moment = lax.dot_general(
        signal_flat, signal_flat, dims, preferred_element_type=jnp.float32
    )
    noise_moment = lax.dot_general(noise_flat, noise_flat, dims, preferred_element_type=jnp.float32)
    count_column = jnp.full((bands,), count, jnp.float32)
    side = jnp.stack(
        [signal_first, noise_first, count_column, jnp.diagonal(noise_moment)], axis=1
    )
    packed = jnp.tril(signal_moment) + jnp.triu(noise_moment, 1)
    total = total_of(jnp.concatenate([packed, side], axis=1))
    packed_total = total[:, :bands]
    total_side = total[:, bands:]
    below = jnp.tril(packed_total, -1)
    above = jnp.triu(packed_total, 1)
    eye = jnp.eye(bands, dtype=jnp.bool_)
    signal_total = jnp.tril(packed_total) + below.T
    noise_total = jnp.where(eye, total_side[:, 3:4], above + above.T)
    count_total = total_side[0, 2]
    signal_sum = total_side[:, 0]
    inverse_lower, whitened_cov = finish(
        signal_total, noise_total, signal_sum, total_side[:, 1], count_total
    )
    inverse_cast = inverse_lower.astype(jnp.bfloat16)
    mean_signal = signal_sum / count_total
    centered = (
        (weight * (smooth - mean_signal[:, None, None]))
        .astype(jnp.bfloat16)
        .reshape(bands, rows * cols)
    )
    product = jnp.dot(inverse_cast, centered, preferred_element_type=jnp.float32)
    whitened = product.astype(jnp.bfloat16).reshape(bands, rows, cols)
    return (whitened, whitened_cov)


def solution(mesh):
    return jax.shard_map(
        body,
        mesh=mesh,
        in_specs=(P(None, "tile", "group"), P("tile", "group")),
        out_specs=(P(None, "tile", "group"), P()),
        check_vma=False,
    )
```

profile of v0, /device:TPU:1, one launch (start us, length us, event | category | flops | bytes accessed | tf_op | source)
XLA Modules:
  0.0 208.1 jit_solution(6781299914849313967)
XLA Ops:
  0.6 10.8 %fusion.49 = (bf16[224,96,2]{2,1,0:T(8,128)(2,1)}, bf16[224,96,2]{2,1,0:T(8,128)(2,1)}) fusion(bf16[224,96,128]{2,1,0:T(8,128)(2,1)} %param.2), kind=kLoop, calls=%fused_computation.88 | loop fusion | bytes 344064 | tf_op jit(solution)/shard_map/slice | solution.py:15
  11.5 5.8 %copy.50 = bf16[224,96,2]{0,1,2:T(8,128)(2,1)S(1)} copy(bf16[224,96,2]{2,1,0:T(8,128)(2,1)} %get-tuple-element.12) | data formatting | bytes 172032
  17.3 5.3 %collective-permute-start.1 = (bf16[224,96,2]{0,1,2:T(8,128)(2,1)S(1)}, bf16[224,96,2]{0,1,2:T(8,128)(2,1)S(1)}, u32[]{:S(2)}, u32[]{:S(2)}) collective-permute-start(bf16[224,96,2]{0,1,2:T(8,128)(2,1)S(1)} %copy.50), channel_id=1, source_target_pairs={{32,0},{64,32},{96,64},{128,96},{160,128},{192,160},{224,192},{33,... | collective-permute-start | bytes 258056 | tf_op jit(solution)/shard_map/ppermute | solution.py:17
  22.6 5.8 %copy.49 = bf16[224,96,2]{0,1,2:T(8,128)(2,1)S(1)} copy(bf16[224,96,2]{2,1,0:T(8,128)(2,1)} %get-tuple-element.11) | data formatting | bytes 172032
  28.4 1.9 collective-permute-start
  30.4 9.3 %copy.30 = bf16[224,96,128]{0,2,1:T(8,128)(2,1)} copy(bf16[224,96,128]{2,1,0:T(8,128)(2,1)} %param.2) | data formatting | bytes 11010048 | tf_op args[0]
  40.9 2.6 %collective-permute-start.2 = (bf16[224,2,132]{0,2,1:T(8,128)(2,1)S(1)}, bf16[224,2,132]{0,2,1:T(8,128)(2,1)S(1)}, u32[]{:S(2)}, u32[]{:S(2)}) collective-permute-start(bf16[224,2,132]{0,2,1:T(8,128)(2,1)S(1)} %get-tuple-element.9), channel_id=1, source_target_pairs={{0,1},{1,2},{2,3},{3,4},{4,5},{5,6},{6,7},{7,8},{8,9},{9,10},{10,1... | collective-permute-start | bytes 354824 | tf_op jit(solution)/shard_map/ppermute | solution.py:14
  43.5 1.5 collective-permute-start.3
  46.7 4.3 %collective-permute-done.3 = bf16[224,2,132]{0,2,1:T(8,128)(2,1)S(1)} collective-permute-done((bf16[224,2,132]{0,2,1:T(8,128)(2,1)S(1)}, bf16[224,2,132]{0,2,1:T(8,128)(2,1)S(1)}, u32[]{:S(2)}, u32[]{:S(2)}) %collective-permute-start.3) | collective-permute-done | bytes 118304 | tf_op jit(solution)/shard_map/ppermute | solution.py:17
  51.0 8.8 %maximum_convert_fusion = f32[224,100,132]{0,2,1:T(8,128)S(1)} fusion(bf16[224,2,132]{0,2,1:T(8,128)(2,1)S(1)} %collective-permute-done.3, bf16[224,96,2]{0,2,1:T(2,128)(2,1)S(1)} %copy.31, bf16[224,96,128]{0,2,1:T(8,128)(2,1)} %copy.30, bf16[224,96,2]{0,2,1:T(2,128)(2,1)S(1)} %copy.29, bf16[224,2,132]{0,2,1:T(8,128)(2,1)S(1)} %collective-permute-done.2), kind=kLoop, calls=%fused_computation.24 | loop fusion | flops 29568000 | bytes 17740800 | tf_op jit(solution)/shard_map/convert_element_type | solution.py:23
  59.8 8.1 %fusion = f32[224,96,132]{0,2,1:T(8,128)} fusion(f32[224,100,132]{0,2,1:T(8,128)S(1)} %maximum_convert_fusion), kind=kLoop, calls=%fused_computation.3 | loop fusion | flops 22708224 | bytes 68124672 | tf_op jit(solution)/shard_map/div | solution.py:24
  67.9 7.3 %fusion.47 = (f32[224]{0:T(256)S(1)}, bf16[224,96,128]{0,2,1:T(8,128)(2,1)}) fusion(f32[96,128]{1,0:T(8,128)S(1)} %convert_element_type.22, f32[224,100,132]{0,2,1:T(8,128)S(1)} %maximum_convert_fusion), kind=kLoop, calls=%fused_computation.87 | loop fusion | flops 16514848 | bytes 38585216 | tf_op jit(solution)/shard_map/reduce_sum | solution.py:171
  75.3 29.0 %multiply_reduce_fusion = (f32[224]{0:T(256)S(1)}, f32[224,96,128]{0,2,1:T(8,128)}) fusion(f32[96,128]{1,0:T(8,128)S(1)} %get-tuple-element.16, f32[224,96,132]{0,2,1:T(8,128)} %fusion), kind=kLoop, calls=%fused_computation.22 | loop fusion | flops 24772384 | bytes 66110336 | tf_op jit(solution)/shard_map/reduce_sum | solution.py:170
  104.5 6.5 %fusion.15 = f32[224,224]{1,0:T(8,128)S(1)} fusion(bf16[224,96,128]{0,2,1:T(8,128)(2,1)} %get-tuple-element.6), kind=kOutput, calls=%fused_computation.30 | convolution fusion | flops 1233125376 | bytes 5705728 | tf_op jit(solution)/shard_map/dot_general | solution.py:179
  110.9 2.3 %gather_fusion = f32[224]{0:T(256)S(1)} fusion(f32[224,224]{1,0:T(8,128)S(1)} %fusion.15, s32[224]{0:T(256)S(1)} %bitcast.39), kind=kCustom, calls=%fused_computation | custom fusion | bytes 3584 | tf_op jit(solution)/shard_map/jit(diagonal)/cond/branch_0_fun/gather | solution.py:182
  113.3 12.9 %fusion.20 = f32[224,224]{1,0:T(8,128)S(1)} fusion(f32[224,96,128]{0,2,1:T(8,128)} %get-tuple-element.8, f32[96,128]{1,0:T(8,128)S(1)} %get-tuple-element.16, f32[224,224]{1,0:T(8,128)S(1)} %fusion.15), kind=kOutput, calls=%fused_computation.33 | convolution fusion | flops 1238831104 | bytes 11460608 | tf_op jit(solution)/shard_map/dot_general | solution.py:176
  128.7 5.0 %collective-permute-start.7 = (f32[112,228]{1,0:T(8,128)S(1)}, f32[112,228]{1,0:T(8,128)S(1)}, u32[]{:S(2)}, u32[]{:S(2)}) collective-permute-start(f32[112,228]{1,0:T(8,128)S(1)} %dynamic-slice_add_fusion), channel_id=1, source_target_pairs={{0,3},{1,2},{2,1},{3,0},{4,7},{5,6},{6,5},{7,4},{8,11},{9,10},{10,... | collective-permute-start | bytes 306440 | tf_op jit(solution)/shard_map/ppermute | solution.py:77
  134.7 3.6 %collective-permute-done.7 = f32[112,228]{1,0:T(8,128)S(1)} collective-permute-done((f32[112,228]{1,0:T(8,128)S(1)}, f32[112,228]{1,0:T(8,128)S(1)}, u32[]{:S(2)}, u32[]{:S(2)}) %collective-permute-start.7) | collective-permute-done | bytes 102176 | tf_op jit(solution)/shard_map/ppermute | solution.py:77
  140.1 1.4 collective-permute-start.10
  141.5 1.8 collective-permute-start.9
  143.4 1.6 collective-permute-done.10
  145.0 1.6 collective-permute-done.9
  147.2 6.8 %collective-permute-start.13 = (f32[112,228]{1,0:T(8,128)S(1)}, f32[112,228]{1,0:T(8,128)S(1)}, u32[]{:S(2)}, u32[]{:S(2)}) collective-permute-start(f32[112,228]{1,0:T(8,128)S(1)} %add_add_fusion.1), channel_id=1, source_target_pairs={{0,12},{1,13},{2,14},{3,15},{4,8},{5,9},{6,10},{7,11},{8,4},{9,5},... | collective-permute-start | bytes 306440 | tf_op jit(solution)/shard_map/ppermute | solution.py:77
  154.5 1.9 collective-permute-done.13
  156.4 5.8 %collective-permute-done.12 = f32[112,228]{1,0:T(8,128)S(1)} collective-permute-done((f32[112,228]{1,0:T(8,128)S(1)}, f32[112,228]{1,0:T(8,128)S(1)}, u32[]{:S(2)}, u32[]{:S(2)}) %collective-permute-start.12) | collective-permute-done | bytes 102176 | tf_op jit(solution)/shard_map/ppermute | solution.py:77
  163.5 3.8 %collective-permute-done.14 = f32[112,228]{1,0:T(8,128)S(1)} collective-permute-done((f32[112,228]{1,0:T(8,128)S(1)}, f32[112,228]{1,0:T(8,128)S(1)}, u32[]{:S(2)}, u32[]{:S(2)}) %collective-permute-start.14) | collective-permute-done | bytes 102176 | tf_op jit(solution)/shard_map/ppermute | solution.py:77
  167.4 3.3 %collective-permute-start.15 = (f32[112,228]{1,0:T(8,128)S(1)}, f32[112,228]{1,0:T(8,128)S(1)}, u32[]{:S(2)}, u32[]{:S(2)}) collective-permute-start(f32[112,228]{1,0:T(8,128)S(1)} %add.116), channel_id=1, source_target_pairs={{0,32},{1,33},{2,34},{3,35},{4,36},{5,37},{6,38},{7,39},{8,40},{9,... | collective-permute-start | bytes 306440 | tf_op jit(solution)/shard_map/ppermute | solution.py:82
  173.6 8.7 %multiply_convert_fusion = bf16[224,96,128]{0,2,1:T(8,128)(2,1)} fusion(f32[224,96,128]{0,2,1:T(8,128)} %get-tuple-element.8, f32[224]{0:T(256)S(1)} %broadcast_divide_fusion, f32[96,128]{1,0:T(8,128)S(1)} %convert_element_type.22), kind=kLoop, calls=%fused_computation.21 | loop fusion | flops 11010048 | bytes 16565120 | tf_op jit(solution)/shard_map/convert_element_type | solution.py:202
  184.0 12.5 %inverse_factor.1 = f32[224,224]{1,0:T(8,128)} custom-call(f32[224,224]{1,0:T(8,128)} %fusion.28.cov_ref), custom_call_target="tpu_custom_call" | custom-call | flops 22478848 | bytes 401408 | tf_op jit(solution)/shard_map/inverse_factor/pallas_call | solution.py:141
  196.4 5.1 %fusion.14 = bf16[28,8,96,128]{3,1,2,0:T(8,128)(2,1)S(1)} fusion(bf16[224,12288]{0,1:T(8,128)(2,1)} %bitcast.38, f32[224,224]{1,0:T(8,128)} %inverse_factor.1), kind=kOutput, calls=%fused_computation.29 | convolution fusion | flops 1235928064 | bytes 11210752 | tf_op jit(solution)/shard_map/dot_general | solution.py:205
  201.5 1.9 fusion.24
  204.5 3.6 %copy.55 = bf16[28,8,96,128]{3,2,1,0:T(8,128)(2,1)} copy(bf16[28,8,96,128]{3,1,2,0:T(8,128)(2,1)S(1)} %fusion.14) | data formatting | bytes 11010048
  (50 shorter events, 16.1 us)
Async XLA Ops:
  17.3 27.7 %copy-start.1 = (s32[96,128]{1,0:T(8,128)S(1)}, s32[96,128]{1,0:T(8,128)}, u32[]{:S(2)}) copy-start(s32[96,128]{1,0:T(8,128)} %param.3) | copy-start | bytes 147460
  17.3 22.3 %collective-permute-start.1 = (bf16[224,96,2]{0,1,2:T(8,128)(2,1)S(1)}, bf16[224,96,2]{0,1,2:T(8,128)(2,1)S(1)}, u32[]{:S(2)}, u32[]{:S(2)}) collective-permute-start(bf16[224,96,2]{0,1,2:T(8,128)(2,1)S(1)} %copy.50), channel_id=1, source_target_pairs={{32,0},{64,32},{96,64},{128,96},{160,128},{192,160},{224,192},{33,... | collective-permute-start | bytes 258056 | tf_op jit(solution)/shard_map/ppermute | solution.py:17
  28.4 11.3 %collective-permute-start = (bf16[224,96,2]{0,1,2:T(8,128)(2,1)S(1)}, bf16[224,96,2]{0,1,2:T(8,128)(2,1)S(1)}, u32[]{:S(2)}, u32[]{:S(2)}) collective-permute-start(bf16[224,96,2]{0,1,2:T(8,128)(2,1)S(1)} %copy.49), channel_id=1, source_target_pairs={{0,32},{32,64},{64,96},{96,128},{128,160},{160,192},{192,224},{1,3... | collective-permute-start | bytes 258056 | tf_op jit(solution)/shard_map/ppermute | solution.py:14
  40.9 5.8 %collective-permute-start.2 = (bf16[224,2,132]{0,2,1:T(8,128)(2,1)S(1)}, bf16[224,2,132]{0,2,1:T(8,128)(2,1)S(1)}, u32[]{:S(2)}, u32[]{:S(2)}) collective-permute-start(bf16[224,2,132]{0,2,1:T(8,128)(2,1)S(1)} %get-tuple-element.9), channel_id=1, source_target_pairs={{0,1},{1,2},{2,3},{3,4},{4,5},{5,6},{6,7},{7,8},{8,9},{9,10},{10,1... | collective-permute-start | bytes 354824 | tf_op jit(solution)/shard_map/ppermute | solution.py:14
  43.5 7.5 %collective-permute-start.3 = (bf16[224,2,132]{0,2,1:T(8,128)(2,1)S(1)}, bf16[224,2,132]{0,2,1:T(8,128)(2,1)S(1)}, u32[]{:S(2)}, u32[]{:S(2)}) collective-permute-start(bf16[224,2,132]{0,2,1:T(8,128)(2,1)S(1)} %get-tuple-element.10), channel_id=1, source_target_pairs={{1,0},{2,1},{3,2},{4,3},{5,4},{6,5},{7,6},{8,7},{9,8},{10,9},{11,1... | collective-permute-start | bytes 354824 | tf_op jit(solution)/shard_map/ppermute | solution.py:17
  127.2 1.5 collective-permute-start.4
  128.7 9.6 %collective-permute-start.7 = (f32[112,228]{1,0:T(8,128)S(1)}, f32[112,228]{1,0:T(8,128)S(1)}, u32[]{:S(2)}, u32[]{:S(2)}) collective-permute-start(f32[112,228]{1,0:T(8,128)S(1)} %dynamic-slice_add_fusion), channel_id=1, source_target_pairs={{0,3},{1,2},{2,1},{3,0},{4,7},{5,6},{6,5},{7,4},{8,11},{9,10},{10,... | collective-permute-start | bytes 306440 | tf_op jit(solution)/shard_map/ppermute | solution.py:77
  133.8 5.6 %collective-permute-start.6 = (f32[112,228]{1,0:T(8,128)S(1)}, f32[112,228]{1,0:T(8,128)S(1)}, u32[]{:S(2)}, u32[]{:S(2)}) collective-permute-start(f32[112,228]{1,0:T(8,128)S(1)} %dynamic-slice_add_fusion), channel_id=1, source_target_pairs={{0,2},{1,3},{2,0},{3,1},{4,6},{5,7},{6,4},{7,5},{8,10},{9,11},{10,... | collective-permute-start | bytes 306440 | tf_op jit(solution)/shard_map/ppermute | solution.py:77
  133.8 6.3 %collective-permute-start.5 = (f32[112,228]{1,0:T(8,128)S(1)}, f32[112,228]{1,0:T(8,128)S(1)}, u32[]{:S(2)}, u32[]{:S(2)}) collective-permute-start(f32[112,228]{1,0:T(8,128)S(1)} %dynamic-slice_add_fusion), channel_id=1, source_target_pairs={{0,1},{1,0},{2,3},{3,2},{4,5},{5,4},{6,7},{7,6},{8,9},{9,8},{10,11... | collective-permute-start | bytes 306440 | tf_op jit(solution)/shard_map/ppermute | solution.py:77
  140.1 4.9 %collective-permute-start.10 = (f32[112,228]{1,0:T(8,128)S(1)}, f32[112,228]{1,0:T(8,128)S(1)}, u32[]{:S(2)}, u32[]{:S(2)}) collective-permute-start(f32[112,228]{1,0:T(8,128)S(1)} %add_add_fusion.2), channel_id=1, source_target_pairs={{0,192},{1,193},{2,194},{3,195},{4,196},{5,197},{6,198},{7,199},{8... | collective-permute-start | bytes 306440 | tf_op jit(solution)/shard_map/ppermute | solution.py:77
  141.5 5.2 %collective-permute-start.9 = (f32[112,228]{1,0:T(8,128)S(1)}, f32[112,228]{1,0:T(8,128)S(1)}, u32[]{:S(2)}, u32[]{:S(2)}) collective-permute-start(f32[112,228]{1,0:T(8,128)S(1)} %add_add_fusion.2), channel_id=1, source_target_pairs={{0,128},{1,129},{2,130},{3,131},{4,132},{5,133},{6,134},{7,135},{8... | collective-permute-start | bytes 306440 | tf_op jit(solution)/shard_map/ppermute | solution.py:77
  143.3 3.9 %collective-permute-start.8 = (f32[112,228]{1,0:T(8,128)S(1)}, f32[112,228]{1,0:T(8,128)S(1)}, u32[]{:S(2)}, u32[]{:S(2)}) collective-permute-start(f32[112,228]{1,0:T(8,128)S(1)} %add_add_fusion.2), channel_id=1, source_target_pairs={{0,64},{1,65},{2,66},{3,67},{4,68},{5,69},{6,70},{7,71},{8,72},{9,... | collective-permute-start | bytes 306440 | tf_op jit(solution)/shard_map/ppermute | solution.py:77
  147.2 9.1 %collective-permute-start.13 = (f32[112,228]{1,0:T(8,128)S(1)}, f32[112,228]{1,0:T(8,128)S(1)}, u32[]{:S(2)}, u32[]{:S(2)}) collective-permute-start(f32[112,228]{1,0:T(8,128)S(1)} %add_add_fusion.1), channel_id=1, source_target_pairs={{0,12},{1,13},{2,14},{3,15},{4,8},{5,9},{6,10},{7,11},{8,4},{9,5},... | collective-permute-start | bytes 306440 | tf_op jit(solution)/shard_map/ppermute | solution.py:77
  154.1 8.1 %collective-permute-start.12 = (f32[112,228]{1,0:T(8,128)S(1)}, f32[112,228]{1,0:T(8,128)S(1)}, u32[]{:S(2)}, u32[]{:S(2)}) collective-permute-start(f32[112,228]{1,0:T(8,128)S(1)} %add_add_fusion.1), channel_id=1, source_target_pairs={{0,8},{1,9},{2,10},{3,11},{4,12},{5,13},{6,14},{7,15},{8,0},{9,1},... | collective-permute-start | bytes 306440 | tf_op jit(solution)/shard_map/ppermute | solution.py:77
  154.1 8.1 %collective-permute-start.11 = (f32[112,228]{1,0:T(8,128)S(1)}, f32[112,228]{1,0:T(8,128)S(1)}, u32[]{:S(2)}, u32[]{:S(2)}) collective-permute-start(f32[112,228]{1,0:T(8,128)S(1)} %add_add_fusion.1), channel_id=1, source_target_pairs={{0,4},{1,5},{2,6},{3,7},{4,0},{5,1},{6,2},{7,3},{8,12},{9,13},{10,... | collective-permute-start | bytes 306440 | tf_op jit(solution)/shard_map/ppermute | solution.py:77
  162.3 5.1 %collective-permute-start.14 = (f32[112,228]{1,0:T(8,128)S(1)}, f32[112,228]{1,0:T(8,128)S(1)}, u32[]{:S(2)}, u32[]{:S(2)}) collective-permute-start(f32[112,228]{1,0:T(8,128)S(1)} %add_add_fusion), channel_id=1, source_target_pairs={{0,28},{1,29},{2,30},{3,31},{4,24},{5,25},{6,26},{7,27},{8,20},{9,... | collective-permute-start | bytes 306440 | tf_op jit(solution)/shard_map/ppermute | solution.py:77
  167.4 4.2 %collective-permute-start.15 = (f32[112,228]{1,0:T(8,128)S(1)}, f32[112,228]{1,0:T(8,128)S(1)}, u32[]{:S(2)}, u32[]{:S(2)}) collective-permute-start(f32[112,228]{1,0:T(8,128)S(1)} %add.116), channel_id=1, source_target_pairs={{0,32},{1,33},{2,34},{3,35},{4,36},{5,37},{6,38},{7,39},{8,40},{9,... | collective-permute-start | bytes 306440 | tf_op jit(solution)/shard_map/ppermute | solution.py:82
  196.4 7.0 %copy-start = (f32[224,224]{1,0:T(8,128)S(1)}, f32[224,224]{1,0:T(8,128)}, u32[]{:S(2)}) copy-start(f32[224,224]{1,0:T(8,128)} %inverse_factor.1) | copy-start | bytes 602116
where the time goes:
time: 209 us; the launch traced here: 208 us
  other arithmetic  65.9 us (32%)
  local copies, waits for them, and re-layouts  40.1 us (19%)
  starting transfers between devices  32.6 us (16%)
  waiting for transfers between devices  28.1 us (13%)
  matrix products  27.4 us (13%)
  Pallas kernels  12.5 us (6%)
    reduce_sum x1, other arithmetic, body(): signal_first = jnp.sum(signal_masked, axis=(1, 2))  29 us
    unnamed x9, local copies, waits for them, and re-layouts  24.6 us
    ppermute x10, waiting for transfers between devices, total_of(): parts = [lax.ppermute(own, AXES, pairs) for pairs in stage]  20.7 us
    ppermute x10, starting transfers between devices, total_of(): parts = [lax.ppermute(own, AXES, pairs) for pairs in stage]  17.6 us
    dot_general x1, matrix products, body(): lax.dot_general(signal_flat, signal_flat, dims, preferred_element_type=jn...  12.9 us
    pallas_call x1, Pallas kernels, inverse_factor(): pl.pallas_call(inverse_factor_kernel, out_shape=jax.ShapeDtypeStruct((siz...  12.5 us
    slice x1, local copies, waits for them, and re-layouts, padded_2(): lax.slice_in_dim(block, block.shape[dim] - width, None, axis=dim)  10.8 us
    convert_element_type x1, other arithmetic, smooth_noise(): field = padded.astype(jnp.float32)  8.77 us
  transfers between devices with their start and end apart: 16, of which 13 were waited for; matrix products, arithmetic and copies ran while one was open for 8% of the time, Pallas kernels for 0%

commit v1 on v0

v1 whole, which is shorter than its diff:
```python
import jax
import jax.numpy as jnp
from jax import lax
from jax.experimental import pallas as pl
from jax.experimental.pallas import tpu as pltpu
from jax.sharding import PartitionSpec as P

F32 = jnp.float32
BF16 = jnp.bfloat16
VMEM_SPEC = pl.BlockSpec(memory_space=pltpu.VMEM)
GROUP = 8
TAPS = (0.0625, 0.25, 0.375, 0.25, 0.0625)


def flat_pairs(sizes, move):
    y_size, z_size, x_size = sizes
    pairs = []
    for y in range(y_size):
        for core in range(2):
            for z in range(z_size):
                for x in range(x_size):
                    y2, core2, z2, x2 = move(y, core, z, x)
                    source = ((y * 2 + core) * z_size + z) * x_size + x
                    target = ((y2 * 2 + core2) * z_size + z2) * x_size + x2
                    pairs.append((source, target))
    return pairs


SIZES = (4, 8, 4)
CORE_SWAP = flat_pairs(SIZES, lambda y, c, z, x: (y, 1 - c, z, x))
STAGES = (
    [flat_pairs(SIZES, lambda y, c, z, x, k=k: (y, c, z, x ^ k)) for k in (1, 2, 3)],
    [flat_pairs(SIZES, lambda y, c, z, x, k=k: (y ^ k, c, z, x)) for k in (1, 2, 3)],
    [flat_pairs(SIZES, lambda y, c, z, x, k=k: (y, c, z ^ k, x)) for k in (1, 2, 3)],
    [flat_pairs(SIZES, lambda y, c, z, x: (y, c, 7 - z, x))],
)
AXES = ("group", "tile")


def total_of(value):
    half = value.shape[0] // 2
    core = lax.axis_index("group") % 2
    own = lax.dynamic_slice_in_dim(value, core * half, half, axis=0)
    other = lax.dynamic_slice_in_dim(value, (1 - core) * half, half, axis=0)
    own = own + lax.ppermute(other, AXES, CORE_SWAP)
    for stage in STAGES:
        parts = [lax.ppermute(own, AXES, pairs) for pairs in stage]
        if len(parts) == 1:
            own = own + parts[0]
        else:
            own = (own + parts[0]) + (parts[1] + parts[2])
    other = lax.ppermute(own, AXES, CORE_SWAP)
    first = core == 0
    return jnp.concatenate(
        [jnp.where(first, own, other), jnp.where(first, other, own)], axis=0
    )


def split_three(value):
    first = value.astype(jnp.bfloat16)
    rest = value - first.astype(jnp.float32)
    second = rest.astype(jnp.bfloat16)
    third = (rest - second.astype(jnp.float32)).astype(jnp.bfloat16)
    return (first, second, third)


def params(mebibytes):
    return pltpu.CompilerParams(vmem_limit_bytes=mebibytes << 20)


def cost(flops, bytes_accessed):
    return pl.CostEstimate(flops=flops, bytes_accessed=bytes_accessed, transcendentals=0)


def edges_kernel(top_ref, low_ref, first_ref, last_ref):
    first_ref[...] = jnp.swapaxes(top_ref[...], 0, 1)[:2]
    last_ref[...] = jnp.swapaxes(low_ref[...], 0, 1)[14:]


def edge_rows(x):
    bands, rows, cols = x.shape
    shape = jax.ShapeDtypeStruct((2, bands, cols), BF16)
    whole = pl.BlockSpec((2, bands, cols), lambda i: (0, 0, 0))
    return pl.pallas_call(
        edges_kernel,
        grid=(1,),
        out_shape=(shape, shape),
        in_specs=[
            pl.BlockSpec((bands, 16, cols), lambda i: (0, 0, 0)),
            pl.BlockSpec((bands, 16, cols), lambda i: (0, rows // 16 - 1, 0)),
        ],
        out_specs=(whole, whole),
        compiler_params=params(6),
        cost_estimate=cost(0, 4 * bands * 16 * cols),
        name="edge_rows",
    )(x, x)


def rows_first_kernel(x_ref, out_ref):
    out_ref[...] = jnp.swapaxes(x_ref[...], 0, 1)


def rows_first(x):
    bands, rows, cols = x.shape
    return pl.pallas_call(
        rows_first_kernel,
        grid=(rows // 16,),
        out_shape=jax.ShapeDtypeStruct((rows, bands, cols), BF16),
        in_specs=[pl.BlockSpec((bands, 16, cols), lambda i: (0, i, 0))],
        out_specs=pl.BlockSpec((16, bands, cols), lambda i: (i, 0, 0)),
        compiler_params=params(8),
        cost_estimate=cost(0, 4 * bands * rows * cols),
        name="rows_first",
    )(x)


def fold(moment, columns):
    size = moment.shape[0]
    half = size // 2
    wide = moment if moment.shape[1] == 256 else jnp.concatenate(
        [moment, jnp.zeros((size, 256 - size), F32)], axis=1
    )
    row = lax.broadcasted_iota(jnp.int32, (half, 256), 0)
    lane = lax.broadcasted_iota(jnp.int32, (half, 256), 1)
    moved = pltpu.roll(wide[:half], half + 1, 1)
    out = jnp.where(lane <= half + row, wide[half:], moved)
    for place, column in enumerate(columns):
        out = jnp.where(lane == size + 2 + place, column, out)
    return out


def unfold(folded):
    half = folded.shape[0]
    size = 2 * half
    row = lax.broadcasted_iota(jnp.int32, (half, 256), 0)
    lane = lax.broadcasted_iota(jnp.int32, (half, 256), 1)
    back = pltpu.roll(folded, 256 - half - 1, 1)
    upper = jnp.where((lane >= row) & (lane < half), back, 0.0)
    lower = jnp.where(lane <= half + row, folded, 0.0)
    part = jnp.concatenate([upper, lower], axis=0)
    turned = jnp.concatenate([part, jnp.zeros((256 - size, 256), F32)], axis=0).T[:size]
    row = lax.broadcasted_iota(jnp.int32, (size, 256), 0)
    lane = lax.broadcasted_iota(jnp.int32, (size, 256), 1)
    return part + jnp.where(row == lane, 0.0, turned)


def noise_kernel(xt_ref, up_ref, down_ref, weight_ref, out_ref, moment_ref, first_ref):
    rows, bands, cols = xt_ref.shape
    groups = rows // GROUP
    moment_ref[...] = jnp.zeros_like(moment_ref)
    first_ref[...] = jnp.zeros_like(first_ref)

    def step(weights, field):
        parts = []
        total = None
        for i in range(GROUP):
            value = field[i + 1] - 0.5 * (field[i] + field[i + 2])
            value = value * weights[i : i + 1, :]
            total = value if total is None else total + value
            parts.append(value.astype(BF16))
        first_ref[...] += total
        flat = jnp.concatenate(parts, axis=1)
        moment_ref[...] += lax.dot_general(
            flat, flat, (((1,), (1,)), ((), ())), preferred_element_type=F32
        )

    def weights_of(g):
        return weight_ref[pl.ds(pl.multiple_of(g * GROUP, GROUP), GROUP), :].astype(F32)

    def load(r):
        return xt_ref[r].astype(F32)

    step(weights_of(0), [up_ref[1].astype(F32)] + [load(r) for r in range(GROUP + 1)])

    @pl.loop(1, groups - 1)
    def _(g):
        step(weights_of(g), [load(g * GROUP + i - 1) for i in range(GROUP + 2)])

    base = rows - GROUP
    step(
        weights_of(groups - 1),
        [load(base + i - 1) for i in range(GROUP + 1)] + [down_ref[0].astype(F32)],
    )
    first = jnp.sum(first_ref[...], axis=1, keepdims=True)
    count = jnp.sum(weight_ref[...].astype(F32), keepdims=True)
    half = bands // 2
    out_ref[...] = fold(moment_ref[...], [first[:half], first[half:], count])


def noise_moments(xt, up, down, weight):
    rows, bands, cols = xt.shape
    return pl.pallas_call(
        noise_kernel,
        out_shape=jax.ShapeDtypeStruct((bands // 2, 256), F32),
        in_specs=[VMEM_SPEC] * 4,
        out_specs=VMEM_SPEC,
        scratch_shapes=[pltpu.VMEM((bands, bands), F32), pltpu.VMEM((bands, cols), F32)],
        compiler_params=params(6),
        cost_estimate=cost(2 * bands * bands * rows * cols, 2 * bands * rows * cols),
        name="noise_moments",
    )(xt, up, down, weight)


def side_columns_kernel(xt_ref, up_ref, down_ref, out_ref):
    rows, bands, cols = xt_ref.shape
    groups = rows // GROUP
    place = lax.broadcasted_iota(jnp.int32, (GROUP * cols, 128), 0)
    lane = lax.broadcasted_iota(jnp.int32, (GROUP * cols, 128), 1)
    pixel_row, col = place // cols, place % cols
    wanted_low = 2 * pixel_row + col
    wanted_high = 2 * GROUP + 2 * pixel_row + (col - (cols - 2))
    pick = ((col < 2) & (lane == wanted_low)) | ((col >= cols - 2) & (lane == wanted_high))
    pick = jnp.where(pick, 1.0, 0.0).astype(BF16)
    zero = jnp.zeros((bands, cols), BF16)
    sums = [[jnp.zeros((bands, 128), F32) for _ in range(2)] for _ in range(2)]
    lane = lax.broadcasted_iota(jnp.int32, (bands, 128), 1)
    for g in range(groups + 1):
        if g < groups:
            pieces = [xt_ref[g * GROUP + i] for i in range(GROUP)]
        else:
            pieces = [up_ref[0], up_ref[1], down_ref[0], down_ref[1]] + [zero] * 4
        got = jnp.dot(jnp.concatenate(pieces, axis=1), pick, preferred_element_type=F32)
        shift = 16 * (g % 8)
        low = jnp.where(lane < 16, got, 0.0)
        high = jnp.where((lane >= 16) & (lane < 32), got, 0.0)
        chunk = g // 8
        sums[0][chunk] += pltpu.roll(low, shift, 1) if shift else low
        turn = (shift - 16) % 128
        sums[1][chunk] += pltpu.roll(high, turn, 1) if turn else high
    for side in range(2):
        out_ref[side] = jnp.concatenate(sums[side], axis=1).astype(BF16)


def side_columns(xt, up, down):
    rows, bands, cols = xt.shape
    return pl.pallas_call(
        side_columns_kernel,
        out_shape=jax.ShapeDtypeStruct((2, bands, 256), BF16),
        in_specs=[VMEM_SPEC] * 3,
        out_specs=VMEM_SPEC,
        compiler_params=params(8),
        cost_estimate=cost(2 * bands * rows * cols * 32, 2 * bands * rows * cols),
        name="side_columns",
    )(xt, up, down)


def signal_kernel(
    xt_ref, up_ref, down_ref, low_ref, high_ref, weight_ref,
    smooth_ref, out_ref, col_ref, moment_ref, first_ref,
):
    rows, bands, cols = xt_ref.shape
    groups = rows // GROUP
    moment_ref[...] = jnp.zeros_like(moment_ref)
    first_ref[...] = jnp.zeros_like(first_ref)

    def taps_of(distance):
        out = jnp.zeros(distance.shape, F32)
        for k, tap in enumerate(TAPS):
            out = jnp.where(distance == k - 2, tap, out)
        return out

    source = lax.broadcasted_iota(jnp.int32, (2 * cols, 2 * cols), 0)
    target = lax.broadcasted_iota(jnp.int32, (2 * cols, 2 * cols), 1)
    band = jnp.where(
        source // cols == target // cols, taps_of(source % cols - target % cols), 0.0
    ).astype(BF16)
    source = lax.broadcasted_iota(jnp.int32, (128, 2 * cols), 0)
    target = lax.broadcasted_iota(jnp.int32, (128, 2 * cols), 1)
    is_low = source < 16
    pixel_row = (source % 16) // 2
    position = jnp.where(is_low, source % 2 - 2, cols + source % 2)
    sides = []
    for q in range(4):
        keep = (source < 32) & (pixel_row == 2 * q + target // cols)
        sides.append(jnp.where(keep, taps_of(position - target % cols), 0.0).astype(BF16))
    lane = lax.broadcasted_iota(jnp.int32, (bands, 128), 1)

    def side_lanes(chunk, shift):
        low = low_ref[:, 128 * chunk : 128 * chunk + 128].astype(F32)
        high = high_ref[:, 128 * chunk : 128 * chunk + 128].astype(F32)
        low = pltpu.roll(low, (128 - shift) % 128, 1)
        high = pltpu.roll(high, (128 + 16 - shift) % 128, 1)
        return jnp.where(lane < 16, low, jnp.where(lane < 32, high, 0.0)).astype(BF16)

    def smooth_pair(one, two, extra, q):
        pair = jnp.concatenate([one, two], axis=1)
        out = jnp.dot(pair, band, preferred_element_type=F32)
        out += jnp.dot(extra, sides[q], preferred_element_type=F32)
        return (out[:, :cols], out[:, cols:])

    for g in range(groups):
        extra = side_lanes(g // 8, 16 * (g % 8))
        for q in range(4):
            r = g * GROUP + 2 * q
            one, two = smooth_pair(xt_ref[r], xt_ref[r + 1], extra, q)
            col_ref[r + 2] = one
            col_ref[r + 3] = two
    extra = side_lanes(groups // 8, 16 * (groups % 8))
    col_ref[0], col_ref[1] = smooth_pair(up_ref[0], up_ref[1], extra, 0)
    col_ref[rows + 2], col_ref[rows + 3] = smooth_pair(down_ref[0], down_ref[1], extra, 1)

    @pl.loop(0, groups)
    def _(g):
        base = pl.multiple_of(g * GROUP, GROUP)
        weights = weight_ref[pl.ds(base, GROUP), :].astype(F32)
        field = [col_ref[base + i] for i in range(GROUP + 4)]
        parts = []
        total = None
        for i in range(GROUP):
            value = (
                0.0625 * (field[i] + field[i + 4])
                + 0.25 * (field[i + 1] + field[i + 3])
                + 0.375 * field[i + 2]
            )
            smooth_ref[base + i] = value
            value = value * weights[i : i + 1, :]
            total = value if total is None else total + value
            parts.append(value.astype(BF16))
        first_ref[...] += total
        flat = jnp.concatenate(parts, axis=1)
        moment_ref[...] += lax.dot_general(
            flat, flat, (((1,), (1,)), ((), ())), preferred_element_type=F32
        )

    first = jnp.sum(first_ref[...], axis=1, keepdims=True)
    count = jnp.sum(weight_ref[...].astype(F32), keepdims=True)
    half = bands // 2
    out_ref[...] = fold(moment_ref[...], [first[:half], first[half:], count])


def signal_moments(xt, up, down, low, high, weight):
    rows, bands, cols = xt.shape
    return pl.pallas_call(
        signal_kernel,
        out_shape=(
            jax.ShapeDtypeStruct((rows, bands, cols), F32),
            jax.ShapeDtypeStruct((bands // 2, 256), F32),
        ),
        in_specs=[VMEM_SPEC] * 6,
        out_specs=(VMEM_SPEC, VMEM_SPEC),
        scratch_shapes=[
            pltpu.VMEM((rows + 4, bands, cols), F32),
            pltpu.VMEM((bands, bands), F32),
            pltpu.VMEM((bands, cols), F32),
        ],
        compiler_params=params(20),
        cost_estimate=cost(4 * bands * bands * rows * cols, 6 * bands * rows * cols),
        name="signal_moments",
    )(xt, up, down, low, high, weight)


def sums_of(folded):
    size = 2 * folded.shape[0]
    first = jnp.concatenate(
        [folded[:, size + 2 : size + 3], folded[:, size + 3 : size + 4]], axis=0
    )
    return (first, folded[:1, size + 4 : size + 5])


def covariance_of(folded):
    size = 2 * folded.shape[0]
    first, count = sums_of(folded)
    down = jnp.broadcast_to(first, (size, 256))
    across = jnp.concatenate([down, jnp.zeros((256 - size, 256), F32)], axis=0).T[:size]
    return (unfold(folded) - down * across / count) / (count - 1.0)


def whiten_kernel(inverse_ref, sums_ref, weight_ref, smooth_ref, out_ref):
    step_rows, bands, cols = smooth_ref.shape
    weights = weight_ref[...].astype(F32)
    first, count = sums_of(sums_ref[...])
    mean = jnp.broadcast_to(first / count, (bands, cols))
    inverse = inverse_ref[...]
    parts = []
    for pair in range(step_rows // 2):
        pieces = []
        for i in (2 * pair, 2 * pair + 1):
            pieces.append((weights[i : i + 1, :] * (smooth_ref[i] - mean)).astype(BF16))
        product = jnp.dot(inverse, jnp.concatenate(pieces, axis=1), preferred_element_type=F32)
        product = product.astype(BF16)
        parts += [product[None, :, :cols], product[None, :, cols:]]
    out_ref[...] = jnp.swapaxes(jnp.concatenate(parts, axis=0), 0, 1)


def whiten(inverse, sums, weight, smooth):
    rows, bands, cols = smooth.shape
    return pl.pallas_call(
        whiten_kernel,
        grid=(rows // 16,),
        out_shape=jax.ShapeDtypeStruct((bands, rows, cols), BF16),
        in_specs=[
            pl.BlockSpec((bands, bands), lambda i: (0, 0)),
            pl.BlockSpec((bands // 2, 256), lambda i: (0, 0)),
            pl.BlockSpec((16, cols), lambda i: (i, 0)),
            pl.BlockSpec((16, bands, cols), lambda i: (i, 0, 0)),
        ],
        out_specs=pl.BlockSpec((bands, 16, cols), lambda i: (0, i, 0)),
        compiler_params=params(12),
        cost_estimate=cost(2 * bands * bands * rows * cols, 6 * bands * rows * cols),
        name="whiten",
    )(inverse, sums, weight, smooth)


def inverse_factor_kernel(sums_ref, out_ref, cast_ref, work_ref):
    size = out_ref.shape[0]
    width = work_ref.shape[1]
    sub = lax.broadcasted_iota(jnp.int32, (8, 128), 0)
    lane = lax.broadcasted_iota(jnp.int32, (8, width), 1)
    sub_wide = lax.broadcasted_iota(jnp.int32, (8, width), 0)
    work_ref[...] = covariance_of(sums_ref[...])
    for block in range(size // 8):
        base, low = 8 * block, 8 * block + 8
        panel = work_ref[base:low, :]
        cols = [
            jnp.broadcast_to(panel[:, base + j : base + j + 1], (8, 128)) for j in range(8)
        ]
        eye = jnp.where(lane - base == sub_wide, 1.0, 0.0)
        rows = jnp.where((lane >= base) & (lane < low), eye, panel)
        scale = jnp.zeros((8, 128), jnp.float32)
        for j in range(8):
            root = lax.rsqrt(jnp.broadcast_to(cols[j][j : j + 1, :], (8, 128)))
            scale = jnp.where(sub == j, root, scale)
            if j < 7:
                ratio = jnp.where(sub > j, cols[j] * (root * root), 0.0)
                for i in range(j + 1, 8):
                    cols[i] = cols[i] - ratio * jnp.broadcast_to(cols[i][j : j + 1, :], (8, 128))
                ratio_wide = jnp.concatenate([ratio, ratio], axis=1)
                rows = rows - ratio_wide * jnp.broadcast_to(rows[j : j + 1, :], (8, width))
        rows = rows * jnp.concatenate([scale, scale], axis=1)
        work_ref[base:low, :] = jnp.where(lane < low, rows, 0.0)
        if low < size:
            one, two, three = split_three(rows)
            left = jnp.concatenate([one, one, two, two, one, three], axis=0)
            right = jnp.concatenate([one, two, one, two, three, one], axis=0)
            update = lax.dot_general(
                left, right, (((0,), (0,)), ((), ())), preferred_element_type=jnp.float32
            )
            rest = work_ref[low:size, :]
            rest_lane = lax.broadcasted_iota(jnp.int32, rest.shape, 1)
            rest = jnp.where((rest_lane >= base) & (rest_lane < low), 0.0, rest)
            work_ref[low:size, :] = rest - update[low:size, :]
    out_ref[...] = work_ref[:, :size]
    cast_ref[...] = work_ref[:, :size].astype(BF16)


def inverse_factor(sums):
    size = 2 * sums.shape[0]
    return pl.pallas_call(
        inverse_factor_kernel,
        out_shape=(
            jax.ShapeDtypeStruct((size, size), F32),
            jax.ShapeDtypeStruct((size, size), BF16),
        ),
        in_specs=[VMEM_SPEC],
        out_specs=(VMEM_SPEC, VMEM_SPEC),
        scratch_shapes=[pltpu.VMEM((size, 256), F32)],
        compiler_params=params(6),
        cost_estimate=cost(2 * size**3, 8 * size**2),
        name="inverse_factor",
    )(sums)


def whitened_cov_kernel(inverse_ref, sums_ref, out_ref):
    size = inverse_ref.shape[0]
    cov = covariance_of(sums_ref[...])[:, :size]
    inverse = inverse_ref[...]
    left = jnp.dot(inverse, cov, precision=lax.Precision.HIGHEST, preferred_element_type=F32)
    out_ref[...] = lax.dot_general(
        left, inverse, (((1,), (1,)), ((), ())),
        precision=lax.Precision.HIGHEST, preferred_element_type=F32,
    )


def whitened_cov_of(inverse, sums):
    size = inverse.shape[0]
    return pl.pallas_call(
        whitened_cov_kernel,
        out_shape=jax.ShapeDtypeStruct((size, size), F32),
        in_specs=[VMEM_SPEC, VMEM_SPEC],
        out_specs=VMEM_SPEC,
        compiler_params=params(6),
        cost_estimate=cost(24 * size**3, 12 * size**2),
        name="whitened_cov",
    )(inverse, sums)


def line(count):
    forward = [(i, i + 1) for i in range(count - 1)]
    return (forward, [(target, source) for source, target in forward])


def body(radiance, valid_mask):
    first, last = edge_rows(radiance)
    forward, backward = line(lax.axis_size("tile"))
    up = lax.ppermute(last, "tile", forward)
    down = lax.ppermute(first, "tile", backward)
    xt = rows_first(radiance)
    noise = noise_moments(xt, up, down, valid_mask)
    columns = side_columns(xt, up, down)
    forward, backward = line(lax.axis_size("group"))
    low = lax.ppermute(columns[1], "group", forward)
    high = lax.ppermute(columns[0], "group", backward)
    smooth, signal = signal_moments(xt, up, down, low, high, valid_mask)
    noise_total = total_of(noise)
    signal_total = total_of(signal)
    inverse, inverse_cast = inverse_factor(noise_total)
    whitened = whiten(inverse_cast, signal_total, valid_mask, smooth)
    return (whitened, whitened_cov_of(inverse, signal_total))


def solution(mesh):
    return jax.shard_map(
        body,
        mesh=mesh,
        in_specs=(P(None, "tile", "group"), P("tile", "group")),
        out_specs=(P(None, "tile", "group"), P()),
        check_vma=False,
    )
```

time: 209 us -> 118 us (0.56)
  other arithmetic: 65.9 us -> 0.18 us
  matrix products: 27.4 us -> 0 us
  starting transfers between devices: 32.6 us -> 59.7 us
  waiting for transfers between devices: 28.1 us -> 1.74 us
  Pallas kernels: 12.5 us -> 36.6 us
  local copies, waits for them, and re-layouts: 40.1 us -> 18.5 us
    reduce_sum x3 -> x0, other arithmetic: 36.9 us -> none  [the longest x1 29 us: body(): signal_first = jnp.sum(signal_masked, axis=(1, 2))]
    dot_general x5 -> x0, matrix products: 27.4 us -> none  [the longest x1 12.9 us: body(): lax.dot_general(signal_flat, signal_flat, dims, preferred_element_type=jn...]
    pallas_call x1 -> x8, Pallas kernels: 12.5 us -> 36.6 us  [the longest x1 11 us: inverse_factor(): pl.pallas_call(inverse_factor_kernel, out_shape=(jax.ShapeDtypeStruct((si...]
    ppermute x10 -> x20, starting transfers between devices: 17.6 us -> 37.6 us  [total_of(): parts = [lax.ppermute(own, AXES, pairs) for pairs in stage]]
    ppermute x10 -> x20, waiting for transfers between devices: 20.7 us -> 1.72 us  [total_of(): parts = [lax.ppermute(own, AXES, pairs) for pairs in stage]]
    convert_element_type x3 -> x0, other arithmetic: 17.4 us -> none  [the longest x1 8.77 us: smooth_noise(): field = padded.astype(jnp.float32)]
    slice x2 -> x0, local copies, waits for them, and re-layouts: 11.4 us -> none  [the longest x1 10.8 us: padded_2(): lax.slice_in_dim(block, block.shape[dim] - width, None, axis=dim)]
    div x3 -> x0, other arithmetic: 9.99 us -> none  [the longest x1 8.07 us: smooth_noise(): (field[:, 0:rows] + 4.0 * field[:, 1:rows + 1] + 6.0 * field[:, 2:rows +...]
  transfers between devices with their start and end apart: 16 -> 28, of which waited for: 13 -> 1; matrix products, arithmetic and copies ran while one was open for 8% -> 0% of each run, Pallas kernels for 0% -> 21%
where the time goes in v1:
time: 118 us
  starting transfers between devices  59.7 us (51%)
  Pallas kernels  36.6 us (31%)
  local copies, waits for them, and re-layouts  18.5 us (16%)
  waiting for transfers between devices  1.74 us (1%)
    ppermute x20, starting transfers between devices, total_of(): parts = [lax.ppermute(own, AXES, pairs) for pairs in stage]  37.6 us
    unnamed x16, local copies, waits for them, and re-layouts  18.4 us
    pallas_call x1, Pallas kernels, inverse_factor(): pl.pallas_call(inverse_factor_kernel, out_shape=(jax.ShapeDtypeStruct((si...  11 us
    ppermute x2, starting transfers between devices, total_of(): other = lax.ppermute(own, AXES, CORE_SWAP)  10.8 us
    pallas_call x1, Pallas kernels, signal_moments(): pl.pallas_call(signal_kernel, out_shape=(jax.ShapeDtypeStruct((rows, band...  9.52 us
    pallas_call x1, Pallas kernels, whiten(): pl.pallas_call(whiten_kernel, grid=(rows // 16,), out_shape=jax.ShapeDtyp...  5.12 us
    pallas_call x1, Pallas kernels, noise_moments(): pl.pallas_call(noise_kernel, out_shape=jax.ShapeDtypeStruct((bands // 2,...  5.09 us
    ppermute x1, starting transfers between devices, body(): up = lax.ppermute(last, 'tile', forward)  3.95 us
  transfers between devices with their start and end apart: 28, of which 1 were waited for; matrix products, arithmetic and copies ran while one was open for 0% of the time, Pallas kernels for 21%

profile of v1, /device:TPU:1, one launch (start us, length us, event | category | flops | bytes accessed | tf_op | source)
XLA Modules:
  0.0 117.6 jit_solution(7675264108064260501)
XLA Ops:
  0.6 2.6 %copy-done = bf16[224,96,128]{2,1,0:T(8,128)(2,1)S(1)} copy-done((bf16[224,96,128]{2,1,0:T(8,128)(2,1)S(1)}, bf16[224,96,128]{2,1,0:T(8,128)(2,1)}, u32[]{:S(2)}) %copy-start) | copy-done | bytes 5505048
  3.4 4.0 %collective-permute-start = (bf16[2,224,128]{2,1,0:T(8,128)(2,1)S(1)}, bf16[2,224,128]{2,1,0:T(8,128)(2,1)S(1)}, u32[]{:S(2)}, u32[]{:S(2)}) collective-permute-start(bf16[2,224,128]{2,1,0:T(8,128)(2,1)S(1)} %get-tuple-element.8), channel_id=1, source_target_pairs={{0,1},{1,2},{2,3},{3,4},{4,5},{5,6},{6,7},{7,8},{8,9},{9,10},{10,1... | collective-permute-start | bytes 344072 | tf_op jit(solution)/shard_map/ppermute | solution.py:495
  7.3 1.3 %collective-permute-start.1 = (bf16[2,224,128]{2,1,0:T(8,128)(2,1)S(1)}, bf16[2,224,128]{2,1,0:T(8,128)(2,1)S(1)}, u32[]{:S(2)}, u32[]{:S(2)}) collective-permute-start(bf16[2,224,128]{2,1,0:T(8,128)(2,1)S(1)} %get-tuple-element.9), channel_id=1, source_target_pairs={{1,0},{2,1},{3,2},{4,3},{5,4},{6,5},{7,6},{8,7},{9,8},{10,9},{11,1... | collective-permute-start | bytes 344072 | tf_op jit(solution)/shard_map/ppermute | solution.py:496
  8.7 2.6 %copy-done.1 = bf16[224,96,128]{2,1,0:T(8,128)(2,1)S(1)} copy-done((bf16[224,96,128]{2,1,0:T(8,128)(2,1)S(1)}, bf16[224,96,128]{2,1,0:T(8,128)(2,1)}, u32[]{:S(2)}) %copy-start.1) | copy-done | bytes 5505048
  11.2 2.0 %rows_first.1.xt_ref = bf16[96,224,128]{2,1,0:T(8,128)(2,1)S(1)} custom-call(bf16[224,96,128]{2,1,0:T(8,128)(2,1)S(1)} %copy-done.1), custom_call_target="tpu_custom_call" | custom-call | bytes 11010048 | tf_op jit(solution)/shard_map/rows_first/pallas_call | solution.py:105
  13.2 2.4 %copy-done.2 = bf16[96,224,128]{2,1,0:T(8,128)(2,1)} copy-done((bf16[96,224,128]{2,1,0:T(8,128)(2,1)}, bf16[96,224,128]{2,1,0:T(8,128)(2,1)S(1)}, u32[]{:S(2)}) %copy-start.2) | copy-done | bytes 5505048
  15.7 2.6 %copy-done.3 = bf16[96,224,128]{2,1,0:T(8,128)(2,1)S(1)} copy-done((bf16[96,224,128]{2,1,0:T(8,128)(2,1)S(1)}, bf16[96,224,128]{2,1,0:T(8,128)(2,1)}, u32[]{:S(2)}) %copy-start.3) | copy-done | bytes 5505048
  18.2 5.1 %noise_moments.1 = f32[112,256]{1,0:T(8,128)S(1)} custom-call(bf16[96,224,128]{2,1,0:T(8,128)(2,1)S(1)} %copy-done.3, bf16[2,224,128]{2,1,0:T(8,128)(2,1)S(1)} %collective-permute-done.up_ref, bf16[2,224,128]{2,1,0:T(8,128)(2,1)S(1)} %collective-permute-done.1.down_ref, s32[96,128]{1,0:T(8,128)S(1)} %copy-done.7), custom_call_target="tpu_custom_call" | custom-call | flops 1233125376 | bytes 5505024 | tf_op jit(solution)/shard_map/noise_moments/pallas_call | solution.py:192
  24.4 1.8 %side_columns.1 = bf16[2,224,256]{2,1,0:T(8,128)(2,1)S(1)} custom-call(bf16[96,224,128]{2,1,0:T(8,128)(2,1)S(1)} %copy-done.4, bf16[2,224,128]{2,1,0:T(8,128)(2,1)S(1)} %collective-permute-done.up_ref, bf16[2,224,128]{2,1,0:T(8,128)(2,1)S(1)} %collective-permute-done.1.down_ref), custom_call_target="tpu_custom_call" | custom-call | flops 176160768 | bytes 5505024 | tf_op jit(solution)/shard_map/side_columns/pallas_call | solution.py:236
  26.2 3.1 %collective-permute-start.14 = (bf16[224,256]{1,0:T(8,128)(2,1)S(1)}, bf16[224,256]{1,0:T(8,128)(2,1)S(1)}, u32[]{:S(2)}, u32[]{:S(2)}) collective-permute-start(bf16[224,256]{1,0:T(8,128)(2,1)S(1)} %get-tuple-element.15), channel_id=1, source_target_pairs={{0,32},{32,64},{64,96},{96,128},{128,160},{160,192},{192,224},{1,3... | collective-permute-start | bytes 344072 | tf_op jit(solution)/shard_map/ppermute | solution.py:501
  29.3 1.9 %collective-permute-start.15 = (bf16[224,256]{1,0:T(8,128)(2,1)S(1)}, bf16[224,256]{1,0:T(8,128)(2,1)S(1)}, u32[]{:S(2)}, u32[]{:S(2)}) collective-permute-start(bf16[224,256]{1,0:T(8,128)(2,1)S(1)} %get-tuple-element.14), channel_id=1, source_target_pairs={{32,0},{64,32},{96,64},{128,96},{160,128},{192,160},{224,192},{33,... | collective-permute-start | bytes 344072 | tf_op jit(solution)/shard_map/ppermute | solution.py:502
  31.3 2.4 %collective-permute-start.3 = (f32[56,256]{1,0:T(8,128)S(1)}, f32[56,256]{1,0:T(8,128)S(1)}, u32[]{:S(2)}, u32[]{:S(2)}) collective-permute-start(f32[56,256]{1,0:T(8,128)S(1)} %dynamic-slice_add_fusion.1), channel_id=1, source_target_pairs={{0,1},{1,0},{2,3},{3,2},{4,5},{5,4},{6,7},{7,6},{8,9},{9,8},{10,11... | collective-permute-start | bytes 172040 | tf_op jit(solution)/shard_map/ppermute | solution.py:47
  33.7 2.4 %collective-permute-start.4 = (f32[56,256]{1,0:T(8,128)S(1)}, f32[56,256]{1,0:T(8,128)S(1)}, u32[]{:S(2)}, u32[]{:S(2)}) collective-permute-start(f32[56,256]{1,0:T(8,128)S(1)} %dynamic-slice_add_fusion.1), channel_id=1, source_target_pairs={{0,2},{1,3},{2,0},{3,1},{4,6},{5,7},{6,4},{7,5},{8,10},{9,11},{10,... | collective-permute-start | bytes 172040 | tf_op jit(solution)/shard_map/ppermute | solution.py:47
  36.2 9.5 %signal_moments.1 = (f32[96,224,128]{2,1,0:T(8,128)S(1)}, f32[112,256]{1,0:T(8,128)S(1)}) custom-call(bf16[96,224,128]{2,1,0:T(8,128)(2,1)S(1)} %copy-done.4, bf16[2,224,128]{2,1,0:T(8,128)(2,1)S(1)} %collective-permute-done.up_ref, bf16[2,224,128]{2,1,0:T(8,128)(2,1)S(1)} %collective-permute-done.1.down_ref, ...), custom_call_target="tpu_custom_call" | custom-call | flops 2466250752 | bytes 16515072 | tf_op jit(solution)/shard_map/signal_moments/pallas_call | solution.py:333
  45.8 4.2 %copy-done.5 = f32[96,224,128]{2,1,0:T(8,128)} copy-done((f32[96,224,128]{2,1,0:T(8,128)}, f32[96,224,128]{2,1,0:T(8,128)S(1)}, u32[]{:S(2)}) %copy-start.5) | copy-done | bytes 11010072
  50.0 2.4 %collective-permute-start.6 = (f32[56,256]{1,0:T(8,128)S(1)}, f32[56,256]{1,0:T(8,128)S(1)}, u32[]{:S(2)}, u32[]{:S(2)}) collective-permute-start(f32[56,256]{1,0:T(8,128)S(1)} %add_add_fusion.5), channel_id=1, source_target_pairs={{0,64},{1,65},{2,66},{3,67},{4,68},{5,69},{6,70},{7,71},{8,72},{9,... | collective-permute-start | bytes 172040 | tf_op jit(solution)/shard_map/ppermute | solution.py:47
  52.4 2.7 %collective-permute-start.7 = (f32[56,256]{1,0:T(8,128)S(1)}, f32[56,256]{1,0:T(8,128)S(1)}, u32[]{:S(2)}, u32[]{:S(2)}) collective-permute-start(f32[56,256]{1,0:T(8,128)S(1)} %add_add_fusion.5), channel_id=1, source_target_pairs={{0,128},{1,129},{2,130},{3,131},{4,132},{5,133},{6,134},{7,135},{8... | collective-permute-start | bytes 172040 | tf_op jit(solution)/shard_map/ppermute | solution.py:47
  56.0 3.4 %collective-permute-start.18 = (f32[56,256]{1,0:T(8,128)S(1)}, f32[56,256]{1,0:T(8,128)S(1)}, u32[]{:S(2)}, u32[]{:S(2)}) collective-permute-start(f32[56,256]{1,0:T(8,128)S(1)} %dynamic-slice_add_fusion), channel_id=1, source_target_pairs={{0,2},{1,3},{2,0},{3,1},{4,6},{5,7},{6,4},{7,5},{8,10},{9,11},{10,... | collective-permute-start | bytes 172040 | tf_op jit(solution)/shard_map/ppermute | solution.py:47
  59.5 5.5 %collective-permute-start.10 = (f32[56,256]{1,0:T(8,128)S(1)}, f32[56,256]{1,0:T(8,128)S(1)}, u32[]{:S(2)}, u32[]{:S(2)}) collective-permute-start(f32[56,256]{1,0:T(8,128)S(1)} %add_add_fusion.4), channel_id=1, source_target_pairs={{0,8},{1,9},{2,10},{3,11},{4,12},{5,13},{6,14},{7,15},{8,0},{9,1},... | collective-permute-start | bytes 172040 | tf_op jit(solution)/shard_map/ppermute | solution.py:47
  64.9 1.4 %collective-permute-start.11 = (f32[56,256]{1,0:T(8,128)S(1)}, f32[56,256]{1,0:T(8,128)S(1)}, u32[]{:S(2)}, u32[]{:S(2)}) collective-permute-start(f32[56,256]{1,0:T(8,128)S(1)} %add_add_fusion.4), channel_id=1, source_target_pairs={{0,12},{1,13},{2,14},{3,15},{4,8},{5,9},{6,10},{7,11},{8,4},{9,5},... | collective-permute-start | bytes 172040 | tf_op jit(solution)/shard_map/ppermute | solution.py:47
  66.9 3.5 %collective-permute-start.21 = (f32[56,256]{1,0:T(8,128)S(1)}, f32[56,256]{1,0:T(8,128)S(1)}, u32[]{:S(2)}, u32[]{:S(2)}) collective-permute-start(f32[56,256]{1,0:T(8,128)S(1)} %add_add_fusion.2), channel_id=1, source_target_pairs={{0,128},{1,129},{2,130},{3,131},{4,132},{5,133},{6,134},{7,135},{8... | collective-permute-start | bytes 172040 | tf_op jit(solution)/shard_map/ppermute | solution.py:47
  70.6 4.2 %collective-permute-start.12 = (f32[56,256]{1,0:T(8,128)S(1)}, f32[56,256]{1,0:T(8,128)S(1)}, u32[]{:S(2)}, u32[]{:S(2)}) collective-permute-start(f32[56,256]{1,0:T(8,128)S(1)} %add_add_fusion.3), channel_id=1, source_target_pairs={{0,28},{1,29},{2,30},{3,31},{4,24},{5,25},{6,26},{7,27},{8,20},{9,... | collective-permute-start | bytes 172040 | tf_op jit(solution)/shard_map/ppermute | solution.py:47
  74.8 2.2 %collective-permute-start.23 = (f32[56,256]{1,0:T(8,128)S(1)}, f32[56,256]{1,0:T(8,128)S(1)}, u32[]{:S(2)}, u32[]{:S(2)}) collective-permute-start(f32[56,256]{1,0:T(8,128)S(1)} %add_add_fusion.1), channel_id=1, source_target_pairs={{0,4},{1,5},{2,6},{3,7},{4,0},{5,1},{6,2},{7,3},{8,12},{9,13},{10,... | collective-permute-start | bytes 172040 | tf_op jit(solution)/shard_map/ppermute | solution.py:47
  77.0 1.7 %collective-permute-start.24 = (f32[56,256]{1,0:T(8,128)S(1)}, f32[56,256]{1,0:T(8,128)S(1)}, u32[]{:S(2)}, u32[]{:S(2)}) collective-permute-start(f32[56,256]{1,0:T(8,128)S(1)} %add_add_fusion.1), channel_id=1, source_target_pairs={{0,8},{1,9},{2,10},{3,11},{4,12},{5,13},{6,14},{7,15},{8,0},{9,1},... | collective-permute-start | bytes 172040 | tf_op jit(solution)/shard_map/ppermute | solution.py:47
  79.2 4.6 %collective-permute-start.13 = (f32[56,256]{1,0:T(8,128)S(1)}, f32[56,256]{1,0:T(8,128)S(1)}, u32[]{:S(2)}, u32[]{:S(2)}) collective-permute-start(f32[56,256]{1,0:T(8,128)S(1)} %add.92), channel_id=1, source_target_pairs={{0,32},{1,33},{2,34},{3,35},{4,36},{5,37},{6,38},{7,39},{8,40},{9,... | collective-permute-start | bytes 172040 | tf_op jit(solution)/shard_map/ppermute | solution.py:52
  83.8 3.6 %collective-permute-start.26 = (f32[56,256]{1,0:T(8,128)S(1)}, f32[56,256]{1,0:T(8,128)S(1)}, u32[]{:S(2)}, u32[]{:S(2)}) collective-permute-start(f32[56,256]{1,0:T(8,128)S(1)} %add_add_fusion), channel_id=1, source_target_pairs={{0,28},{1,29},{2,30},{3,31},{4,24},{5,25},{6,26},{7,27},{8,20},{9,... | collective-permute-start | bytes 172040 | tf_op jit(solution)/shard_map/ppermute | solution.py:47
  87.5 1.7 %collective-permute-done.26 = f32[56,256]{1,0:T(8,128)S(1)} collective-permute-done((f32[56,256]{1,0:T(8,128)S(1)}, f32[56,256]{1,0:T(8,128)S(1)}, u32[]{:S(2)}, u32[]{:S(2)}) %collective-permute-start.26) | collective-permute-done | bytes 57376 | tf_op jit(solution)/shard_map/ppermute | solution.py:47
  89.1 6.2 %collective-permute-start.27 = (f32[56,256]{1,0:T(8,128)S(1)}, f32[56,256]{1,0:T(8,128)S(1)}, u32[]{:S(2)}, u32[]{:S(2)}) collective-permute-start(f32[56,256]{1,0:T(8,128)S(1)} %add.103), channel_id=1, source_target_pairs={{0,32},{1,33},{2,34},{3,35},{4,36},{5,37},{6,38},{7,39},{8,40},{9,... | collective-permute-start | bytes 172040 | tf_op jit(solution)/shard_map/ppermute | solution.py:52
  95.3 11.0 %inverse_factor.1 = (f32[224,224]{1,0:T(8,128)S(1)}, bf16[224,224]{1,0:T(8,128)(2,1)S(1)}) custom-call(f32[112,256]{1,0:T(8,128)S(1)} %pad_maximum_fusion.sums_ref), custom_call_target="tpu_custom_call" | custom-call | flops 22478848 | bytes 401408 | tf_op jit(solution)/shard_map/inverse_factor/pallas_call | solution.py:448
  106.4 1.9 %whitened_cov.1 = f32[224,224]{1,0:T(8,128)} custom-call(f32[224,224]{1,0:T(8,128)S(1)} %get-tuple-element.13.inverse_ref, f32[112,256]{1,0:T(8,128)S(1)} %pad_maximum_fusion.1.sums_ref), custom_call_target="tpu_custom_call" | custom-call | flops 269746176 | bytes 602112 | tf_op jit(solution)/shard_map/whitened_cov/pallas_call | solution.py:476
  108.3 4.1 %copy-done.6 = f32[96,224,128]{2,1,0:T(8,128)S(1)} copy-done((f32[96,224,128]{2,1,0:T(8,128)S(1)}, f32[96,224,128]{2,1,0:T(8,128)}, u32[]{:S(2)}) %copy-start.6) | copy-done | bytes 11010072
  112.5 5.1 %whiten.1 = bf16[224,96,128]{2,1,0:T(8,128)(2,1)} custom-call(bf16[224,224]{1,0:T(8,128)(2,1)S(1)} %get-tuple-element.10.inverse_ref, f32[112,256]{1,0:T(8,128)S(1)} %pad_maximum_fusion.1.sums_ref, s32[96,128]{1,0:T(8,128)S(1)} %copy-done.7, f32[96,224,128]{2,1,0:T(8,128)S(1)} %copy-done.6), custom_call_target="tpu_custom_call" | custom-call | flops 1233125376 | bytes 16515072 | tf_op jit(solution)/shard_map/whiten/pallas_call | solution.py:387
  (65 shorter events, 3.6 us)
Async XLA Ops:
  3.4 12.3 %collective-permute-start = (bf16[2,224,128]{2,1,0:T(8,128)(2,1)S(1)}, bf16[2,224,128]{2,1,0:T(8,128)(2,1)S(1)}, u32[]{:S(2)}, u32[]{:S(2)}) collective-permute-start(bf16[2,224,128]{2,1,0:T(8,128)(2,1)S(1)} %get-tuple-element.8), channel_id=1, source_target_pairs={{0,1},{1,2},{2,3},{3,4},{4,5},{5,6},{6,7},{7,8},{8,9},{9,10},{10,1... | collective-permute-start | bytes 344072 | tf_op jit(solution)/shard_map/ppermute | solution.py:495
  7.3 8.3 %collective-permute-start.1 = (bf16[2,224,128]{2,1,0:T(8,128)(2,1)S(1)}, bf16[2,224,128]{2,1,0:T(8,128)(2,1)S(1)}, u32[]{:S(2)}, u32[]{:S(2)}) collective-permute-start(bf16[2,224,128]{2,1,0:T(8,128)(2,1)S(1)} %get-tuple-element.9), channel_id=1, source_target_pairs={{1,0},{2,1},{3,2},{4,3},{5,4},{6,5},{7,6},{8,7},{9,8},{10,9},{11,1... | collective-permute-start | bytes 344072 | tf_op jit(solution)/shard_map/ppermute | solution.py:496
  11.2 4.4 %copy-start.7 = (s32[96,128]{1,0:T(8,128)S(1)}, s32[96,128]{1,0:T(8,128)}, u32[]{:S(2)}) copy-start(s32[96,128]{1,0:T(8,128)} %weight_ref.5) | copy-start | bytes 147460
  18.2 6.2 %copy-start.4 = (bf16[96,224,128]{2,1,0:T(8,128)(2,1)S(1)}, bf16[96,224,128]{2,1,0:T(8,128)(2,1)}, u32[]{:S(2)}) copy-start(bf16[96,224,128]{2,1,0:T(8,128)(2,1)} %copy-done.2) | copy-start | bytes 16515076
  23.3 7.9 %collective-permute-start.2 = (f32[56,256]{1,0:T(8,128)S(1)}, f32[56,256]{1,0:T(8,128)S(1)}, u32[]{:S(2)}, u32[]{:S(2)}) collective-permute-start(f32[56,256]{1,0:T(8,128)S(1)} %constant_dynamic-slice_fusion.1), channel_id=1, source_target_pairs={{0,32},{1,33},{2,34},{3,35},{4,36},{5,37},{6,38},{7,39},{8,40},{9,... | collective-permute-start | bytes 172040 | tf_op jit(solution)/shard_map/ppermute | solution.py:45
  26.2 10.0 %collective-permute-start.14 = (bf16[224,256]{1,0:T(8,128)(2,1)S(1)}, bf16[224,256]{1,0:T(8,128)(2,1)S(1)}, u32[]{:S(2)}, u32[]{:S(2)}) collective-permute-start(bf16[224,256]{1,0:T(8,128)(2,1)S(1)} %get-tuple-element.15), channel_id=1, source_target_pairs={{0,32},{32,64},{64,96},{96,128},{128,160},{160,192},{192,224},{1,3... | collective-permute-start | bytes 344072 | tf_op jit(solution)/shard_map/ppermute | solution.py:501
  29.3 6.9 %collective-permute-start.15 = (bf16[224,256]{1,0:T(8,128)(2,1)S(1)}, bf16[224,256]{1,0:T(8,128)(2,1)S(1)}, u32[]{:S(2)}, u32[]{:S(2)}) collective-permute-start(bf16[224,256]{1,0:T(8,128)(2,1)S(1)} %get-tuple-element.14), channel_id=1, source_target_pairs={{32,0},{64,32},{96,64},{128,96},{160,128},{192,160},{224,192},{33,... | collective-permute-start | bytes 344072 | tf_op jit(solution)/shard_map/ppermute | solution.py:502
  31.3 18.7 %collective-permute-start.3 = (f32[56,256]{1,0:T(8,128)S(1)}, f32[56,256]{1,0:T(8,128)S(1)}, u32[]{:S(2)}, u32[]{:S(2)}) collective-permute-start(f32[56,256]{1,0:T(8,128)S(1)} %dynamic-slice_add_fusion.1), channel_id=1, source_target_pairs={{0,1},{1,0},{2,3},{3,2},{4,5},{5,4},{6,7},{7,6},{8,9},{9,8},{10,11... | collective-permute-start | bytes 172040 | tf_op jit(solution)/shard_map/ppermute | solution.py:47
  33.7 16.2 %collective-permute-start.4 = (f32[56,256]{1,0:T(8,128)S(1)}, f32[56,256]{1,0:T(8,128)S(1)}, u32[]{:S(2)}, u32[]{:S(2)}) collective-permute-start(f32[56,256]{1,0:T(8,128)S(1)} %dynamic-slice_add_fusion.1), channel_id=1, source_target_pairs={{0,2},{1,3},{2,0},{3,1},{4,6},{5,7},{6,4},{7,5},{8,10},{9,11},{10,... | collective-permute-start | bytes 172040 | tf_op jit(solution)/shard_map/ppermute | solution.py:47
  36.2 13.8 %collective-permute-start.5 = (f32[56,256]{1,0:T(8,128)S(1)}, f32[56,256]{1,0:T(8,128)S(1)}, u32[]{:S(2)}, u32[]{:S(2)}) collective-permute-start(f32[56,256]{1,0:T(8,128)S(1)} %dynamic-slice_add_fusion.1), channel_id=1, source_target_pairs={{0,3},{1,2},{2,1},{3,0},{4,7},{5,6},{6,5},{7,4},{8,11},{9,10},{10,... | collective-permute-start | bytes 172040 | tf_op jit(solution)/shard_map/ppermute | solution.py:47
  45.8 4.2 %copy-start.5 = (f32[96,224,128]{2,1,0:T(8,128)}, f32[96,224,128]{2,1,0:T(8,128)S(1)}, u32[]{:S(2)}) copy-start(f32[96,224,128]{2,1,0:T(8,128)S(1)} %get-tuple-element.12.smooth_ref) | copy-start | bytes 33030148
  49.9 5.2 %collective-permute-start.16 = (f32[56,256]{1,0:T(8,128)S(1)}, f32[56,256]{1,0:T(8,128)S(1)}, u32[]{:S(2)}, u32[]{:S(2)}) collective-permute-start(f32[56,256]{1,0:T(8,128)S(1)} %constant_dynamic-slice_fusion), channel_id=1, source_target_pairs={{0,32},{1,33},{2,34},{3,35},{4,36},{5,37},{6,38},{7,39},{8,40},{9,... | collective-permute-start | bytes 172040 | tf_op jit(solution)/shard_map/ppermute | solution.py:45
  50.0 9.4 %collective-permute-start.6 = (f32[56,256]{1,0:T(8,128)S(1)}, f32[56,256]{1,0:T(8,128)S(1)}, u32[]{:S(2)}, u32[]{:S(2)}) collective-permute-start(f32[56,256]{1,0:T(8,128)S(1)} %add_add_fusion.5), channel_id=1, source_target_pairs={{0,64},{1,65},{2,66},{3,67},{4,68},{5,69},{6,70},{7,71},{8,72},{9,... | collective-permute-start | bytes 172040 | tf_op jit(solution)/shard_map/ppermute | solution.py:47
  52.4 7.0 %collective-permute-start.7 = (f32[56,256]{1,0:T(8,128)S(1)}, f32[56,256]{1,0:T(8,128)S(1)}, u32[]{:S(2)}, u32[]{:S(2)}) collective-permute-start(f32[56,256]{1,0:T(8,128)S(1)} %add_add_fusion.5), channel_id=1, source_target_pairs={{0,128},{1,129},{2,130},{3,131},{4,132},{5,133},{6,134},{7,135},{8... | collective-permute-start | bytes 172040 | tf_op jit(solution)/shard_map/ppermute | solution.py:47
  55.1 4.3 %collective-permute-start.8 = (f32[56,256]{1,0:T(8,128)S(1)}, f32[56,256]{1,0:T(8,128)S(1)}, u32[]{:S(2)}, u32[]{:S(2)}) collective-permute-start(f32[56,256]{1,0:T(8,128)S(1)} %add_add_fusion.5), channel_id=1, source_target_pairs={{0,192},{1,193},{2,194},{3,195},{4,196},{5,197},{6,198},{7,199},{8... | collective-permute-start | bytes 172040 | tf_op jit(solution)/shard_map/ppermute | solution.py:47
  55.1 11.2 %collective-permute-start.17 = (f32[56,256]{1,0:T(8,128)S(1)}, f32[56,256]{1,0:T(8,128)S(1)}, u32[]{:S(2)}, u32[]{:S(2)}) collective-permute-start(f32[56,256]{1,0:T(8,128)S(1)} %dynamic-slice_add_fusion), channel_id=1, source_target_pairs={{0,1},{1,0},{2,3},{3,2},{4,5},{5,4},{6,7},{7,6},{8,9},{9,8},{10,11... | collective-permute-start | bytes 172040 | tf_op jit(solution)/shard_map/ppermute | solution.py:47
  56.0 10.5 %collective-permute-start.18 = (f32[56,256]{1,0:T(8,128)S(1)}, f32[56,256]{1,0:T(8,128)S(1)}, u32[]{:S(2)}, u32[]{:S(2)}) collective-permute-start(f32[56,256]{1,0:T(8,128)S(1)} %dynamic-slice_add_fusion), channel_id=1, source_target_pairs={{0,2},{1,3},{2,0},{3,1},{4,6},{5,7},{6,4},{7,5},{8,10},{9,11},{10,... | collective-permute-start | bytes 172040 | tf_op jit(solution)/shard_map/ppermute | solution.py:47
  59.4 7.1 %collective-permute-start.19 = (f32[56,256]{1,0:T(8,128)S(1)}, f32[56,256]{1,0:T(8,128)S(1)}, u32[]{:S(2)}, u32[]{:S(2)}) collective-permute-start(f32[56,256]{1,0:T(8,128)S(1)} %dynamic-slice_add_fusion), channel_id=1, source_target_pairs={{0,3},{1,2},{2,1},{3,0},{4,7},{5,6},{6,5},{7,4},{8,11},{9,10},{10,... | collective-permute-start | bytes 172040 | tf_op jit(solution)/shard_map/ppermute | solution.py:47
  59.5 11.0 %collective-permute-start.10 = (f32[56,256]{1,0:T(8,128)S(1)}, f32[56,256]{1,0:T(8,128)S(1)}, u32[]{:S(2)}, u32[]{:S(2)}) collective-permute-start(f32[56,256]{1,0:T(8,128)S(1)} %add_add_fusion.4), channel_id=1, source_target_pairs={{0,8},{1,9},{2,10},{3,11},{4,12},{5,13},{6,14},{7,15},{8,0},{9,1},... | collective-permute-start | bytes 172040 | tf_op jit(solution)/shard_map/ppermute | solution.py:47
  64.9 5.6 %collective-permute-start.11 = (f32[56,256]{1,0:T(8,128)S(1)}, f32[56,256]{1,0:T(8,128)S(1)}, u32[]{:S(2)}, u32[]{:S(2)}) collective-permute-start(f32[56,256]{1,0:T(8,128)S(1)} %add_add_fusion.4), channel_id=1, source_target_pairs={{0,12},{1,13},{2,14},{3,15},{4,8},{5,9},{6,10},{7,11},{8,4},{9,5},... | collective-permute-start | bytes 172040 | tf_op jit(solution)/shard_map/ppermute | solution.py:47
  66.4 4.2 %collective-permute-start.9 = (f32[56,256]{1,0:T(8,128)S(1)}, f32[56,256]{1,0:T(8,128)S(1)}, u32[]{:S(2)}, u32[]{:S(2)}) collective-permute-start(f32[56,256]{1,0:T(8,128)S(1)} %add_add_fusion.4), channel_id=1, source_target_pairs={{0,4},{1,5},{2,6},{3,7},{4,0},{5,1},{6,2},{7,3},{8,12},{9,13},{10,... | collective-permute-start | bytes 172040 | tf_op jit(solution)/shard_map/ppermute | solution.py:47
  66.6 8.2 %collective-permute-start.20 = (f32[56,256]{1,0:T(8,128)S(1)}, f32[56,256]{1,0:T(8,128)S(1)}, u32[]{:S(2)}, u32[]{:S(2)}) collective-permute-start(f32[56,256]{1,0:T(8,128)S(1)} %add_add_fusion.2), channel_id=1, source_target_pairs={{0,64},{1,65},{2,66},{3,67},{4,68},{5,69},{6,70},{7,71},{8,72},{9,... | collective-permute-start | bytes 172040 | tf_op jit(solution)/shard_map/ppermute | solution.py:47
  66.9 7.8 %collective-permute-start.21 = (f32[56,256]{1,0:T(8,128)S(1)}, f32[56,256]{1,0:T(8,128)S(1)}, u32[]{:S(2)}, u32[]{:S(2)}) collective-permute-start(f32[56,256]{1,0:T(8,128)S(1)} %add_add_fusion.2), channel_id=1, source_target_pairs={{0,128},{1,129},{2,130},{3,131},{4,132},{5,133},{6,134},{7,135},{8... | collective-permute-start | bytes 172040 | tf_op jit(solution)/shard_map/ppermute | solution.py:47
  70.5 4.3 %collective-permute-start.22 = (f32[56,256]{1,0:T(8,128)S(1)}, f32[56,256]{1,0:T(8,128)S(1)}, u32[]{:S(2)}, u32[]{:S(2)}) collective-permute-start(f32[56,256]{1,0:T(8,128)S(1)} %add_add_fusion.2), channel_id=1, source_target_pairs={{0,192},{1,193},{2,194},{3,195},{4,196},{5,197},{6,198},{7,199},{8... | collective-permute-start | bytes 172040 | tf_op jit(solution)/shard_map/ppermute | solution.py:47
  70.6 8.6 %collective-permute-start.12 = (f32[56,256]{1,0:T(8,128)S(1)}, f32[56,256]{1,0:T(8,128)S(1)}, u32[]{:S(2)}, u32[]{:S(2)}) collective-permute-start(f32[56,256]{1,0:T(8,128)S(1)} %add_add_fusion.3), channel_id=1, source_target_pairs={{0,28},{1,29},{2,30},{3,31},{4,24},{5,25},{6,26},{7,27},{8,20},{9,... | collective-permute-start | bytes 172040 | tf_op jit(solution)/shard_map/ppermute | solution.py:47
  74.8 9.0 %collective-permute-start.23 = (f32[56,256]{1,0:T(8,128)S(1)}, f32[56,256]{1,0:T(8,128)S(1)}, u32[]{:S(2)}, u32[]{:S(2)}) collective-permute-start(f32[56,256]{1,0:T(8,128)S(1)} %add_add_fusion.1), channel_id=1, source_target_pairs={{0,4},{1,5},{2,6},{3,7},{4,0},{5,1},{6,2},{7,3},{8,12},{9,13},{10,... | collective-permute-start | bytes 172040 | tf_op jit(solution)/shard_map/ppermute | solution.py:47
  77.0 6.8 %collective-permute-start.24 = (f32[56,256]{1,0:T(8,128)S(1)}, f32[56,256]{1,0:T(8,128)S(1)}, u32[]{:S(2)}, u32[]{:S(2)}) collective-permute-start(f32[56,256]{1,0:T(8,128)S(1)} %add_add_fusion.1), channel_id=1, source_target_pairs={{0,8},{1,9},{2,10},{3,11},{4,12},{5,13},{6,14},{7,15},{8,0},{9,1},... | collective-permute-start | bytes 172040 | tf_op jit(solution)/shard_map/ppermute | solution.py:47
  78.7 5.1 %collective-permute-start.25 = (f32[56,256]{1,0:T(8,128)S(1)}, f32[56,256]{1,0:T(8,128)S(1)}, u32[]{:S(2)}, u32[]{:S(2)}) collective-permute-start(f32[56,256]{1,0:T(8,128)S(1)} %add_add_fusion.1), channel_id=1, source_target_pairs={{0,12},{1,13},{2,14},{3,15},{4,8},{5,9},{6,10},{7,11},{8,4},{9,5},... | collective-permute-start | bytes 172040 | tf_op jit(solution)/shard_map/ppermute | solution.py:47
  79.2 8.2 %collective-permute-start.13 = (f32[56,256]{1,0:T(8,128)S(1)}, f32[56,256]{1,0:T(8,128)S(1)}, u32[]{:S(2)}, u32[]{:S(2)}) collective-permute-start(f32[56,256]{1,0:T(8,128)S(1)} %add.92), channel_id=1, source_target_pairs={{0,32},{1,33},{2,34},{3,35},{4,36},{5,37},{6,38},{7,39},{8,40},{9,... | collective-permute-start | bytes 172040 | tf_op jit(solution)/shard_map/ppermute | solution.py:52
  83.8 5.3 %collective-permute-start.26 = (f32[56,256]{1,0:T(8,128)S(1)}, f32[56,256]{1,0:T(8,128)S(1)}, u32[]{:S(2)}, u32[]{:S(2)}) collective-permute-start(f32[56,256]{1,0:T(8,128)S(1)} %add_add_fusion), channel_id=1, source_target_pairs={{0,28},{1,29},{2,30},{3,31},{4,24},{5,25},{6,26},{7,27},{8,20},{9,... | collective-permute-start | bytes 172040 | tf_op jit(solution)/shard_map/ppermute | solution.py:47
  89.1 17.3 %collective-permute-start.27 = (f32[56,256]{1,0:T(8,128)S(1)}, f32[56,256]{1,0:T(8,128)S(1)}, u32[]{:S(2)}, u32[]{:S(2)}) collective-permute-start(f32[56,256]{1,0:T(8,128)S(1)} %add.103), channel_id=1, source_target_pairs={{0,32},{1,33},{2,34},{3,35},{4,36},{5,37},{6,38},{7,39},{8,40},{9,... | collective-permute-start | bytes 172040 | tf_op jit(solution)/shard_map/ppermute | solution.py:52
  108.3 4.1 %copy-start.6 = (f32[96,224,128]{2,1,0:T(8,128)S(1)}, f32[96,224,128]{2,1,0:T(8,128)}, u32[]{:S(2)}) copy-start(f32[96,224,128]{2,1,0:T(8,128)} %copy-done.5) | copy-start | bytes 33030148
  (4 other events, 10.1 us)

commit v2 on v1

v2 whole, which is shorter than its diff:
```python
import jax
import jax.numpy as jnp
from jax import lax
from jax.experimental import pallas as pl
from jax.experimental.pallas import tpu as pltpu
from jax.sharding import PartitionSpec as P

F32 = jnp.float32
BF16 = jnp.bfloat16
VMEM_SPEC = pl.BlockSpec(memory_space=pltpu.VMEM)
HBM_SPEC = pl.BlockSpec(memory_space=pltpu.HBM)
GROUP = 8
CORNER_GROUP = 12
PIVOTS = 16
TAPS = (0.0625, 0.25, 0.375, 0.25, 0.0625)


def flat_pairs(sizes, move):
    y_size, z_size, x_size = sizes
    pairs = []
    for y in range(y_size):
        for core in range(2):
            for z in range(z_size):
                for x in range(x_size):
                    y2, core2, z2, x2 = move(y, core, z, x)
                    source = ((y * 2 + core) * z_size + z) * x_size + x
                    target = ((y2 * 2 + core2) * z_size + z2) * x_size + x2
                    pairs.append((source, target))
    return pairs


SIZES = (4, 8, 4)
CORE_SWAP = flat_pairs(SIZES, lambda y, c, z, x: (y, 1 - c, z, x))
X_PAIRS = [flat_pairs(SIZES, lambda y, c, z, x, k=k: (y, c, z, x ^ k)) for k in (1, 2, 3)]
STAGES = (
    [flat_pairs(SIZES, lambda y, c, z, x, k=k: (y ^ k, c, z, x)) for k in (1, 2, 3)],
    [flat_pairs(SIZES, lambda y, c, z, x, k=k: (y, c, z ^ k, x)) for k in (1, 2, 3)],
    [flat_pairs(SIZES, lambda y, c, z, x: (y, c, 7 - z, x))],
)
AXES = ("group", "tile")


def total_of(value):
    half = value.shape[1] // 2
    core = lax.axis_index("group") % 2
    x = lax.axis_index("tile") % 4
    own = lax.dynamic_slice_in_dim(value, core * half, half, axis=1)
    other = lax.dynamic_slice_in_dim(value, (1 - core) * half, half, axis=1)
    mine = own + lax.ppermute(other, AXES, CORE_SWAP)

    def block(index):
        return lax.dynamic_index_in_dim(mine, index, axis=0, keepdims=False)

    parts = [lax.ppermute(block(x ^ k), AXES, X_PAIRS[k - 1]) for k in (1, 2, 3)]
    piece = (block(x) + parts[0]) + (parts[1] + parts[2])
    for stage in STAGES:
        parts = [lax.ppermute(piece, AXES, pairs) for pairs in stage]
        if len(parts) == 1:
            piece = piece + parts[0]
        else:
            piece = (piece + parts[0]) + (parts[1] + parts[2])
    got = [piece] + [lax.ppermute(piece, AXES, pairs) for pairs in X_PAIRS]
    blocks = []
    for place in range(4):
        value = got[3]
        for k in (0, 1, 2):
            value = jnp.where(x == place ^ k, got[k], value)
        blocks.append(value)
    mine = jnp.stack(blocks)
    other = lax.ppermute(mine, AXES, CORE_SWAP)
    first = core == 0
    return jnp.concatenate([jnp.where(first, mine, other), jnp.where(first, other, mine)], axis=1)


def split_three(value):
    first = value.astype(jnp.bfloat16)
    rest = value - first.astype(jnp.float32)
    second = rest.astype(jnp.bfloat16)
    third = (rest - second.astype(jnp.float32)).astype(jnp.bfloat16)
    return (first, second, third)


def params(mebibytes):
    return pltpu.CompilerParams(vmem_limit_bytes=mebibytes << 20)


def cost(flops, bytes_accessed):
    return pl.CostEstimate(flops=flops, bytes_accessed=bytes_accessed, transcendentals=0)


def in_hbm(value):
    return pltpu.with_memory_space_constraint(value, pltpu.HBM)


def in_vmem(value):
    return pltpu.with_memory_space_constraint(value, pltpu.VMEM)


def edges_kernel(x_ref, first_ref, last_ref, slab_ref, sems):
    rows = x_ref.shape[1]
    top = pltpu.make_async_copy(x_ref.at[:, pl.ds(0, 16), :], slab_ref.at[0], sems.at[0])
    low = pltpu.make_async_copy(x_ref.at[:, pl.ds(rows - 16, 16), :], slab_ref.at[1], sems.at[1])
    top.start()
    low.start()
    top.wait()
    first_ref[...] = jnp.swapaxes(slab_ref[0], 0, 1)[:2]
    low.wait()
    last_ref[...] = jnp.swapaxes(slab_ref[1], 0, 1)[14:]


def edge_rows(x):
    bands, rows, cols = x.shape
    shape = jax.ShapeDtypeStruct((2, bands, cols), BF16)
    return pl.pallas_call(
        edges_kernel,
        out_shape=(shape, shape),
        in_specs=[HBM_SPEC],
        out_specs=(VMEM_SPEC, VMEM_SPEC),
        scratch_shapes=[pltpu.VMEM((2, bands, 16, cols), BF16), pltpu.SemaphoreType.DMA((2,))],
        compiler_params=params(8),
        cost_estimate=cost(0, 4 * bands * 16 * cols),
        name="edge_rows",
    )(in_hbm(x))


def side_picker(cols):
    place = lax.broadcasted_iota(jnp.int32, (GROUP * cols, 128), 0)
    lane = lax.broadcasted_iota(jnp.int32, (GROUP * cols, 128), 1)
    pixel_row, col = place // cols, place % cols
    wanted_low = 2 * pixel_row + col
    wanted_high = 2 * GROUP + 2 * pixel_row + (col - (cols - 2))
    pick = ((col < 2) & (lane == wanted_low)) | ((col >= cols - 2) & (lane == wanted_high))
    return jnp.where(pick, 1.0, 0.0).astype(BF16)


def side_lanes_of(pieces, pick, g):
    got = jnp.dot(jnp.concatenate(pieces, axis=1), pick, preferred_element_type=F32)
    lane = lax.broadcasted_iota(jnp.int32, got.shape, 1)
    shift = 16 * (g % 8)
    turn = (shift - 16) % 128
    low = jnp.where(lane < 16, got, 0.0)
    high = jnp.where((lane >= 16) & (lane < 32), got, 0.0)
    return (
        pltpu.roll(low, shift, 1) if shift else low,
        pltpu.roll(high, turn, 1) if turn else high,
    )


def rows_first_kernel(x_ref, out_ref, side_ref, slab_ref, turned_ref, in_sems, out_sems):
    slabs, bands, _, cols = slab_ref.shape
    inward = [
        pltpu.make_async_copy(x_ref.at[:, pl.ds(16 * s, 16), :], slab_ref.at[s], in_sems.at[s])
        for s in range(slabs)
    ]
    outward = [
        pltpu.make_async_copy(
            turned_ref.at[pl.ds(16 * s, 16)], out_ref.at[pl.ds(16 * s, 16)], out_sems.at[s]
        )
        for s in range(slabs)
    ]
    for copy in inward:
        copy.start()
    pick = side_picker(cols)
    sums = [[jnp.zeros((bands, 128), F32) for _ in range(2)] for _ in range(2)]
    for s in range(slabs):
        inward[s].wait()
        turned_ref[16 * s : 16 * s + 16] = jnp.swapaxes(slab_ref[s], 0, 1)
        outward[s].start()
        for g in (2 * s, 2 * s + 1):
            pieces = [turned_ref[g * GROUP + i] for i in range(GROUP)]
            low, high = side_lanes_of(pieces, pick, g)
            sums[0][g // 8] += low
            sums[1][g // 8] += high
    for side in range(2):
        side_ref[side] = jnp.concatenate(sums[side], axis=1).astype(BF16)
    for copy in outward:
        copy.wait()


def rows_first(x):
    bands, rows, cols = x.shape
    slabs = rows // 16
    return pl.pallas_call(
        rows_first_kernel,
        out_shape=(
            pltpu.HBM((rows, bands, cols), BF16),
            jax.ShapeDtypeStruct((2, bands, 256), BF16),
        ),
        in_specs=[HBM_SPEC],
        out_specs=(HBM_SPEC, VMEM_SPEC),
        scratch_shapes=[
            pltpu.VMEM((slabs, bands, 16, cols), BF16),
            pltpu.VMEM((rows, bands, cols), BF16),
            pltpu.SemaphoreType.DMA((slabs,)),
            pltpu.SemaphoreType.DMA((slabs,)),
        ],
        compiler_params=params(20),
        cost_estimate=cost(2 * bands * rows * cols * 32, 4 * bands * rows * cols),
        name="rows_first",
    )(in_hbm(x))


def corners_kernel(side_ref, up_ref, down_ref, low_ref, high_ref):
    bands, cols = up_ref.shape[1:]
    zero = jnp.zeros((bands, cols), BF16)
    pieces = [up_ref[0], up_ref[1], down_ref[0], down_ref[1]] + [zero] * 4
    parts = side_lanes_of(pieces, side_picker(cols), CORNER_GROUP)
    for side, out_ref in ((0, low_ref), (1, high_ref)):
        out_ref[:, :128] = side_ref[side][:, :128]
        out_ref[:, 128:] = (side_ref[side][:, 128:].astype(F32) + parts[side]).astype(BF16)


def side_columns(side, up, down):
    bands = side.shape[1]
    shape = jax.ShapeDtypeStruct((bands, 256), BF16)
    return pl.pallas_call(
        corners_kernel,
        out_shape=(shape, shape),
        in_specs=[VMEM_SPEC] * 3,
        out_specs=(VMEM_SPEC, VMEM_SPEC),
        compiler_params=params(8),
        cost_estimate=cost(2 * bands * 1024 * 128, 6 * bands * 256),
        name="side_columns",
    )(side, up, down)


def group_copy(source_ref, target_ref, sems, g):
    start = g * GROUP if isinstance(g, int) else pl.multiple_of(g * GROUP, GROUP)
    window = pl.ds(start, GROUP)
    return pltpu.make_async_copy(source_ref.at[window], target_ref.at[window], sems.at[g])


def fold(moment, columns):
    size = moment.shape[0]
    half = size // 2
    wide = moment if moment.shape[1] == 256 else jnp.concatenate(
        [moment, jnp.zeros((size, 256 - size), F32)], axis=1
    )
    row = lax.broadcasted_iota(jnp.int32, (half, 256), 0)
    lane = lax.broadcasted_iota(jnp.int32, (half, 256), 1)
    moved = pltpu.roll(wide[:half], half + 1, 1)
    out = jnp.where(lane <= half + row, wide[half:], moved)
    for place, column in enumerate(columns):
        out = jnp.where(lane == size + 2 + place, column, out)
    return out


def unfold(folded):
    half = folded.shape[0]
    size = 2 * half
    row = lax.broadcasted_iota(jnp.int32, (half, 256), 0)
    lane = lax.broadcasted_iota(jnp.int32, (half, 256), 1)
    back = pltpu.roll(folded, 256 - half - 1, 1)
    upper = jnp.where((lane >= row) & (lane < half), back, 0.0)
    lower = jnp.where(lane <= half + row, folded, 0.0)
    part = jnp.concatenate([upper, lower], axis=0)
    turned = jnp.concatenate([part, jnp.zeros((256 - size, 256), F32)], axis=0).T[:size]
    row = lax.broadcasted_iota(jnp.int32, (size, 256), 0)
    lane = lax.broadcasted_iota(jnp.int32, (size, 256), 1)
    return part + jnp.where(row == lane, 0.0, turned)


def noise_kernel(xt_ref, up_ref, down_ref, weight_ref, out_ref, moment_ref, first_ref):
    rows, bands, cols = xt_ref.shape
    groups = rows // GROUP
    moment_ref[...] = jnp.zeros_like(moment_ref)
    first_ref[...] = jnp.zeros_like(first_ref)

    def step(weights, field):
        parts = []
        total = None
        for i in range(GROUP):
            value = field[i + 1] - 0.5 * (field[i] + field[i + 2])
            value = value * weights[i : i + 1, :]
            total = value if total is None else total + value
            parts.append(value.astype(BF16))
        first_ref[...] += total
        flat = jnp.concatenate(parts, axis=1)
        moment_ref[...] += lax.dot_general(
            flat, flat, (((1,), (1,)), ((), ())), preferred_element_type=F32
        )

    def weights_of(g):
        return weight_ref[pl.ds(pl.multiple_of(g * GROUP, GROUP), GROUP), :].astype(F32)

    def load(r):
        return xt_ref[r].astype(F32)

    step(weights_of(0), [up_ref[1].astype(F32)] + [load(r) for r in range(GROUP + 1)])

    @pl.loop(1, groups - 1)
    def _(g):
        step(weights_of(g), [load(g * GROUP + i - 1) for i in range(GROUP + 2)])

    base = rows - GROUP
    step(
        weights_of(groups - 1),
        [load(base + i - 1) for i in range(GROUP + 1)] + [down_ref[0].astype(F32)],
    )
    first = jnp.sum(first_ref[...], axis=1, keepdims=True)
    count = jnp.sum(weight_ref[...].astype(F32), keepdims=True)
    half = bands // 2
    folded = fold(moment_ref[...], [first[:half], first[half:], count])
    out_ref[0] = folded[:, :128]
    out_ref[1] = folded[:, 128:]


def noise_moments(xt, up, down, weight):
    rows, bands, cols = xt.shape
    return pl.pallas_call(
        noise_kernel,
        out_shape=jax.ShapeDtypeStruct((2, bands // 2, 128), F32),
        in_specs=[VMEM_SPEC] * 4,
        out_specs=VMEM_SPEC,
        scratch_shapes=[pltpu.VMEM((bands, bands), F32), pltpu.VMEM((bands, cols), F32)],
        compiler_params=params(6),
        cost_estimate=cost(2 * bands * bands * rows * cols, 2 * bands * rows * cols),
        name="noise_moments",
    )(in_vmem(xt), up, down, weight)


def signal_kernel(
    xt_ref, up_ref, down_ref, low_ref, high_ref, weight_ref,
    result_ref, out_ref, col_ref, moment_ref, first_ref, smooth_ref, sems,
):
    rows, bands, cols = xt_ref.shape
    groups = rows // GROUP
    moment_ref[...] = jnp.zeros_like(moment_ref)
    first_ref[...] = jnp.zeros_like(first_ref)

    def taps_of(distance):
        out = jnp.zeros(distance.shape, F32)
        for k, tap in enumerate(TAPS):
            out = jnp.where(distance == k - 2, tap, out)
        return out

    source = lax.broadcasted_iota(jnp.int32, (2 * cols, 2 * cols), 0)
    target = lax.broadcasted_iota(jnp.int32, (2 * cols, 2 * cols), 1)
    band = jnp.where(
        source // cols == target // cols, taps_of(source % cols - target % cols), 0.0
    ).astype(BF16)
    source = lax.broadcasted_iota(jnp.int32, (128, 2 * cols), 0)
    target = lax.broadcasted_iota(jnp.int32, (128, 2 * cols), 1)
    is_low = source < 16
    pixel_row = (source % 16) // 2
    position = jnp.where(is_low, source % 2 - 2, cols + source % 2)
    sides = []
    for q in range(4):
        keep = (source < 32) & (pixel_row == 2 * q + target // cols)
        sides.append(jnp.where(keep, taps_of(position - target % cols), 0.0).astype(BF16))
    lane = lax.broadcasted_iota(jnp.int32, (bands, 128), 1)

    def side_lanes(chunk, shift):
        low = low_ref[:, 128 * chunk : 128 * chunk + 128].astype(F32)
        high = high_ref[:, 128 * chunk : 128 * chunk + 128].astype(F32)
        low = pltpu.roll(low, (128 - shift) % 128, 1)
        high = pltpu.roll(high, (128 + 16 - shift) % 128, 1)
        return jnp.where(lane < 16, low, jnp.where(lane < 32, high, 0.0)).astype(BF16)

    def smooth_pair(one, two, extra, q):
        pair = jnp.concatenate([one, two], axis=1)
        out = jnp.dot(pair, band, preferred_element_type=F32)
        out += jnp.dot(extra, sides[q], preferred_element_type=F32)
        return (out[:, :cols], out[:, cols:])

    def column_pass(g):
        if g < groups:
            extra = side_lanes(g // 8, 16 * (g % 8))
            for q in range(4):
                r = g * GROUP + 2 * q
                one, two = smooth_pair(xt_ref[r], xt_ref[r + 1], extra, q)
                col_ref[r + 2] = one
                col_ref[r + 3] = two
        elif g == groups:
            extra = side_lanes(groups // 8, 16 * (groups % 8))
            one, two = smooth_pair(down_ref[0], down_ref[1], extra, 1)
            col_ref[rows + 2] = one
            col_ref[rows + 3] = two

    def row_pass(g):
        base = g * GROUP
        weights = weight_ref[base : base + GROUP, :].astype(F32)
        field = [col_ref[base + i] for i in range(GROUP + 4)]
        parts = []
        total = None
        for i in range(GROUP):
            value = (
                0.0625 * (field[i] + field[i + 4])
                + 0.25 * (field[i + 1] + field[i + 3])
                + 0.375 * field[i + 2]
            )
            smooth_ref[base + i] = value
            value = value * weights[i : i + 1, :]
            total = value if total is None else total + value
            parts.append(value.astype(BF16))
        group_copy(smooth_ref, result_ref, sems, g).start()
        first_ref[...] += total
        flat = jnp.concatenate(parts, axis=1)
        moment_ref[...] += lax.dot_general(
            flat, flat, (((1,), (1,)), ((), ())), preferred_element_type=F32
        )

    extra = side_lanes(groups // 8, 16 * (groups % 8))
    one, two = smooth_pair(up_ref[0], up_ref[1], extra, 0)
    col_ref[0] = one
    col_ref[1] = two
    column_pass(0)
    column_pass(1)
    for g in range(groups):
        column_pass(g + 2)
        row_pass(g)

    first = jnp.sum(first_ref[...], axis=1, keepdims=True)
    count = jnp.sum(weight_ref[...].astype(F32), keepdims=True)
    half = bands // 2
    folded = fold(moment_ref[...], [first[:half], first[half:], count])
    out_ref[0] = folded[:, :128]
    out_ref[1] = folded[:, 128:]
    for g in range(groups):
        group_copy(smooth_ref, result_ref, sems, g).wait()


def signal_moments(xt, up, down, low, high, weight):
    rows, bands, cols = xt.shape
    return pl.pallas_call(
        signal_kernel,
        out_shape=(
            pltpu.HBM((rows, bands, cols), F32),
            jax.ShapeDtypeStruct((2, bands // 2, 128), F32),
        ),
        in_specs=[VMEM_SPEC] * 6,
        out_specs=(HBM_SPEC, VMEM_SPEC),
        scratch_shapes=[
            pltpu.VMEM((rows + 4, bands, cols), F32),
            pltpu.VMEM((bands, bands), F32),
            pltpu.VMEM((bands, cols), F32),
            pltpu.VMEM((rows, bands, cols), F32),
            pltpu.SemaphoreType.DMA((rows // GROUP,)),
        ],
        compiler_params=params(32),
        cost_estimate=cost(4 * bands * bands * rows * cols, 6 * bands * rows * cols),
        name="signal_moments",
    )(in_vmem(xt), up, down, low, high, weight)


def folded_of(sums_ref, which):
    return jnp.concatenate([sums_ref[2 * which], sums_ref[2 * which + 1]], axis=1)


def sums_of(folded):
    size = 2 * folded.shape[0]
    first = jnp.concatenate(
        [folded[:, size + 2 : size + 3], folded[:, size + 3 : size + 4]], axis=0
    )
    return (first, folded[:1, size + 4 : size + 5])


def covariance_of(folded):
    size = 2 * folded.shape[0]
    first, count = sums_of(folded)
    down = jnp.broadcast_to(first, (size, 256))
    across = jnp.concatenate([down, jnp.zeros((256 - size, 256), F32)], axis=0).T[:size]
    return (unfold(folded) - down * across / count) / (count - 1.0)


def factor_into(work_ref, size):
    width = work_ref.shape[1]
    step = PIVOTS
    sub = lax.broadcasted_iota(jnp.int32, (step, 128), 0)
    lane = lax.broadcasted_iota(jnp.int32, (step, width), 1)
    sub_wide = lax.broadcasted_iota(jnp.int32, (step, width), 0)
    for base in range(0, size, step):
        low = base + step
        panel = work_ref[base:low, :]
        cols = [
            jnp.broadcast_to(panel[:, base + j : base + j + 1], (step, 128)) for j in range(step)
        ]
        eye = jnp.where(lane - base == sub_wide, 1.0, 0.0)
        rows = jnp.where((lane >= base) & (lane < low), eye, panel)
        scale = jnp.zeros((step, 128), F32)
        for j in range(step):
            root = lax.rsqrt(jnp.broadcast_to(cols[j][j : j + 1, :], (step, 128)))
            scale = jnp.where(sub == j, root, scale)
            if j < step - 1:
                ratio = jnp.where(sub > j, cols[j] * (root * root), 0.0)
                for i in range(j + 1, step):
                    cols[i] = cols[i] - ratio * jnp.broadcast_to(
                        cols[i][j : j + 1, :], (step, 128)
                    )
                ratio_wide = jnp.concatenate([ratio, ratio], axis=1)
                rows = rows - ratio_wide * jnp.broadcast_to(rows[j : j + 1, :], (step, width))
        rows = rows * jnp.concatenate([scale, scale], axis=1)
        work_ref[base:low, :] = jnp.where(lane < low, rows, 0.0)
        if low < size:
            cut = 128 if low >= 128 else 0
            one, two, three = split_three(rows)
            left = jnp.concatenate([one, one, two, two, one, three], axis=0)
            right = jnp.concatenate([one, two, one, two, three, one], axis=0)
            update = lax.dot_general(
                left[:, cut:], right, (((0,), (0,)), ((), ())), preferred_element_type=F32
            )
            rest = work_ref[low:size, :]
            rest_lane = lax.broadcasted_iota(jnp.int32, rest.shape, 1)
            rest = jnp.where((rest_lane >= base) & (rest_lane < low), 0.0, rest)
            work_ref[low:size, :] = rest - update[low - cut : size - cut, :]


def finish_kernel(
    sums_ref, weight_ref, field_ref, result_ref, cov_ref,
    work_ref, smooth_ref, out_ref, in_sems, out_sems,
):
    rows, bands, cols = smooth_ref.shape
    groups, slabs = rows // GROUP, rows // 16
    for g in range(groups):
        group_copy(field_ref, smooth_ref, in_sems, g).start()
    work_ref[...] = covariance_of(folded_of(sums_ref, 0))
    factor_into(work_ref, bands)
    inverse = work_ref[:, :bands]
    inverse_cast = inverse.astype(BF16)
    first, count = sums_of(folded_of(sums_ref, 1))
    mean = jnp.broadcast_to(first / count, (bands, cols))

    def outward(s):
        window = pl.ds(16 * s if isinstance(s, int) else pl.multiple_of(16 * s, 16), 16)
        return pltpu.make_async_copy(out_ref.at[s], result_ref.at[:, window, :], out_sems.at[s])

    @pl.loop(0, slabs)
    def _(s):
        base = pl.multiple_of(16 * s, 16)
        weights = weight_ref[pl.ds(base, 16), :].astype(F32)
        parts = []
        for pair in range(8):
            if pair % 4 == 0:
                group_copy(field_ref, smooth_ref, in_sems, 2 * s + pair // 4).wait()
            pieces = []
            for i in (2 * pair, 2 * pair + 1):
                pieces.append((weights[i : i + 1, :] * (smooth_ref[base + i] - mean)).astype(BF16))
            product = jnp.dot(
                inverse_cast, jnp.concatenate(pieces, axis=1), preferred_element_type=F32
            )
            product = product.astype(BF16)
            parts += [product[None, :, :cols], product[None, :, cols:]]
        out_ref[s] = jnp.swapaxes(jnp.concatenate(parts, axis=0), 0, 1)
        outward(s).start()

    cov = covariance_of(folded_of(sums_ref, 1))[:, :bands]
    left = jnp.dot(inverse, cov, precision=lax.Precision.HIGHEST, preferred_element_type=F32)
    cov_ref[...] = lax.dot_general(
        left, inverse, (((1,), (1,)), ((), ())),
        precision=lax.Precision.HIGHEST, preferred_element_type=F32,
    )
    for s in range(slabs):
        outward(s).wait()


def finish(sums, weight, smooth):
    rows, bands, cols = smooth.shape
    groups, slabs = rows // GROUP, rows // 16
    return pl.pallas_call(
        finish_kernel,
        out_shape=(
            pltpu.HBM((bands, rows, cols), BF16),
            jax.ShapeDtypeStruct((bands, bands), F32),
        ),
        in_specs=[VMEM_SPEC, VMEM_SPEC, HBM_SPEC],
        out_specs=(HBM_SPEC, VMEM_SPEC),
        scratch_shapes=[
            pltpu.VMEM((bands, 256), F32),
            pltpu.VMEM((rows, bands, cols), F32),
            pltpu.VMEM((slabs, bands, 16, cols), BF16),
            pltpu.SemaphoreType.DMA((groups,)),
            pltpu.SemaphoreType.DMA((slabs,)),
        ],
        compiler_params=params(36),
        cost_estimate=cost(2 * bands * bands * rows * cols, 6 * bands * rows * cols),
        name="finish",
    )(sums, weight, in_hbm(smooth))


def line(count):
    forward = [(i, i + 1) for i in range(count - 1)]
    return (forward, [(target, source) for source, target in forward])


def body(radiance, valid_mask):
    first, last = edge_rows(radiance)
    forward, backward = line(lax.axis_size("tile"))
    up = lax.ppermute(last, "tile", forward)
    down = lax.ppermute(first, "tile", backward)
    xt, side = rows_first(radiance)
    to_low, to_high = side_columns(side, up, down)
    forward, backward = line(lax.axis_size("group"))
    low = lax.ppermute(to_high, "group", forward)
    high = lax.ppermute(to_low, "group", backward)
    noise = noise_moments(xt, up, down, valid_mask)
    smooth, signal = signal_moments(xt, up, down, low, high, valid_mask)
    sums = total_of(jnp.concatenate([noise, signal], axis=0))
    whitened, whitened_cov = finish(sums, valid_mask, smooth)
    return (whitened, whitened_cov)


def solution(mesh):
    return jax.shard_map(
        body,
        mesh=mesh,
        in_specs=(P(None, "tile", "group"), P("tile", "group")),
        out_specs=(P(None, "tile", "group"), P()),
        check_vma=False,
    )
```

time: 118 us -> 97.6 us (0.83)
  starting transfers between devices: 59.7 us -> 41.3 us
  waiting for transfers between devices: 1.74 us -> 18.5 us
  local copies, waits for them, and re-layouts: 18.5 us -> 2.58 us
  Pallas kernels: 36.6 us -> 33.7 us
    ppermute x26 -> x17, starting transfers between devices: 54.4 us -> 36.1 us  [the longest x7 12.5 us: total_of(): parts = [lax.ppermute(piece, AXES, pairs) for pairs in stage]]
    ppermute x26 -> x17, waiting for transfers between devices: 1.74 us -> 18.5 us  [the longest x7 10.4 us: total_of(): parts = [lax.ppermute(piece, AXES, pairs) for pairs in stage]]
    unnamed x16 -> x6, local copies, waits for them, and re-layouts: 18.4 us -> 2.56 us
    pallas_call x8 -> x6, Pallas kernels: 36.6 us -> 33.7 us  [the longest x1 14.4 us: finish(): pl.pallas_call(finish_kernel, out_shape=(pltpu.HBM((bands, rows, cols), B...]
  transfers between devices with their start and end apart: 28 -> 19, of which waited for: 1 -> 11; matrix products, arithmetic and copies ran while one was open for 0% -> 0% of each run, Pallas kernels for 21% -> 11%
where the time goes in v2:
time: 97.6 us; the launch traced here: 97.3 us
  starting transfers between devices  41.3 us (42%)
  Pallas kernels  33.7 us (35%)
  waiting for transfers between devices  18.5 us (19%)
  local copies, waits for them, and re-layouts  2.58 us (3%)
  between operations  1.06 us (1%)
    pallas_call x1, Pallas kernels, finish(): pl.pallas_call(finish_kernel, out_shape=(pltpu.HBM((bands, rows, cols), B...  14.4 us
    ppermute x7, starting transfers between devices, total_of(): parts = [lax.ppermute(piece, AXES, pairs) for pairs in stage]  12.5 us
    ppermute x7, waiting for transfers between devices, total_of(): parts = [lax.ppermute(piece, AXES, pairs) for pairs in stage]  10.4 us
    ppermute x1, starting transfers between devices, total_of(): other = lax.ppermute(mine, AXES, CORE_SWAP)  8.27 us
    pallas_call x1, Pallas kernels, signal_moments(): pl.pallas_call(signal_kernel, out_shape=(pltpu.HBM((rows, bands, cols), F...  6.6 us
    ppermute x3, starting transfers between devices, total_of(): lax.ppermute(block(x ^ k), AXES, X_PAIRS[k - 1])  5.98 us
    pallas_call x1, Pallas kernels, rows_first(): pl.pallas_call(rows_first_kernel, out_shape=(pltpu.HBM((rows, bands, cols...  5.74 us
    pallas_call x1, Pallas kernels, noise_moments(): pl.pallas_call(noise_kernel, out_shape=jax.ShapeDtypeStruct((2, bands //...  5.09 us
  transfers between devices with their start and end apart: 19, of which 11 were waited for; matrix products, arithmetic and copies ran while one was open for 0% of the time, Pallas kernels for 11%

profile of v2, /device:TPU:1, one launch (start us, length us, event | category | flops | bytes accessed | tf_op | source)
XLA Modules:
  0.0 97.3 jit_solution(3559644309564071083)
XLA Ops:
  0.6 1.6 %edge_rows.1 = (bf16[2,224,128]{2,1,0:T(8,128)(2,1)S(1)}, bf16[2,224,128]{2,1,0:T(8,128)(2,1)S(1)}) custom-call(bf16[224,96,128]{2,1,0:T(8,128)(2,1)} %x_ref.3), custom_call_target="tpu_custom_call" | custom-call | bytes 1835008 | tf_op jit(solution)/shard_map/edge_rows/pallas_call | solution.py:114
  2.2 4.0 %collective-permute-start = (bf16[2,224,128]{2,1,0:T(8,128)(2,1)S(1)}, bf16[2,224,128]{2,1,0:T(8,128)(2,1)S(1)}, u32[]{:S(2)}, u32[]{:S(2)}) collective-permute-start(bf16[2,224,128]{2,1,0:T(8,128)(2,1)S(1)} %get-tuple-element.11), channel_id=1, source_target_pairs={{0,1},{1,2},{2,3},{3,4},{4,5},{5,6},{6,7},{7,8},{8,9},{9,10},{10,1... | collective-permute-start | bytes 344072 | tf_op jit(solution)/shard_map/ppermute | solution.py:588
  6.2 1.3 %collective-permute-start.1 = (bf16[2,224,128]{2,1,0:T(8,128)(2,1)S(1)}, bf16[2,224,128]{2,1,0:T(8,128)(2,1)S(1)}, u32[]{:S(2)}, u32[]{:S(2)}) collective-permute-start(bf16[2,224,128]{2,1,0:T(8,128)(2,1)S(1)} %get-tuple-element.12), channel_id=1, source_target_pairs={{1,0},{2,1},{3,2},{4,3},{5,4},{6,5},{7,6},{8,7},{9,8},{10,9},{11,1... | collective-permute-start | bytes 344072 | tf_op jit(solution)/shard_map/ppermute | solution.py:589
  7.5 5.7 %rows_first.1 = (bf16[96,224,128]{2,1,0:T(8,128)(2,1)}, bf16[2,224,256]{2,1,0:T(8,128)(2,1)S(1)}) custom-call(bf16[224,96,128]{2,1,0:T(8,128)(2,1)} %x_ref.3), custom_call_target="tpu_custom_call" | custom-call | flops 176160768 | bytes 11010048 | tf_op jit(solution)/shard_map/rows_first/pallas_call | solution.py:183
  13.3 0.4 side_columns.1
  13.6 4.0 %collective-permute-start.2 = (bf16[224,256]{1,0:T(8,128)(2,1)S(1)}, bf16[224,256]{1,0:T(8,128)(2,1)S(1)}, u32[]{:S(2)}, u32[]{:S(2)}) collective-permute-start(bf16[224,256]{1,0:T(8,128)(2,1)S(1)} %get-tuple-element.14), channel_id=1, source_target_pairs={{0,32},{32,64},{64,96},{96,128},{128,160},{160,192},{192,224},{1,3... | collective-permute-start | bytes 344072 | tf_op jit(solution)/shard_map/ppermute | solution.py:593
  17.7 1.9 %collective-permute-start.3 = (bf16[224,256]{1,0:T(8,128)(2,1)S(1)}, bf16[224,256]{1,0:T(8,128)(2,1)S(1)}, u32[]{:S(2)}, u32[]{:S(2)}) collective-permute-start(bf16[224,256]{1,0:T(8,128)(2,1)S(1)} %get-tuple-element.15), channel_id=1, source_target_pairs={{32,0},{64,32},{96,64},{128,96},{160,128},{192,160},{224,192},{33,... | collective-permute-start | bytes 344072 | tf_op jit(solution)/shard_map/ppermute | solution.py:594
  19.6 2.6 %copy-done = bf16[96,224,128]{2,1,0:T(8,128)(2,1)S(1)} copy-done((bf16[96,224,128]{2,1,0:T(8,128)(2,1)S(1)}, bf16[96,224,128]{2,1,0:T(8,128)(2,1)}, u32[]{:S(2)}) %copy-start) | copy-done | bytes 5505048
  22.2 5.1 %noise_moments.1 = f32[2,112,128]{2,1,0:T(8,128)S(1)} custom-call(bf16[96,224,128]{2,1,0:T(8,128)(2,1)S(1)} %copy-done, bf16[2,224,128]{2,1,0:T(8,128)(2,1)S(1)} %collective-permute-done.up_ref, bf16[2,224,128]{2,1,0:T(8,128)(2,1)S(1)} %collective-permute-done.1.down_ref, s32[96,128]{1,0:T(8,128)S(1)} %copy-done.2), custom_call_target="tpu_custom_call" | custom-call | flops 1233125376 | bytes 5505024 | tf_op jit(solution)/shard_map/noise_moments/pallas_call | solution.py:310
  27.3 6.6 %signal_moments.1 = (f32[96,224,128]{2,1,0:T(8,128)}, f32[2,112,128]{2,1,0:T(8,128)S(1)}) custom-call(bf16[96,224,128]{2,1,0:T(8,128)(2,1)S(1)} %copy-done.1, bf16[2,224,128]{2,1,0:T(8,128)(2,1)S(1)} %collective-permute-done.up_ref, bf16[2,224,128]{2,1,0:T(8,128)(2,1)S(1)} %collective-permute-done.1.down_ref, ...), custom_call_target="tpu_custom_call" | custom-call | flops 2466250752 | bytes 16515072 | tf_op jit(solution)/shard_map/signal_moments/pallas_call | solution.py:425
  34.1 1.3 %collective-permute-done.4 = f32[4,56,128]{2,1,0:T(8,128)S(1)} collective-permute-done((f32[4,56,128]{2,1,0:T(8,128)S(1)}, f32[4,56,128]{2,1,0:T(8,128)S(1)}, u32[]{:S(2)}, u32[]{:S(2)}) %collective-permute-start.4) | collective-permute-done | bytes 114720 | tf_op jit(solution)/shard_map/ppermute | solution.py:49
  35.4 2.6 %collective-permute-start.5 = (f32[56,128]{1,0:T(8,128)S(1)}, f32[56,128]{1,0:T(8,128)S(1)}, u32[]{:S(2)}, u32[]{:S(2)}) collective-permute-start(f32[56,128]{1,0:T(8,128)S(1)} %get-tuple-element.26), channel_id=1, source_target_pairs={{0,1},{1,0},{2,3},{3,2},{4,5},{5,4},{6,7},{7,6},{8,9},{9,8},{10,11... | collective-permute-start | bytes 86024 | tf_op jit(solution)/shard_map/ppermute | solution.py:54
  38.0 3.3 %collective-permute-start.6 = (f32[56,128]{1,0:T(8,128)S(1)}, f32[56,128]{1,0:T(8,128)S(1)}, u32[]{:S(2)}, u32[]{:S(2)}) collective-permute-start(f32[56,128]{1,0:T(8,128)S(1)} %get-tuple-element.25), channel_id=1, source_target_pairs={{0,2},{1,3},{2,0},{3,1},{4,6},{5,7},{6,4},{7,5},{8,10},{9,11},{10,... | collective-permute-start | bytes 86024 | tf_op jit(solution)/shard_map/ppermute | solution.py:54
  41.4 1.6 %collective-permute-done.6 = f32[56,128]{1,0:T(8,128)S(1)} collective-permute-done((f32[56,128]{1,0:T(8,128)S(1)}, f32[56,128]{1,0:T(8,128)S(1)}, u32[]{:S(2)}, u32[]{:S(2)}) %collective-permute-start.6) | collective-permute-done | bytes 28704 | tf_op jit(solution)/shard_map/ppermute | solution.py:54
  42.9 2.4 %collective-permute-done.7 = f32[56,128]{1,0:T(8,128)S(1)} collective-permute-done((f32[56,128]{1,0:T(8,128)S(1)}, f32[56,128]{1,0:T(8,128)S(1)}, u32[]{:S(2)}, u32[]{:S(2)}) %collective-permute-start.7) | collective-permute-done | bytes 28704 | tf_op jit(solution)/shard_map/ppermute | solution.py:54
  45.3 3.0 %collective-permute-start.10 = (f32[56,128]{1,0:T(8,128)S(1)}, f32[56,128]{1,0:T(8,128)S(1)}, u32[]{:S(2)}, u32[]{:S(2)}) collective-permute-start(f32[56,128]{1,0:T(8,128)S(1)} %fusion.3), channel_id=1, source_target_pairs={{0,192},{1,193},{2,194},{3,195},{4,196},{5,197},{6,198},{7,199},{8... | collective-permute-start | bytes 86024 | tf_op jit(solution)/shard_map/ppermute | solution.py:57
  48.3 1.3 %collective-permute-start.9 = (f32[56,128]{1,0:T(8,128)S(1)}, f32[56,128]{1,0:T(8,128)S(1)}, u32[]{:S(2)}, u32[]{:S(2)}) collective-permute-start(f32[56,128]{1,0:T(8,128)S(1)} %fusion.3), channel_id=1, source_target_pairs={{0,128},{1,129},{2,130},{3,131},{4,132},{5,133},{6,134},{7,135},{8... | collective-permute-start | bytes 86024 | tf_op jit(solution)/shard_map/ppermute | solution.py:57
  49.6 1.4 %collective-permute-done.8 = f32[56,128]{1,0:T(8,128)S(1)} collective-permute-done((f32[56,128]{1,0:T(8,128)S(1)}, f32[56,128]{1,0:T(8,128)S(1)}, u32[]{:S(2)}, u32[]{:S(2)}) %collective-permute-start.8) | collective-permute-done | bytes 28704 | tf_op jit(solution)/shard_map/ppermute | solution.py:57
  51.1 1.5 %collective-permute-done.9 = f32[56,128]{1,0:T(8,128)S(1)} collective-permute-done((f32[56,128]{1,0:T(8,128)S(1)}, f32[56,128]{1,0:T(8,128)S(1)}, u32[]{:S(2)}, u32[]{:S(2)}) %collective-permute-start.9) | collective-permute-done | bytes 28704 | tf_op jit(solution)/shard_map/ppermute | solution.py:57
  52.6 1.7 %collective-permute-start.11 = (f32[56,128]{1,0:T(8,128)S(1)}, f32[56,128]{1,0:T(8,128)S(1)}, u32[]{:S(2)}, u32[]{:S(2)}) collective-permute-start(f32[56,128]{1,0:T(8,128)S(1)} %add_add_fusion.1), channel_id=1, source_target_pairs={{0,4},{1,5},{2,6},{3,7},{4,0},{5,1},{6,2},{7,3},{8,12},{9,13},{10,... | collective-permute-start | bytes 86024 | tf_op jit(solution)/shard_map/ppermute | solution.py:57
  54.3 5.4 %collective-permute-start.12 = (f32[56,128]{1,0:T(8,128)S(1)}, f32[56,128]{1,0:T(8,128)S(1)}, u32[]{:S(2)}, u32[]{:S(2)}) collective-permute-start(f32[56,128]{1,0:T(8,128)S(1)} %add_add_fusion.1), channel_id=1, source_target_pairs={{0,8},{1,9},{2,10},{3,11},{4,12},{5,13},{6,14},{7,15},{8,0},{9,1},... | collective-permute-start | bytes 86024 | tf_op jit(solution)/shard_map/ppermute | solution.py:57
  59.7 1.6 %collective-permute-done.12 = f32[56,128]{1,0:T(8,128)S(1)} collective-permute-done((f32[56,128]{1,0:T(8,128)S(1)}, f32[56,128]{1,0:T(8,128)S(1)}, u32[]{:S(2)}, u32[]{:S(2)}) %collective-permute-start.12) | collective-permute-done | bytes 28704 | tf_op jit(solution)/shard_map/ppermute | solution.py:57
  61.3 3.0 %collective-permute-done.13 = f32[56,128]{1,0:T(8,128)S(1)} collective-permute-done((f32[56,128]{1,0:T(8,128)S(1)}, f32[56,128]{1,0:T(8,128)S(1)}, u32[]{:S(2)}, u32[]{:S(2)}) %collective-permute-start.13) | collective-permute-done | bytes 28704 | tf_op jit(solution)/shard_map/ppermute | solution.py:57
  64.3 1.1 %collective-permute-start.14 = (f32[56,128]{1,0:T(8,128)S(1)}, f32[56,128]{1,0:T(8,128)S(1)}, u32[]{:S(2)}, u32[]{:S(2)}) collective-permute-start(f32[56,128]{1,0:T(8,128)S(1)} %add_add_fusion), channel_id=1, source_target_pairs={{0,28},{1,29},{2,30},{3,31},{4,24},{5,25},{6,26},{7,27},{8,20},{9,... | collective-permute-start | bytes 86024 | tf_op jit(solution)/shard_map/ppermute | solution.py:57
  65.4 2.9 %collective-permute-done.14 = f32[56,128]{1,0:T(8,128)S(1)} collective-permute-done((f32[56,128]{1,0:T(8,128)S(1)}, f32[56,128]{1,0:T(8,128)S(1)}, u32[]{:S(2)}, u32[]{:S(2)}) %collective-permute-start.14) | collective-permute-done | bytes 28704 | tf_op jit(solution)/shard_map/ppermute | solution.py:57
  68.3 0.9 collective-permute-start.15
  69.5 2.1 %collective-permute-start.17 = (f32[56,128]{1,0:T(8,128)S(1)}, f32[56,128]{1,0:T(8,128)S(1)}, u32[]{:S(2)}, u32[]{:S(2)}) collective-permute-start(f32[56,128]{1,0:T(8,128)S(1)} %add.77), channel_id=1, source_target_pairs={{0,3},{1,2},{2,1},{3,0},{4,7},{5,6},{6,5},{7,4},{8,11},{9,10},{10,... | collective-permute-start | bytes 86024 | tf_op jit(solution)/shard_map/ppermute | solution.py:62
  71.6 1.0 collective-permute-done.15
  72.5 0.9 collective-permute-done.17
  73.5 8.3 %collective-permute-start.18 = (f32[4,56,128]{2,1,0:T(8,128)S(1)}, f32[4,56,128]{2,1,0:T(8,128)S(1)}, u32[]{:S(2)}, u32[]{:S(2)}) collective-permute-start(f32[4,56,128]{2,1,0:T(8,128)S(1)} %pad_maximum_fusion.1), channel_id=1, source_target_pairs={{0,32},{1,33},{2,34},{3,35},{4,36},{5,37},{6,38},{7,39},{8,40},{9,... | collective-permute-start | bytes 344072 | tf_op jit(solution)/shard_map/ppermute | solution.py:70
  81.7 1.0 collective-permute-done.18
  82.8 14.4 %finish.1 = (bf16[224,96,128]{2,1,0:T(8,128)(2,1)}, f32[224,224]{1,0:T(8,128)}) custom-call(f32[4,112,128]{2,1,0:T(8,128)S(1)} %pad_maximum_fusion.sums_ref, s32[96,128]{1,0:T(8,128)S(1)} %copy-done.2, f32[96,224,128]{2,1,0:T(8,128)} %get-tuple-element.17.field_ref), custom_call_target="tpu_custom_call" | custom-call | flops 1233125376 | bytes 16515072 | tf_op jit(solution)/shard_map/finish/pallas_call | solution.py:559
  (29 shorter events, 0.6 us)
Async XLA Ops:
  0.6 19.0 %copy-start.2 = (s32[96,128]{1,0:T(8,128)S(1)}, s32[96,128]{1,0:T(8,128)}, u32[]{:S(2)}) copy-start(s32[96,128]{1,0:T(8,128)} %weight_ref.5) | copy-start | bytes 147460
  2.2 11.0 %collective-permute-start = (bf16[2,224,128]{2,1,0:T(8,128)(2,1)S(1)}, bf16[2,224,128]{2,1,0:T(8,128)(2,1)S(1)}, u32[]{:S(2)}, u32[]{:S(2)}) collective-permute-start(bf16[2,224,128]{2,1,0:T(8,128)(2,1)S(1)} %get-tuple-element.11), channel_id=1, source_target_pairs={{0,1},{1,2},{2,3},{3,4},{4,5},{5,6},{6,7},{7,8},{8,9},{9,10},{10,1... | collective-permute-start | bytes 344072 | tf_op jit(solution)/shard_map/ppermute | solution.py:588
  6.2 7.1 %collective-permute-start.1 = (bf16[2,224,128]{2,1,0:T(8,128)(2,1)S(1)}, bf16[2,224,128]{2,1,0:T(8,128)(2,1)S(1)}, u32[]{:S(2)}, u32[]{:S(2)}) collective-permute-start(bf16[2,224,128]{2,1,0:T(8,128)(2,1)S(1)} %get-tuple-element.12), channel_id=1, source_target_pairs={{1,0},{2,1},{3,2},{4,3},{5,4},{6,5},{7,6},{8,7},{9,8},{10,9},{11,1... | collective-permute-start | bytes 344072 | tf_op jit(solution)/shard_map/ppermute | solution.py:589
  13.6 13.7 %collective-permute-start.2 = (bf16[224,256]{1,0:T(8,128)(2,1)S(1)}, bf16[224,256]{1,0:T(8,128)(2,1)S(1)}, u32[]{:S(2)}, u32[]{:S(2)}) collective-permute-start(bf16[224,256]{1,0:T(8,128)(2,1)S(1)} %get-tuple-element.14), channel_id=1, source_target_pairs={{0,32},{32,64},{64,96},{96,128},{128,160},{160,192},{192,224},{1,3... | collective-permute-start | bytes 344072 | tf_op jit(solution)/shard_map/ppermute | solution.py:593
  17.7 9.6 %collective-permute-start.3 = (bf16[224,256]{1,0:T(8,128)(2,1)S(1)}, bf16[224,256]{1,0:T(8,128)(2,1)S(1)}, u32[]{:S(2)}, u32[]{:S(2)}) collective-permute-start(bf16[224,256]{1,0:T(8,128)(2,1)S(1)} %get-tuple-element.15), channel_id=1, source_target_pairs={{32,0},{64,32},{96,64},{128,96},{160,128},{192,160},{224,192},{33,... | collective-permute-start | bytes 344072 | tf_op jit(solution)/shard_map/ppermute | solution.py:594
  19.6 2.6 %copy-start = (bf16[96,224,128]{2,1,0:T(8,128)(2,1)S(1)}, bf16[96,224,128]{2,1,0:T(8,128)(2,1)}, u32[]{:S(2)}) copy-start(bf16[96,224,128]{2,1,0:T(8,128)(2,1)} %get-tuple-element.10.xt_ref) | copy-start | bytes 16515076
  22.2 5.1 %copy-start.1 = (bf16[96,224,128]{2,1,0:T(8,128)(2,1)S(1)}, bf16[96,224,128]{2,1,0:T(8,128)(2,1)}, u32[]{:S(2)}) copy-start(bf16[96,224,128]{2,1,0:T(8,128)(2,1)} %get-tuple-element.10.xt_ref) | copy-start | bytes 16515076
  33.9 1.4 %collective-permute-start.4 = (f32[4,56,128]{2,1,0:T(8,128)S(1)}, f32[4,56,128]{2,1,0:T(8,128)S(1)}, u32[]{:S(2)}, u32[]{:S(2)}) collective-permute-start(f32[4,56,128]{2,1,0:T(8,128)S(1)} %fusion), channel_id=1, source_target_pairs={{0,32},{1,33},{2,34},{3,35},{4,36},{5,37},{6,38},{7,39},{8,40},{9,... | collective-permute-start | bytes 344072 | tf_op jit(solution)/shard_map/ppermute | solution.py:49
  35.4 6.0 %collective-permute-start.5 = (f32[56,128]{1,0:T(8,128)S(1)}, f32[56,128]{1,0:T(8,128)S(1)}, u32[]{:S(2)}, u32[]{:S(2)}) collective-permute-start(f32[56,128]{1,0:T(8,128)S(1)} %get-tuple-element.26), channel_id=1, source_target_pairs={{0,1},{1,0},{2,3},{3,2},{4,5},{5,4},{6,7},{7,6},{8,9},{9,8},{10,11... | collective-permute-start | bytes 86024 | tf_op jit(solution)/shard_map/ppermute | solution.py:54
  38.0 4.9 %collective-permute-start.6 = (f32[56,128]{1,0:T(8,128)S(1)}, f32[56,128]{1,0:T(8,128)S(1)}, u32[]{:S(2)}, u32[]{:S(2)}) collective-permute-start(f32[56,128]{1,0:T(8,128)S(1)} %get-tuple-element.25), channel_id=1, source_target_pairs={{0,2},{1,3},{2,0},{3,1},{4,6},{5,7},{6,4},{7,5},{8,10},{9,11},{10,... | collective-permute-start | bytes 86024 | tf_op jit(solution)/shard_map/ppermute | solution.py:54
  41.4 3.9 %collective-permute-start.7 = (f32[56,128]{1,0:T(8,128)S(1)}, f32[56,128]{1,0:T(8,128)S(1)}, u32[]{:S(2)}, u32[]{:S(2)}) collective-permute-start(f32[56,128]{1,0:T(8,128)S(1)} %get-tuple-element.24), channel_id=1, source_target_pairs={{0,3},{1,2},{2,1},{3,0},{4,7},{5,6},{6,5},{7,4},{8,11},{9,10},{10,... | collective-permute-start | bytes 86024 | tf_op jit(solution)/shard_map/ppermute | solution.py:54
  45.3 4.3 %collective-permute-start.10 = (f32[56,128]{1,0:T(8,128)S(1)}, f32[56,128]{1,0:T(8,128)S(1)}, u32[]{:S(2)}, u32[]{:S(2)}) collective-permute-start(f32[56,128]{1,0:T(8,128)S(1)} %fusion.3), channel_id=1, source_target_pairs={{0,192},{1,193},{2,194},{3,195},{4,196},{5,197},{6,198},{7,199},{8... | collective-permute-start | bytes 86024 | tf_op jit(solution)/shard_map/ppermute | solution.py:57
  48.3 2.7 %collective-permute-start.8 = (f32[56,128]{1,0:T(8,128)S(1)}, f32[56,128]{1,0:T(8,128)S(1)}, u32[]{:S(2)}, u32[]{:S(2)}) collective-permute-start(f32[56,128]{1,0:T(8,128)S(1)} %fusion.3), channel_id=1, source_target_pairs={{0,64},{1,65},{2,66},{3,67},{4,68},{5,69},{6,70},{7,71},{8,72},{9,... | collective-permute-start | bytes 86024 | tf_op jit(solution)/shard_map/ppermute | solution.py:57
  48.3 4.2 %collective-permute-start.9 = (f32[56,128]{1,0:T(8,128)S(1)}, f32[56,128]{1,0:T(8,128)S(1)}, u32[]{:S(2)}, u32[]{:S(2)}) collective-permute-start(f32[56,128]{1,0:T(8,128)S(1)} %fusion.3), channel_id=1, source_target_pairs={{0,128},{1,129},{2,130},{3,131},{4,132},{5,133},{6,134},{7,135},{8... | collective-permute-start | bytes 86024 | tf_op jit(solution)/shard_map/ppermute | solution.py:57
  52.6 7.1 %collective-permute-start.11 = (f32[56,128]{1,0:T(8,128)S(1)}, f32[56,128]{1,0:T(8,128)S(1)}, u32[]{:S(2)}, u32[]{:S(2)}) collective-permute-start(f32[56,128]{1,0:T(8,128)S(1)} %add_add_fusion.1), channel_id=1, source_target_pairs={{0,4},{1,5},{2,6},{3,7},{4,0},{5,1},{6,2},{7,3},{8,12},{9,13},{10,... | collective-permute-start | bytes 86024 | tf_op jit(solution)/shard_map/ppermute | solution.py:57
  54.3 7.0 %collective-permute-start.12 = (f32[56,128]{1,0:T(8,128)S(1)}, f32[56,128]{1,0:T(8,128)S(1)}, u32[]{:S(2)}, u32[]{:S(2)}) collective-permute-start(f32[56,128]{1,0:T(8,128)S(1)} %add_add_fusion.1), channel_id=1, source_target_pairs={{0,8},{1,9},{2,10},{3,11},{4,12},{5,13},{6,14},{7,15},{8,0},{9,1},... | collective-permute-start | bytes 86024 | tf_op jit(solution)/shard_map/ppermute | solution.py:57
  59.7 4.6 %collective-permute-start.13 = (f32[56,128]{1,0:T(8,128)S(1)}, f32[56,128]{1,0:T(8,128)S(1)}, u32[]{:S(2)}, u32[]{:S(2)}) collective-permute-start(f32[56,128]{1,0:T(8,128)S(1)} %add_add_fusion.1), channel_id=1, source_target_pairs={{0,12},{1,13},{2,14},{3,15},{4,8},{5,9},{6,10},{7,11},{8,4},{9,5},... | collective-permute-start | bytes 86024 | tf_op jit(solution)/shard_map/ppermute | solution.py:57
  64.3 4.0 %collective-permute-start.14 = (f32[56,128]{1,0:T(8,128)S(1)}, f32[56,128]{1,0:T(8,128)S(1)}, u32[]{:S(2)}, u32[]{:S(2)}) collective-permute-start(f32[56,128]{1,0:T(8,128)S(1)} %add_add_fusion), channel_id=1, source_target_pairs={{0,28},{1,29},{2,30},{3,31},{4,24},{5,25},{6,26},{7,27},{8,20},{9,... | collective-permute-start | bytes 86024 | tf_op jit(solution)/shard_map/ppermute | solution.py:57
  68.3 4.2 %collective-permute-start.15 = (f32[56,128]{1,0:T(8,128)S(1)}, f32[56,128]{1,0:T(8,128)S(1)}, u32[]{:S(2)}, u32[]{:S(2)}) collective-permute-start(f32[56,128]{1,0:T(8,128)S(1)} %add.77), channel_id=1, source_target_pairs={{0,2},{1,3},{2,0},{3,1},{4,6},{5,7},{6,4},{7,5},{8,10},{9,11},{10,... | collective-permute-start | bytes 86024 | tf_op jit(solution)/shard_map/ppermute | solution.py:62
  69.2 3.3 %collective-permute-start.16 = (f32[56,128]{1,0:T(8,128)S(1)}, f32[56,128]{1,0:T(8,128)S(1)}, u32[]{:S(2)}, u32[]{:S(2)}) collective-permute-start(f32[56,128]{1,0:T(8,128)S(1)} %add.77), channel_id=1, source_target_pairs={{0,1},{1,0},{2,3},{3,2},{4,5},{5,4},{6,7},{7,6},{8,9},{9,8},{10,11... | collective-permute-start | bytes 86024 | tf_op jit(solution)/shard_map/ppermute | solution.py:62
  69.5 3.9 %collective-permute-start.17 = (f32[56,128]{1,0:T(8,128)S(1)}, f32[56,128]{1,0:T(8,128)S(1)}, u32[]{:S(2)}, u32[]{:S(2)}) collective-permute-start(f32[56,128]{1,0:T(8,128)S(1)} %add.77), channel_id=1, source_target_pairs={{0,3},{1,2},{2,1},{3,0},{4,7},{5,6},{6,5},{7,4},{8,11},{9,10},{10,... | collective-permute-start | bytes 86024 | tf_op jit(solution)/shard_map/ppermute | solution.py:62
  73.5 9.2 %collective-permute-start.18 = (f32[4,56,128]{2,1,0:T(8,128)S(1)}, f32[4,56,128]{2,1,0:T(8,128)S(1)}, u32[]{:S(2)}, u32[]{:S(2)}) collective-permute-start(f32[4,56,128]{2,1,0:T(8,128)S(1)} %pad_maximum_fusion.1), channel_id=1, source_target_pairs={{0,32},{1,33},{2,34},{3,35},{4,36},{5,37},{6,38},{7,39},{8,40},{9,... | collective-permute-start | bytes 344072 | tf_op jit(solution)/shard_map/ppermute | solution.py:70

commit v3 on v2

--- a/solution.py
+++ b/solution.py
@@ -31,8 +31,8 @@
 
 SIZES = (4, 8, 4)
 CORE_SWAP = flat_pairs(SIZES, lambda y, c, z, x: (y, 1 - c, z, x))
-X_PAIRS = [flat_pairs(SIZES, lambda y, c, z, x, k=k: (y, c, z, x ^ k)) for k in (1, 2, 3)]
 STAGES = (
+    [flat_pairs(SIZES, lambda y, c, z, x, k=k: (y, c, z, x ^ k)) for k in (1, 2, 3)],
     [flat_pairs(SIZES, lambda y, c, z, x, k=k: (y ^ k, c, z, x)) for k in (1, 2, 3)],
     [flat_pairs(SIZES, lambda y, c, z, x, k=k: (y, c, z ^ k, x)) for k in (1, 2, 3)],
     [flat_pairs(SIZES, lambda y, c, z, x: (y, c, 7 - z, x))],
@@ -41,35 +41,18 @@
 
 
 def total_of(value):
-    half = value.shape[1] // 2
-    core = lax.axis_index("group") % 2
-    x = lax.axis_index("tile") % 4
-    own = lax.dynamic_slice_in_dim(value, core * half, half, axis=1)
-    other = lax.dynamic_slice_in_dim(value, (1 - core) * half, half, axis=1)
-    mine = own + lax.ppermute(other, AXES, CORE_SWAP)
-
-    def block(index):
-        return lax.dynamic_index_in_dim(mine, index, axis=0, keepdims=False)
-
-    parts = [lax.ppermute(block(x ^ k), AXES, X_PAIRS[k - 1]) for k in (1, 2, 3)]
-    piece = (block(x) + parts[0]) + (parts[1] + parts[2])
+    first = lax.axis_index("group") % 2 == 0
+    own = jnp.where(first, value[0], value[1])
+    other = jnp.where(first, value[1], value[0])
+    own = own + lax.ppermute(other, AXES, CORE_SWAP)
     for stage in STAGES:
-        parts = [lax.ppermute(piece, AXES, pairs) for pairs in stage]
+        parts = [lax.ppermute(own, AXES, pairs) for pairs in stage]
         if len(parts) == 1:
-            piece = piece + parts[0]
+            own = own + parts[0]
         else:
-            piece = (piece + parts[0]) + (parts[1] + parts[2])
-    got = [piece] + [lax.ppermute(piece, AXES, pairs) for pairs in X_PAIRS]
-    blocks = []
-    for place in range(4):
-        value = got[3]
-        for k in (0, 1, 2):
-            value = jnp.where(x == place ^ k, got[k], value)
-        blocks.append(value)
-    mine = jnp.stack(blocks)
-    other = lax.ppermute(mine, AXES, CORE_SWAP)
-    first = core == 0
-    return jnp.concatenate([jnp.where(first, mine, other), jnp.where(first, other, mine)], axis=1)
+            own = (own + parts[0]) + (parts[1] + parts[2])
+    other = lax.ppermute(own, AXES, CORE_SWAP)
+    return jnp.stack([jnp.where(first, own, other), jnp.where(first, other, own)])
 
 
 def split_three(value):
@@ -146,12 +129,36 @@
     )
 
 
-def rows_first_kernel(x_ref, out_ref, side_ref, slab_ref, turned_ref, in_sems, out_sems):
+def noise_rows(row_of, weight_ref, rows, moment_ref, first_ref):
+    parts = []
+    total = None
+    for r in rows:
+        value = row_of(r) - 0.5 * (row_of(r - 1) + row_of(r + 1))
+        value = value * weight_ref[r : r + 1, :].astype(F32)
+        total = value if total is None else total + value
+        parts.append(value.astype(BF16))
+    first_ref[...] += total
+    flat = jnp.concatenate(parts, axis=1)
+    moment_ref[...] += lax.dot_general(
+        flat, flat, (((1,), (1,)), ((), ())), preferred_element_type=F32
+    )
+
+
+def rows_first_kernel(
+    x_ref, weight_ref, out_ref, side_ref, moment_ref, first_ref,
+    slab_ref, turned_ref, in_sems, out_sems,
+):
     slabs, bands, _, cols = slab_ref.shape
+    rows = 16 * slabs
+
+    def row_of(r):
+        return turned_ref[r].astype(F32)
+
     inward = [
         pltpu.make_async_copy(x_ref.at[:, pl.ds(16 * s, 16), :], slab_ref.at[s], in_sems.at[s])
         for s in range(slabs)
     ]
+    due = {begin: range(begin, end) for begin, end in spans_of(slabs)}
     outward = [
         pltpu.make_async_copy(
             turned_ref.at[pl.ds(16 * s, 16)], out_ref.at[pl.ds(16 * s, 16)], out_sems.at[s]
@@ -160,10 +167,13 @@
     ]
     for copy in inward:
         copy.start()
+    moment_ref[...] = jnp.zeros_like(moment_ref)
+    first_ref[...] = jnp.zeros_like(first_ref)
     pick = side_picker(cols)
     sums = [[jnp.zeros((bands, 128), F32) for _ in range(2)] for _ in range(2)]
     for s in range(slabs):
-        inward[s].wait()
+        for later in due.get(s, ()):
+            inward[later].wait()
         turned_ref[16 * s : 16 * s + 16] = jnp.swapaxes(slab_ref[s], 0, 1)
         outward[s].start()
         for g in (2 * s, 2 * s + 1):
@@ -171,13 +181,18 @@
             low, high = side_lanes_of(pieces, pick, g)
             sums[0][g // 8] += low
             sums[1][g // 8] += high
+        start = max(16 * s - 7, 1)
+        for base in range(start, 16 * s + 15, 8):
+            stop = min(base + 8, 16 * s + 9 if s < slabs - 1 else rows - 1)
+            if base < stop:
+                noise_rows(row_of, weight_ref, range(base, stop), moment_ref, first_ref)
     for side in range(2):
         side_ref[side] = jnp.concatenate(sums[side], axis=1).astype(BF16)
     for copy in outward:
         copy.wait()
 
 
-def rows_first(x):
+def rows_first(x, weight):
     bands, rows, cols = x.shape
     slabs = rows // 16
     return pl.pallas_call(
@@ -185,9 +200,11 @@
         out_shape=(
             pltpu.HBM((rows, bands, cols), BF16),
             jax.ShapeDtypeStruct((2, bands, 256), BF16),
+            jax.ShapeDtypeStruct((bands, bands), F32),
+            jax.ShapeDtypeStruct((bands, cols), F32),
         ),
-        in_specs=[HBM_SPEC],
-        out_specs=(HBM_SPEC, VMEM_SPEC),
+        in_specs=[HBM_SPEC, VMEM_SPEC],
+        out_specs=(HBM_SPEC, VMEM_SPEC, VMEM_SPEC, VMEM_SPEC),
         scratch_shapes=[
             pltpu.VMEM((slabs, bands, 16, cols), BF16),
             pltpu.VMEM((rows, bands, cols), BF16),
@@ -195,33 +212,64 @@
             pltpu.SemaphoreType.DMA((slabs,)),
         ],
         compiler_params=params(20),
-        cost_estimate=cost(2 * bands * rows * cols * 32, 4 * bands * rows * cols),
+        cost_estimate=cost(2 * bands * bands * rows * cols, 4 * bands * rows * cols),
         name="rows_first",
-    )(in_hbm(x))
-
-
-def corners_kernel(side_ref, up_ref, down_ref, low_ref, high_ref):
+    )(in_hbm(x), weight)
+
+
+def put_folded(out_ref, moment_ref, first_ref, count):
+    half = moment_ref.shape[0] // 2
+    first = jnp.sum(first_ref[...], axis=1, keepdims=True)
+    folded = fold(moment_ref[...], [first[:half], first[half:], count])
+    out_ref[0] = folded[:, :128]
+    out_ref[1] = folded[:, 128:]
+
+
+def corners_kernel(
+    side_ref, up_ref, down_ref, top_ref, bottom_ref, weight_ref, noise_ref, noise_first_ref,
+    low_ref, high_ref, out_ref, moment_ref, first_ref,
+):
     bands, cols = up_ref.shape[1:]
+    rows = weight_ref.shape[0]
     zero = jnp.zeros((bands, cols), BF16)
     pieces = [up_ref[0], up_ref[1], down_ref[0], down_ref[1]] + [zero] * 4
     parts = side_lanes_of(pieces, side_picker(cols), CORNER_GROUP)
-    for side, out_ref in ((0, low_ref), (1, high_ref)):
-        out_ref[:, :128] = side_ref[side][:, :128]
-        out_ref[:, 128:] = (side_ref[side][:, 128:].astype(F32) + parts[side]).astype(BF16)
-
-
-def side_columns(side, up, down):
+    for side, side_out_ref in ((0, low_ref), (1, high_ref)):
+        side_out_ref[:, :128] = side_ref[side][:, :128]
+        side_out_ref[:, 128:] = (side_ref[side][:, 128:].astype(F32) + parts[side]).astype(BF16)
+
+    def row_of(r):
+        if r < 2:
+            row = up_ref[1] if r < 0 else top_ref[r]
+        else:
+            row = down_ref[0] if r == rows else bottom_ref[r - rows + 2]
+        return row.astype(F32)
+
+    moment_ref[...] = noise_ref[...]
+    first_ref[...] = noise_first_ref[...]
+    noise_rows(row_of, weight_ref, (0, rows - 1), moment_ref, first_ref)
+    count = jnp.sum(weight_ref[...].astype(F32), keepdims=True)
+    put_folded(out_ref, moment_ref, first_ref, count)
+
+
+def side_columns(side, up, down, top, bottom, weight, noise, noise_first):
     bands = side.shape[1]
     shape = jax.ShapeDtypeStruct((bands, 256), BF16)
     return pl.pallas_call(
         corners_kernel,
-        out_shape=(shape, shape),
-        in_specs=[VMEM_SPEC] * 3,
-        out_specs=(VMEM_SPEC, VMEM_SPEC),
-        compiler_params=params(8),
+        out_shape=(shape, shape, jax.ShapeDtypeStruct((2, bands // 2, 128), F32)),
+        in_specs=[VMEM_SPEC] * 8,
+        out_specs=(VMEM_SPEC,) * 3,
+        scratch_shapes=[pltpu.VMEM((bands, bands), F32), pltpu.VMEM(noise_first.shape, F32)],
+        compiler_params=params(10),
         cost_estimate=cost(2 * bands * 1024 * 128, 6 * bands * 256),
         name="side_columns",
-    )(side, up, down)
+    )(side, up, down, top, bottom, weight, noise, noise_first)
+
+
+def spans_of(count):
+    marks = (0, count // 6, count // 2, count)
+    return list(zip(marks[:-1], marks[1:]))
 
 
 def group_copy(source_ref, target_ref, sems, g):
@@ -258,65 +306,6 @@
     row = lax.broadcasted_iota(jnp.int32, (size, 256), 0)
     lane = lax.broadcasted_iota(jnp.int32, (size, 256), 1)
     return part + jnp.where(row == lane, 0.0, turned)
-
-
-def noise_kernel(xt_ref, up_ref, down_ref, weight_ref, out_ref, moment_ref, first_ref):
-    rows, bands, cols = xt_ref.shape
-    groups = rows // GROUP
-    moment_ref[...] = jnp.zeros_like(moment_ref)
-    first_ref[...] = jnp.zeros_like(first_ref)
-
-    def step(weights, field):
-        parts = []
-        total = None
-        for i in range(GROUP):
-            value = field[i + 1] - 0.5 * (field[i] + field[i + 2])
-            value = value * weights[i : i + 1, :]
-            total = value if total is None else total + value
-            parts.append(value.astype(BF16))
-        first_ref[...] += total
-        flat = jnp.concatenate(parts, axis=1)
-        moment_ref[...] += lax.dot_general(
-            flat, flat, (((1,), (1,)), ((), ())), preferred_element_type=F32
-        )
-
-    def weights_of(g):
-        return weight_ref[pl.ds(pl.multiple_of(g * GROUP, GROUP), GROUP), :].astype(F32)
-
-    def load(r):
-        return xt_ref[r].astype(F32)
-
-    step(weights_of(0), [up_ref[1].astype(F32)] + [load(r) for r in range(GROUP + 1)])
-
-    @pl.loop(1, groups - 1)
-    def _(g):
-        step(weights_of(g), [load(g * GROUP + i - 1) for i in range(GROUP + 2)])
-
-    base = rows - GROUP
-    step(
-        weights_of(groups - 1),
-        [load(base + i - 1) for i in range(GROUP + 1)] + [down_ref[0].astype(F32)],
-    )
-    first = jnp.sum(first_ref[...], axis=1, keepdims=True)
-    count = jnp.sum(weight_ref[...].astype(F32), keepdims=True)
-    half = bands // 2
-    folded = fold(moment_ref[...], [first[:half], first[half:], count])
-    out_ref[0] = folded[:, :128]
-    out_ref[1] = folded[:, 128:]
-
-
-def noise_moments(xt, up, down, weight):
-    rows, bands, cols = xt.shape
-    return pl.pallas_call(
-        noise_kernel,
-        out_shape=jax.ShapeDtypeStruct((2, bands // 2, 128), F32),
-        in_specs=[VMEM_SPEC] * 4,
-        out_specs=VMEM_SPEC,
-        scratch_shapes=[pltpu.VMEM((bands, bands), F32), pltpu.VMEM((bands, cols), F32)],
-        compiler_params=params(6),
-        cost_estimate=cost(2 * bands * bands * rows * cols, 2 * bands * rows * cols),
-        name="noise_moments",
-    )(in_vmem(xt), up, down, weight)
 
 
 def signal_kernel(
@@ -410,12 +399,7 @@
         column_pass(g + 2)
         row_pass(g)
 
-    first = jnp.sum(first_ref[...], axis=1, keepdims=True)
-    count = jnp.sum(weight_ref[...].astype(F32), keepdims=True)
-    half = bands // 2
-    folded = fold(moment_ref[...], [first[:half], first[half:], count])
-    out_ref[0] = folded[:, :128]
-    out_ref[1] = folded[:, 128:]
+    put_folded(out_ref, moment_ref, first_ref, jnp.sum(weight_ref[...].astype(F32), keepdims=True))
     for g in range(groups):
         group_copy(smooth_ref, result_ref, sems, g).wait()
 
@@ -443,8 +427,8 @@
     )(in_vmem(xt), up, down, low, high, weight)
 
 
-def folded_of(sums_ref, which):
-    return jnp.concatenate([sums_ref[2 * which], sums_ref[2 * which + 1]], axis=1)
+def folded_of(sums_ref):
+    return jnp.concatenate([sums_ref[0], sums_ref[1]], axis=1)
 
 
 def sums_of(folded):
@@ -506,28 +490,27 @@
 
 
 def finish_kernel(
-    sums_ref, weight_ref, field_ref, result_ref, cov_ref,
+    noise_ref, signal_ref, weight_ref, field_ref, result_ref, cov_ref,
     work_ref, smooth_ref, out_ref, in_sems, out_sems,
 ):
     rows, bands, cols = smooth_ref.shape
     groups, slabs = rows // GROUP, rows // 16
     for g in range(groups):
         group_copy(field_ref, smooth_ref, in_sems, g).start()
-    work_ref[...] = covariance_of(folded_of(sums_ref, 0))
+    work_ref[...] = covariance_of(folded_of(noise_ref))
     factor_into(work_ref, bands)
     inverse = work_ref[:, :bands]
     inverse_cast = inverse.astype(BF16)
-    first, count = sums_of(folded_of(sums_ref, 1))
+    first, count = sums_of(folded_of(signal_ref))
     mean = jnp.broadcast_to(first / count, (bands, cols))
 
     def outward(s):
-        window = pl.ds(16 * s if isinstance(s, int) else pl.multiple_of(16 * s, 16), 16)
+        window = pl.ds(16 * s, 16)
         return pltpu.make_async_copy(out_ref.at[s], result_ref.at[:, window, :], out_sems.at[s])
 
-    @pl.loop(0, slabs)
-    def _(s):
-        base = pl.multiple_of(16 * s, 16)
-        weights = weight_ref[pl.ds(base, 16), :].astype(F32)
+    for s in range(slabs):
+        base = 16 * s
+        weights = weight_ref[base : base + 16, :].astype(F32)
         parts = []
         for pair in range(8):
             if pair % 4 == 0:
@@ -543,7 +526,7 @@
         out_ref[s] = jnp.swapaxes(jnp.concatenate(parts, axis=0), 0, 1)
         outward(s).start()
 
-    cov = covariance_of(folded_of(sums_ref, 1))[:, :bands]
+    cov = covariance_of(folded_of(signal_ref))[:, :bands]
     left = jnp.dot(inverse, cov, precision=lax.Precision.HIGHEST, preferred_element_type=F32)
     cov_ref[...] = lax.dot_general(
         left, inverse, (((1,), (1,)), ((), ())),
@@ -553,7 +536,7 @@
         outward(s).wait()
 
 
-def finish(sums, weight, smooth):
+def finish(noise, signal, weight, smooth):
     rows, bands, cols = smooth.shape
     groups, slabs = rows // GROUP, rows // 16
     return pl.pallas_call(
@@ -562,7 +545,7 @@
             pltpu.HBM((bands, rows, cols), BF16),
             jax.ShapeDtypeStruct((bands, bands), F32),
         ),
-        in_specs=[VMEM_SPEC, VMEM_SPEC, HBM_SPEC],
+        in_specs=[VMEM_SPEC, VMEM_SPEC, VMEM_SPEC, HBM_SPEC],
         out_specs=(HBM_SPEC, VMEM_SPEC),
         scratch_shapes=[
             pltpu.VMEM((bands, 256), F32),
@@ -574,7 +557,7 @@
         compiler_params=params(36),
         cost_estimate=cost(2 * bands * bands * rows * cols, 6 * bands * rows * cols),
         name="finish",
-    )(sums, weight, in_hbm(smooth))
+    )(noise, signal, weight, in_hbm(smooth))
 
 
 def line(count):
@@ -587,15 +570,15 @@
     forward, backward = line(lax.axis_size("tile"))
     up = lax.ppermute(last, "tile", forward)
     down = lax.ppermute(first, "tile", backward)
-    xt, side = rows_first(radiance)
-    to_low, to_high = side_columns(side, up, down)
+    xt, side, noise, noise_first = rows_first(radiance, valid_mask)
+    to_low, to_high, noise = side_columns(
+        side, up, down, first, last, valid_mask, noise, noise_first
+    )
     forward, backward = line(lax.axis_size("group"))
     low = lax.ppermute(to_high, "group", forward)
     high = lax.ppermute(to_low, "group", backward)
-    noise = noise_moments(xt, up, down, valid_mask)
     smooth, signal = signal_moments(xt, up, down, low, high, valid_mask)
-    sums = total_of(jnp.concatenate([noise, signal], axis=0))
-    whitened, whitened_cov = finish(sums, valid_mask, smooth)
+    whitened, whitened_cov = finish(total_of(noise), total_of(signal), valid_mask, smooth)
     return (whitened, whitened_cov)
 
 

time: 97.6 us -> 94.3 us (0.966)
  waiting for transfers between devices: 18.5 us -> 3.45 us
  starting transfers between devices: 41.3 us -> 55.9 us
  Pallas kernels: 33.7 us -> 30.9 us
    ppermute x15 -> x24, starting transfers between devices: 30.1 us -> 45.6 us  [the longest x20 34.9 us: total_of(): parts = [lax.ppermute(own, AXES, pairs) for pairs in stage]]
    ppermute x15 -> x24, waiting for transfers between devices: 18.5 us -> 3.41 us  [the longest x20 2.52 us: total_of(): parts = [lax.ppermute(own, AXES, pairs) for pairs in stage]]
    pallas_call x2 -> x1, Pallas kernels: 5.45 us -> 0.43 us  [side_columns(): pl.pallas_call(corners_kernel, out_shape=(shape, shape, jax.ShapeDtypeStr...]
    pallas_call x1, Pallas kernels: 5.74 us -> 7.99 us  [rows_first(): pl.pallas_call(rows_first_kernel, out_shape=(pltpu.HBM((rows, bands, cols...]
    unnamed x6 -> x4, local copies, waits for them, and re-layouts: 2.56 us -> 2.57 us
  transfers between devices with their start and end apart: 19 -> 28, of which waited for: 11 -> 4; matrix products, arithmetic and copies ran while one was open for 0% -> 0% of each run, Pallas kernels for 11% -> 16%
where the time goes in v3:
time: 94.3 us; the launch traced here: 94 us
  starting transfers between devices  55.9 us (59%)
  Pallas kernels  30.9 us (33%)
  waiting for transfers between devices  3.45 us (4%)
  local copies, waits for them, and re-layouts  2.57 us (3%)
  between operations  1.08 us (1%)
    ppermute x20, starting transfers between devices, total_of(): parts = [lax.ppermute(own, AXES, pairs) for pairs in stage]  34.9 us
    pallas_call x1, Pallas kernels, finish(): pl.pallas_call(finish_kernel, out_shape=(pltpu.HBM((bands, rows, cols), B...  14.3 us
    ppermute x2, starting transfers between devices, total_of(): other = lax.ppermute(own, AXES, CORE_SWAP)  9.54 us
    pallas_call x1, Pallas kernels, rows_first(): pl.pallas_call(rows_first_kernel, out_shape=(pltpu.HBM((rows, bands, cols...  7.99 us
    pallas_call x1, Pallas kernels, signal_moments(): pl.pallas_call(signal_kernel, out_shape=(pltpu.HBM((rows, bands, cols), F...  6.62 us
    ppermute x1, starting transfers between devices, body(): up = lax.ppermute(last, 'tile', forward)  3.95 us
    ppermute x1, starting transfers between devices, body(): low = lax.ppermute(to_high, 'group', forward)  3.1 us
    unnamed x4, local copies, waits for them, and re-layouts  2.57 us
  transfers between devices with their start and end apart: 28, of which 4 were waited for; matrix products, arithmetic and copies ran while one was open for 0% of the time, Pallas kernels for 16%

profile of v3, /device:TPU:1, one launch (start us, length us, event | category | flops | bytes accessed | tf_op | source)
XLA Modules:
  0.0 94.0 jit_solution(13138626568191913943)
XLA Ops:
  0.6 1.6 %edge_rows.1 = (bf16[2,224,128]{2,1,0:T(8,128)(2,1)S(1)}, bf16[2,224,128]{2,1,0:T(8,128)(2,1)S(1)}) custom-call(bf16[224,96,128]{2,1,0:T(8,128)(2,1)} %x_ref.3), custom_call_target="tpu_custom_call" | custom-call | bytes 1835008 | tf_op jit(solution)/shard_map/edge_rows/pallas_call | solution.py:97
  2.2 4.0 %collective-permute-start = (bf16[2,224,128]{2,1,0:T(8,128)(2,1)S(1)}, bf16[2,224,128]{2,1,0:T(8,128)(2,1)S(1)}, u32[]{:S(2)}, u32[]{:S(2)}) collective-permute-start(bf16[2,224,128]{2,1,0:T(8,128)(2,1)S(1)} %get-tuple-element.14.bottom_ref), channel_id=1, source_target_pairs={{0,1},{1,2},{2,3},{3,4},{4,5},{5,6},{6,7},{7,8},{8,9},{9,10},{10,1... | collective-permute-start | bytes 344072 | tf_op jit(solution)/shard_map/ppermute | solution.py:571
  6.2 1.3 %collective-permute-start.1 = (bf16[2,224,128]{2,1,0:T(8,128)(2,1)S(1)}, bf16[2,224,128]{2,1,0:T(8,128)(2,1)S(1)}, u32[]{:S(2)}, u32[]{:S(2)}) collective-permute-start(bf16[2,224,128]{2,1,0:T(8,128)(2,1)S(1)} %get-tuple-element.15.top_ref), channel_id=1, source_target_pairs={{1,0},{2,1},{3,2},{4,3},{5,4},{6,5},{7,6},{8,7},{9,8},{10,9},{11,1... | collective-permute-start | bytes 344072 | tf_op jit(solution)/shard_map/ppermute | solution.py:572
  7.5 8.0 %rows_first.1 = (bf16[96,224,128]{2,1,0:T(8,128)(2,1)}, bf16[2,224,256]{2,1,0:T(8,128)(2,1)S(1)}, f32[224,224]{1,0:T(8,128)S(1)}, f32[224,128]{1,0:T(8,128)S(1)}) custom-call(bf16[224,96,128]{2,1,0:T(8,128)(2,1)} %x_ref.3, s32[96,128]{1,0:T(8,128)S(1)} %copy-done), custom_call_target="tpu_custom_call" | custom-call | flops 1233125376 | bytes 11010048 | tf_op jit(solution)/shard_map/rows_first/pallas_call | solution.py:198
  15.5 0.4 side_columns.1
  16.0 1.0 %collective-permute-start.2 = (f32[112,128]{1,0:T(8,128)S(1)}, f32[112,128]{1,0:T(8,128)S(1)}, u32[]{:S(2)}, u32[]{:S(2)}) collective-permute-start(f32[112,128]{1,0:T(8,128)S(1)} %select_bitcast_fusion.5), channel_id=1, source_target_pairs={{0,32},{1,33},{2,34},{3,35},{4,36},{5,37},{6,38},{7,39},{8,40},{9,... | collective-permute-start | bytes 172040 | tf_op jit(solution)/shard_map/ppermute | solution.py:47
  17.0 3.1 %collective-permute-start.14 = (bf16[224,256]{1,0:T(8,128)(2,1)S(1)}, bf16[224,256]{1,0:T(8,128)(2,1)S(1)}, u32[]{:S(2)}, u32[]{:S(2)}) collective-permute-start(bf16[224,256]{1,0:T(8,128)(2,1)S(1)} %get-tuple-element.20), channel_id=1, source_target_pairs={{0,32},{32,64},{64,96},{96,128},{128,160},{160,192},{192,224},{1,3... | collective-permute-start | bytes 344072 | tf_op jit(solution)/shard_map/ppermute | solution.py:578
  20.1 1.9 %collective-permute-start.15 = (bf16[224,256]{1,0:T(8,128)(2,1)S(1)}, bf16[224,256]{1,0:T(8,128)(2,1)S(1)}, u32[]{:S(2)}, u32[]{:S(2)}) collective-permute-start(bf16[224,256]{1,0:T(8,128)(2,1)S(1)} %get-tuple-element.21), channel_id=1, source_target_pairs={{32,0},{64,32},{96,64},{128,96},{160,128},{192,160},{224,192},{33,... | collective-permute-start | bytes 344072 | tf_op jit(solution)/shard_map/ppermute | solution.py:579
  22.1 3.7 %collective-permute-start.5 = (f32[112,128]{1,0:T(8,128)S(1)}, f32[112,128]{1,0:T(8,128)S(1)}, u32[]{:S(2)}, u32[]{:S(2)}) collective-permute-start(f32[112,128]{1,0:T(8,128)S(1)} %bitcast_add_fusion.1), channel_id=1, source_target_pairs={{0,3},{1,2},{2,1},{3,0},{4,7},{5,6},{6,5},{7,4},{8,11},{9,10},{10,... | collective-permute-start | bytes 172040 | tf_op jit(solution)/shard_map/ppermute | solution.py:49
  25.8 0.5 collective-permute-start.4
  26.5 2.6 %copy-done.1 = bf16[96,224,128]{2,1,0:T(8,128)(2,1)S(1)} copy-done((bf16[96,224,128]{2,1,0:T(8,128)(2,1)S(1)}, bf16[96,224,128]{2,1,0:T(8,128)(2,1)}, u32[]{:S(2)}) %copy-start.1) | copy-done | bytes 5505048
  29.1 6.6 %signal_moments.1 = (f32[96,224,128]{2,1,0:T(8,128)}, f32[2,112,128]{2,1,0:T(8,128)S(1)}) custom-call(bf16[96,224,128]{2,1,0:T(8,128)(2,1)S(1)} %copy-done.1, bf16[2,224,128]{2,1,0:T(8,128)(2,1)S(1)} %collective-permute-done.up_ref, bf16[2,224,128]{2,1,0:T(8,128)(2,1)S(1)} %collective-permute-done.1.down_ref, ...), custom_call_target="tpu_custom_call" | custom-call | flops 2466250752 | bytes 16515072 | tf_op jit(solution)/shard_map/signal_moments/pallas_call | solution.py:409
  35.9 3.9 %collective-permute-start.8 = (f32[112,128]{1,0:T(8,128)S(1)}, f32[112,128]{1,0:T(8,128)S(1)}, u32[]{:S(2)}, u32[]{:S(2)}) collective-permute-start(f32[112,128]{1,0:T(8,128)S(1)} %add_add_fusion.5), channel_id=1, source_target_pairs={{0,192},{1,193},{2,194},{3,195},{4,196},{5,197},{6,198},{7,199},{8... | collective-permute-start | bytes 172040 | tf_op jit(solution)/shard_map/ppermute | solution.py:49
  39.7 0.3 collective-permute-start.7
  40.1 0.3 collective-permute-start.6
  40.4 2.9 %collective-permute-start.19 = (f32[112,128]{1,0:T(8,128)S(1)}, f32[112,128]{1,0:T(8,128)S(1)}, u32[]{:S(2)}, u32[]{:S(2)}) collective-permute-start(f32[112,128]{1,0:T(8,128)S(1)} %bitcast_add_fusion), channel_id=1, source_target_pairs={{0,3},{1,2},{2,1},{3,0},{4,7},{5,6},{6,5},{7,4},{8,11},{9,10},{10,... | collective-permute-start | bytes 172040 | tf_op jit(solution)/shard_map/ppermute | solution.py:49
  43.4 0.5 collective-permute-start.18
  44.3 6.9 %collective-permute-start.11 = (f32[112,128]{1,0:T(8,128)S(1)}, f32[112,128]{1,0:T(8,128)S(1)}, u32[]{:S(2)}, u32[]{:S(2)}) collective-permute-start(f32[112,128]{1,0:T(8,128)S(1)} %add_add_fusion.4), channel_id=1, source_target_pairs={{0,12},{1,13},{2,14},{3,15},{4,8},{5,9},{6,10},{7,11},{8,4},{9,5},... | collective-permute-start | bytes 172040 | tf_op jit(solution)/shard_map/ppermute | solution.py:49
  51.2 0.4 collective-permute-start.9
  51.6 2.2 %collective-permute-start.22 = (f32[112,128]{1,0:T(8,128)S(1)}, f32[112,128]{1,0:T(8,128)S(1)}, u32[]{:S(2)}, u32[]{:S(2)}) collective-permute-start(f32[112,128]{1,0:T(8,128)S(1)} %add_add_fusion.2), channel_id=1, source_target_pairs={{0,192},{1,193},{2,194},{3,195},{4,196},{5,197},{6,198},{7,199},{8... | collective-permute-start | bytes 172040 | tf_op jit(solution)/shard_map/ppermute | solution.py:49
  53.8 0.5 collective-permute-start.21
  54.3 0.7 collective-permute-start.20
  55.0 0.5 collective-permute-done.10
  55.5 4.7 %collective-permute-start.12 = (f32[112,128]{1,0:T(8,128)S(1)}, f32[112,128]{1,0:T(8,128)S(1)}, u32[]{:S(2)}, u32[]{:S(2)}) collective-permute-start(f32[112,128]{1,0:T(8,128)S(1)} %add_add_fusion.3), channel_id=1, source_target_pairs={{0,28},{1,29},{2,30},{3,31},{4,24},{5,25},{6,26},{7,27},{8,20},{9,... | collective-permute-start | bytes 172040 | tf_op jit(solution)/shard_map/ppermute | solution.py:49
  60.2 2.2 %collective-permute-start.25 = (f32[112,128]{1,0:T(8,128)S(1)}, f32[112,128]{1,0:T(8,128)S(1)}, u32[]{:S(2)}, u32[]{:S(2)}) collective-permute-start(f32[112,128]{1,0:T(8,128)S(1)} %add_add_fusion.1), channel_id=1, source_target_pairs={{0,12},{1,13},{2,14},{3,15},{4,8},{5,9},{6,10},{7,11},{8,4},{9,5},... | collective-permute-start | bytes 172040 | tf_op jit(solution)/shard_map/ppermute | solution.py:49
  62.4 1.4 %collective-permute-start.23 = (f32[112,128]{1,0:T(8,128)S(1)}, f32[112,128]{1,0:T(8,128)S(1)}, u32[]{:S(2)}, u32[]{:S(2)}) collective-permute-start(f32[112,128]{1,0:T(8,128)S(1)} %add_add_fusion.1), channel_id=1, source_target_pairs={{0,4},{1,5},{2,6},{3,7},{4,0},{5,1},{6,2},{7,3},{8,12},{9,13},{10,... | collective-permute-start | bytes 172040 | tf_op jit(solution)/shard_map/ppermute | solution.py:49
  63.9 4.1 %collective-permute-start.13 = (f32[112,128]{1,0:T(8,128)S(1)}, f32[112,128]{1,0:T(8,128)S(1)}, u32[]{:S(2)}, u32[]{:S(2)}) collective-permute-start(f32[112,128]{1,0:T(8,128)S(1)} %add.82), channel_id=1, source_target_pairs={{0,32},{1,33},{2,34},{3,35},{4,36},{5,37},{6,38},{7,39},{8,40},{9,... | collective-permute-start | bytes 172040 | tf_op jit(solution)/shard_map/ppermute | solution.py:54
  68.0 3.4 %collective-permute-start.26 = (f32[112,128]{1,0:T(8,128)S(1)}, f32[112,128]{1,0:T(8,128)S(1)}, u32[]{:S(2)}, u32[]{:S(2)}) collective-permute-start(f32[112,128]{1,0:T(8,128)S(1)} %add_add_fusion), channel_id=1, source_target_pairs={{0,28},{1,29},{2,30},{3,31},{4,24},{5,25},{6,26},{7,27},{8,20},{9,... | collective-permute-start | bytes 172040 | tf_op jit(solution)/shard_map/ppermute | solution.py:49
  71.4 1.7 %collective-permute-done.26 = f32[112,128]{1,0:T(8,128)S(1)} collective-permute-done((f32[112,128]{1,0:T(8,128)S(1)}, f32[112,128]{1,0:T(8,128)S(1)}, u32[]{:S(2)}, u32[]{:S(2)}) %collective-permute-start.26) | collective-permute-done | bytes 57376 | tf_op jit(solution)/shard_map/ppermute | solution.py:49
  73.2 5.4 %collective-permute-start.27 = (f32[112,128]{1,0:T(8,128)S(1)}, f32[112,128]{1,0:T(8,128)S(1)}, u32[]{:S(2)}, u32[]{:S(2)}) collective-permute-start(f32[112,128]{1,0:T(8,128)S(1)} %add.93), channel_id=1, source_target_pairs={{0,32},{1,33},{2,34},{3,35},{4,36},{5,37},{6,38},{7,39},{8,40},{9,... | collective-permute-start | bytes 172040 | tf_op jit(solution)/shard_map/ppermute | solution.py:54
  78.6 0.9 collective-permute-done.27
  79.6 14.3 %finish.1 = (bf16[224,96,128]{2,1,0:T(8,128)(2,1)}, f32[224,224]{1,0:T(8,128)}) custom-call(f32[2,112,128]{2,1,0:T(8,128)S(1)} %pad_maximum_fusion.noise_ref, f32[2,112,128]{2,1,0:T(8,128)S(1)} %pad_maximum_fusion.1.signal_ref, s32[96,128]{1,0:T(8,128)S(1)} %copy-done, f32[96,224,128]{2,1,0:T(8,128)} %get-tuple-element.23.field_ref), custom_call_target="tpu_custom_call" | custom-call | flops 1233125376 | bytes 16515072 | tf_op jit(solution)/shard_map/finish/pallas_call | solution.py:542
  (49 shorter events, 0.9 us)
Async XLA Ops:
  0.6 6.9 %copy-start = (s32[96,128]{1,0:T(8,128)S(1)}, s32[96,128]{1,0:T(8,128)}, u32[]{:S(2)}) copy-start(s32[96,128]{1,0:T(8,128)} %weight_ref.7) | copy-start | bytes 147460
  2.2 13.3 %collective-permute-start = (bf16[2,224,128]{2,1,0:T(8,128)(2,1)S(1)}, bf16[2,224,128]{2,1,0:T(8,128)(2,1)S(1)}, u32[]{:S(2)}, u32[]{:S(2)}) collective-permute-start(bf16[2,224,128]{2,1,0:T(8,128)(2,1)S(1)} %get-tuple-element.14.bottom_ref), channel_id=1, source_target_pairs={{0,1},{1,2},{2,3},{3,4},{4,5},{5,6},{6,7},{7,8},{8,9},{9,10},{10,1... | collective-permute-start | bytes 344072 | tf_op jit(solution)/shard_map/ppermute | solution.py:571
  6.2 9.3 %collective-permute-start.1 = (bf16[2,224,128]{2,1,0:T(8,128)(2,1)S(1)}, bf16[2,224,128]{2,1,0:T(8,128)(2,1)S(1)}, u32[]{:S(2)}, u32[]{:S(2)}) collective-permute-start(bf16[2,224,128]{2,1,0:T(8,128)(2,1)S(1)} %get-tuple-element.15.top_ref), channel_id=1, source_target_pairs={{1,0},{2,1},{3,2},{4,3},{5,4},{6,5},{7,6},{8,7},{9,8},{10,9},{11,1... | collective-permute-start | bytes 344072 | tf_op jit(solution)/shard_map/ppermute | solution.py:572
  16.0 6.1 %collective-permute-start.2 = (f32[112,128]{1,0:T(8,128)S(1)}, f32[112,128]{1,0:T(8,128)S(1)}, u32[]{:S(2)}, u32[]{:S(2)}) collective-permute-start(f32[112,128]{1,0:T(8,128)S(1)} %select_bitcast_fusion.5), channel_id=1, source_target_pairs={{0,32},{1,33},{2,34},{3,35},{4,36},{5,37},{6,38},{7,39},{8,40},{9,... | collective-permute-start | bytes 172040 | tf_op jit(solution)/shard_map/ppermute | solution.py:47
  17.0 9.5 %collective-permute-start.14 = (bf16[224,256]{1,0:T(8,128)(2,1)S(1)}, bf16[224,256]{1,0:T(8,128)(2,1)S(1)}, u32[]{:S(2)}, u32[]{:S(2)}) collective-permute-start(bf16[224,256]{1,0:T(8,128)(2,1)S(1)} %get-tuple-element.20), channel_id=1, source_target_pairs={{0,32},{32,64},{64,96},{96,128},{128,160},{160,192},{192,224},{1,3... | collective-permute-start | bytes 344072 | tf_op jit(solution)/shard_map/ppermute | solution.py:578
  20.1 6.4 %collective-permute-start.15 = (bf16[224,256]{1,0:T(8,128)(2,1)S(1)}, bf16[224,256]{1,0:T(8,128)(2,1)S(1)}, u32[]{:S(2)}, u32[]{:S(2)}) collective-permute-start(bf16[224,256]{1,0:T(8,128)(2,1)S(1)} %get-tuple-element.21), channel_id=1, source_target_pairs={{32,0},{64,32},{96,64},{128,96},{160,128},{192,160},{224,192},{33,... | collective-permute-start | bytes 344072 | tf_op jit(solution)/shard_map/ppermute | solution.py:579
  22.1 13.7 %collective-permute-start.5 = (f32[112,128]{1,0:T(8,128)S(1)}, f32[112,128]{1,0:T(8,128)S(1)}, u32[]{:S(2)}, u32[]{:S(2)}) collective-permute-start(f32[112,128]{1,0:T(8,128)S(1)} %bitcast_add_fusion.1), channel_id=1, source_target_pairs={{0,3},{1,2},{2,1},{3,0},{4,7},{5,6},{6,5},{7,4},{8,11},{9,10},{10,... | collective-permute-start | bytes 172040 | tf_op jit(solution)/shard_map/ppermute | solution.py:49
  25.8 10.0 %collective-permute-start.4 = (f32[112,128]{1,0:T(8,128)S(1)}, f32[112,128]{1,0:T(8,128)S(1)}, u32[]{:S(2)}, u32[]{:S(2)}) collective-permute-start(f32[112,128]{1,0:T(8,128)S(1)} %bitcast_add_fusion.1), channel_id=1, source_target_pairs={{0,2},{1,3},{2,0},{3,1},{4,6},{5,7},{6,4},{7,5},{8,10},{9,11},{10,... | collective-permute-start | bytes 172040 | tf_op jit(solution)/shard_map/ppermute | solution.py:49
  26.3 9.5 %collective-permute-start.3 = (f32[112,128]{1,0:T(8,128)S(1)}, f32[112,128]{1,0:T(8,128)S(1)}, u32[]{:S(2)}, u32[]{:S(2)}) collective-permute-start(f32[112,128]{1,0:T(8,128)S(1)} %bitcast_add_fusion.1), channel_id=1, source_target_pairs={{0,1},{1,0},{2,3},{3,2},{4,5},{5,4},{6,7},{7,6},{8,9},{9,8},{10,11... | collective-permute-start | bytes 172040 | tf_op jit(solution)/shard_map/ppermute | solution.py:49
  26.5 2.6 %copy-start.1 = (bf16[96,224,128]{2,1,0:T(8,128)(2,1)S(1)}, bf16[96,224,128]{2,1,0:T(8,128)(2,1)}, u32[]{:S(2)}) copy-start(bf16[96,224,128]{2,1,0:T(8,128)(2,1)} %get-tuple-element.19.xt_ref) | copy-start | bytes 16515076
  35.7 4.7 %collective-permute-start.16 = (f32[112,128]{1,0:T(8,128)S(1)}, f32[112,128]{1,0:T(8,128)S(1)}, u32[]{:S(2)}, u32[]{:S(2)}) collective-permute-start(f32[112,128]{1,0:T(8,128)S(1)} %select_bitcast_fusion.2), channel_id=1, source_target_pairs={{0,32},{1,33},{2,34},{3,35},{4,36},{5,37},{6,38},{7,39},{8,40},{9,... | collective-permute-start | bytes 172040 | tf_op jit(solution)/shard_map/ppermute | solution.py:47
  35.9 8.0 %collective-permute-start.8 = (f32[112,128]{1,0:T(8,128)S(1)}, f32[112,128]{1,0:T(8,128)S(1)}, u32[]{:S(2)}, u32[]{:S(2)}) collective-permute-start(f32[112,128]{1,0:T(8,128)S(1)} %add_add_fusion.5), channel_id=1, source_target_pairs={{0,192},{1,193},{2,194},{3,195},{4,196},{5,197},{6,198},{7,199},{8... | collective-permute-start | bytes 172040 | tf_op jit(solution)/shard_map/ppermute | solution.py:49
  39.7 4.5 %collective-permute-start.7 = (f32[112,128]{1,0:T(8,128)S(1)}, f32[112,128]{1,0:T(8,128)S(1)}, u32[]{:S(2)}, u32[]{:S(2)}) collective-permute-start(f32[112,128]{1,0:T(8,128)S(1)} %add_add_fusion.5), channel_id=1, source_target_pairs={{0,128},{1,129},{2,130},{3,131},{4,132},{5,133},{6,134},{7,135},{8... | collective-permute-start | bytes 172040 | tf_op jit(solution)/shard_map/ppermute | solution.py:49
  40.1 4.2 %collective-permute-start.6 = (f32[112,128]{1,0:T(8,128)S(1)}, f32[112,128]{1,0:T(8,128)S(1)}, u32[]{:S(2)}, u32[]{:S(2)}) collective-permute-start(f32[112,128]{1,0:T(8,128)S(1)} %add_add_fusion.5), channel_id=1, source_target_pairs={{0,64},{1,65},{2,66},{3,67},{4,68},{5,69},{6,70},{7,71},{8,72},{9,... | collective-permute-start | bytes 172040 | tf_op jit(solution)/shard_map/ppermute | solution.py:49
  40.4 10.8 %collective-permute-start.19 = (f32[112,128]{1,0:T(8,128)S(1)}, f32[112,128]{1,0:T(8,128)S(1)}, u32[]{:S(2)}, u32[]{:S(2)}) collective-permute-start(f32[112,128]{1,0:T(8,128)S(1)} %bitcast_add_fusion), channel_id=1, source_target_pairs={{0,3},{1,2},{2,1},{3,0},{4,7},{5,6},{6,5},{7,4},{8,11},{9,10},{10,... | collective-permute-start | bytes 172040 | tf_op jit(solution)/shard_map/ppermute | solution.py:49
  43.4 8.2 %collective-permute-start.18 = (f32[112,128]{1,0:T(8,128)S(1)}, f32[112,128]{1,0:T(8,128)S(1)}, u32[]{:S(2)}, u32[]{:S(2)}) collective-permute-start(f32[112,128]{1,0:T(8,128)S(1)} %bitcast_add_fusion), channel_id=1, source_target_pairs={{0,2},{1,3},{2,0},{3,1},{4,6},{5,7},{6,4},{7,5},{8,10},{9,11},{10,... | collective-permute-start | bytes 172040 | tf_op jit(solution)/shard_map/ppermute | solution.py:49
  43.9 7.7 %collective-permute-start.17 = (f32[112,128]{1,0:T(8,128)S(1)}, f32[112,128]{1,0:T(8,128)S(1)}, u32[]{:S(2)}, u32[]{:S(2)}) collective-permute-start(f32[112,128]{1,0:T(8,128)S(1)} %bitcast_add_fusion), channel_id=1, source_target_pairs={{0,1},{1,0},{2,3},{3,2},{4,5},{5,4},{6,7},{7,6},{8,9},{9,8},{10,11... | collective-permute-start | bytes 172040 | tf_op jit(solution)/shard_map/ppermute | solution.py:49
  44.3 10.0 %collective-permute-start.11 = (f32[112,128]{1,0:T(8,128)S(1)}, f32[112,128]{1,0:T(8,128)S(1)}, u32[]{:S(2)}, u32[]{:S(2)}) collective-permute-start(f32[112,128]{1,0:T(8,128)S(1)} %add_add_fusion.4), channel_id=1, source_target_pairs={{0,12},{1,13},{2,14},{3,15},{4,8},{5,9},{6,10},{7,11},{8,4},{9,5},... | collective-permute-start | bytes 172040 | tf_op jit(solution)/shard_map/ppermute | solution.py:49
  51.2 4.3 %collective-permute-start.10 = (f32[112,128]{1,0:T(8,128)S(1)}, f32[112,128]{1,0:T(8,128)S(1)}, u32[]{:S(2)}, u32[]{:S(2)}) collective-permute-start(f32[112,128]{1,0:T(8,128)S(1)} %add_add_fusion.4), channel_id=1, source_target_pairs={{0,8},{1,9},{2,10},{3,11},{4,12},{5,13},{6,14},{7,15},{8,0},{9,1},... | collective-permute-start | bytes 172040 | tf_op jit(solution)/shard_map/ppermute | solution.py:49
  51.2 4.3 %collective-permute-start.9 = (f32[112,128]{1,0:T(8,128)S(1)}, f32[112,128]{1,0:T(8,128)S(1)}, u32[]{:S(2)}, u32[]{:S(2)}) collective-permute-start(f32[112,128]{1,0:T(8,128)S(1)} %add_add_fusion.4), channel_id=1, source_target_pairs={{0,4},{1,5},{2,6},{3,7},{4,0},{5,1},{6,2},{7,3},{8,12},{9,13},{10,... | collective-permute-start | bytes 172040 | tf_op jit(solution)/shard_map/ppermute | solution.py:49
  51.6 8.5 %collective-permute-start.22 = (f32[112,128]{1,0:T(8,128)S(1)}, f32[112,128]{1,0:T(8,128)S(1)}, u32[]{:S(2)}, u32[]{:S(2)}) collective-permute-start(f32[112,128]{1,0:T(8,128)S(1)} %add_add_fusion.2), channel_id=1, source_target_pairs={{0,192},{1,193},{2,194},{3,195},{4,196},{5,197},{6,198},{7,199},{8... | collective-permute-start | bytes 172040 | tf_op jit(solution)/shard_map/ppermute | solution.py:49
  53.8 6.4 %collective-permute-start.21 = (f32[112,128]{1,0:T(8,128)S(1)}, f32[112,128]{1,0:T(8,128)S(1)}, u32[]{:S(2)}, u32[]{:S(2)}) collective-permute-start(f32[112,128]{1,0:T(8,128)S(1)} %add_add_fusion.2), channel_id=1, source_target_pairs={{0,128},{1,129},{2,130},{3,131},{4,132},{5,133},{6,134},{7,135},{8... | collective-permute-start | bytes 172040 | tf_op jit(solution)/shard_map/ppermute | solution.py:49
  54.3 5.9 %collective-permute-start.20 = (f32[112,128]{1,0:T(8,128)S(1)}, f32[112,128]{1,0:T(8,128)S(1)}, u32[]{:S(2)}, u32[]{:S(2)}) collective-permute-start(f32[112,128]{1,0:T(8,128)S(1)} %add_add_fusion.2), channel_id=1, source_target_pairs={{0,64},{1,65},{2,66},{3,67},{4,68},{5,69},{6,70},{7,71},{8,72},{9,... | collective-permute-start | bytes 172040 | tf_op jit(solution)/shard_map/ppermute | solution.py:49
  55.5 8.3 %collective-permute-start.12 = (f32[112,128]{1,0:T(8,128)S(1)}, f32[112,128]{1,0:T(8,128)S(1)}, u32[]{:S(2)}, u32[]{:S(2)}) collective-permute-start(f32[112,128]{1,0:T(8,128)S(1)} %add_add_fusion.3), channel_id=1, source_target_pairs={{0,28},{1,29},{2,30},{3,31},{4,24},{5,25},{6,26},{7,27},{8,20},{9,... | collective-permute-start | bytes 172040 | tf_op jit(solution)/shard_map/ppermute | solution.py:49
  60.2 7.8 %collective-permute-start.25 = (f32[112,128]{1,0:T(8,128)S(1)}, f32[112,128]{1,0:T(8,128)S(1)}, u32[]{:S(2)}, u32[]{:S(2)}) collective-permute-start(f32[112,128]{1,0:T(8,128)S(1)} %add_add_fusion.1), channel_id=1, source_target_pairs={{0,12},{1,13},{2,14},{3,15},{4,8},{5,9},{6,10},{7,11},{8,4},{9,5},... | collective-permute-start | bytes 172040 | tf_op jit(solution)/shard_map/ppermute | solution.py:49
  62.4 5.5 %collective-permute-start.24 = (f32[112,128]{1,0:T(8,128)S(1)}, f32[112,128]{1,0:T(8,128)S(1)}, u32[]{:S(2)}, u32[]{:S(2)}) collective-permute-start(f32[112,128]{1,0:T(8,128)S(1)} %add_add_fusion.1), channel_id=1, source_target_pairs={{0,8},{1,9},{2,10},{3,11},{4,12},{5,13},{6,14},{7,15},{8,0},{9,1},... | collective-permute-start | bytes 172040 | tf_op jit(solution)/shard_map/ppermute | solution.py:49
  62.4 5.5 %collective-permute-start.23 = (f32[112,128]{1,0:T(8,128)S(1)}, f32[112,128]{1,0:T(8,128)S(1)}, u32[]{:S(2)}, u32[]{:S(2)}) collective-permute-start(f32[112,128]{1,0:T(8,128)S(1)} %add_add_fusion.1), channel_id=1, source_target_pairs={{0,4},{1,5},{2,6},{3,7},{4,0},{5,1},{6,2},{7,3},{8,12},{9,13},{10,... | collective-permute-start | bytes 172040 | tf_op jit(solution)/shard_map/ppermute | solution.py:49
  63.9 7.6 %collective-permute-start.13 = (f32[112,128]{1,0:T(8,128)S(1)}, f32[112,128]{1,0:T(8,128)S(1)}, u32[]{:S(2)}, u32[]{:S(2)}) collective-permute-start(f32[112,128]{1,0:T(8,128)S(1)} %add.82), channel_id=1, source_target_pairs={{0,32},{1,33},{2,34},{3,35},{4,36},{5,37},{6,38},{7,39},{8,40},{9,... | collective-permute-start | bytes 172040 | tf_op jit(solution)/shard_map/ppermute | solution.py:54
  68.0 5.2 %collective-permute-start.26 = (f32[112,128]{1,0:T(8,128)S(1)}, f32[112,128]{1,0:T(8,128)S(1)}, u32[]{:S(2)}, u32[]{:S(2)}) collective-permute-start(f32[112,128]{1,0:T(8,128)S(1)} %add_add_fusion), channel_id=1, source_target_pairs={{0,28},{1,29},{2,30},{3,31},{4,24},{5,25},{6,26},{7,27},{8,20},{9,... | collective-permute-start | bytes 172040 | tf_op jit(solution)/shard_map/ppermute | solution.py:49
  73.2 6.3 %collective-permute-start.27 = (f32[112,128]{1,0:T(8,128)S(1)}, f32[112,128]{1,0:T(8,128)S(1)}, u32[]{:S(2)}, u32[]{:S(2)}) collective-permute-start(f32[112,128]{1,0:T(8,128)S(1)} %add.93), channel_id=1, source_target_pairs={{0,32},{1,33},{2,34},{3,35},{4,36},{5,37},{6,38},{7,39},{8,40},{9,... | collective-permute-start | bytes 172040 | tf_op jit(solution)/shard_map/ppermute | solution.py:54

commit v4 on v3

--- a/solution.py
+++ b/solution.py
@@ -40,7 +40,7 @@
 AXES = ("group", "tile")
 
 
-def total_of(value):
+def total_of(value, beside=None):
     first = lax.axis_index("group") % 2 == 0
     own = jnp.where(first, value[0], value[1])
     other = jnp.where(first, value[1], value[0])
@@ -48,11 +48,14 @@
     for stage in STAGES:
         parts = [lax.ppermute(own, AXES, pairs) for pairs in stage]
         if len(parts) == 1:
-            own = own + parts[0]
+            part = parts[0]
+            if beside is not None:
+                part, beside = lax.optimization_barrier((part, beside))
+            own = own + part
         else:
             own = (own + parts[0]) + (parts[1] + parts[2])
     other = lax.ppermute(own, AXES, CORE_SWAP)
-    return jnp.stack([jnp.where(first, own, other), jnp.where(first, other, own)])
+    return (jnp.stack([jnp.where(first, own, other), jnp.where(first, other, own)]), beside)
 
 
 def split_three(value):
@@ -489,17 +492,42 @@
             work_ref[low:size, :] = rest - update[low - cut : size - cut, :]
 
 
+def factor_kernel(noise_ref, out_ref, work_ref):
+    size = out_ref.shape[0]
+    work_ref[...] = covariance_of(folded_of(noise_ref))
+    factor_into(work_ref, size)
+    out_ref[...] = work_ref[:, :size]
+
+
+def inverse_factor(noise):
+    size = 2 * noise.shape[1]
+    return pl.pallas_call(
+        factor_kernel,
+        out_shape=jax.ShapeDtypeStruct((size, size), F32),
+        in_specs=[VMEM_SPEC],
+        out_specs=VMEM_SPEC,
+        scratch_shapes=[pltpu.VMEM((size, 256), F32)],
+        compiler_params=params(6),
+        cost_estimate=cost(400 * size**3, 8 * size**2),
+        name="inverse_factor",
+    )(noise)
+
+
 def finish_kernel(
-    noise_ref, signal_ref, weight_ref, field_ref, result_ref, cov_ref,
-    work_ref, smooth_ref, out_ref, in_sems, out_sems,
+    inverse_ref, signal_ref, weight_ref, field_ref, result_ref, cov_ref,
+    smooth_ref, out_ref, in_sems, out_sems,
 ):
     rows, bands, cols = smooth_ref.shape
     groups, slabs = rows // GROUP, rows // 16
     for g in range(groups):
         group_copy(field_ref, smooth_ref, in_sems, g).start()
-    work_ref[...] = covariance_of(folded_of(noise_ref))
-    factor_into(work_ref, bands)
-    inverse = work_ref[:, :bands]
+    inverse = inverse_ref[...]
+    cov = covariance_of(folded_of(signal_ref))[:, :bands]
+    left = jnp.dot(inverse, cov, precision=lax.Precision.HIGHEST, preferred_element_type=F32)
+    cov_ref[...] = lax.dot_general(
+        left, inverse, (((1,), (1,)), ((), ())),
+        precision=lax.Precision.HIGHEST, preferred_element_type=F32,
+    )
     inverse_cast = inverse.astype(BF16)
     first, count = sums_of(folded_of(signal_ref))
     mean = jnp.broadcast_to(first / count, (bands, cols))
@@ -526,17 +554,11 @@
         out_ref[s] = jnp.swapaxes(jnp.concatenate(parts, axis=0), 0, 1)
         outward(s).start()
 
-    cov = covariance_of(folded_of(signal_ref))[:, :bands]
-    left = jnp.dot(inverse, cov, precision=lax.Precision.HIGHEST, preferred_element_type=F32)
-    cov_ref[...] = lax.dot_general(
-        left, inverse, (((1,), (1,)), ((), ())),
-        precision=lax.Precision.HIGHEST, preferred_element_type=F32,
-    )
     for s in range(slabs):
         outward(s).wait()
 
 
-def finish(noise, signal, weight, smooth):
+def finish(inverse, signal, weight, smooth):
     rows, bands, cols = smooth.shape
     groups, slabs = rows // GROUP, rows // 16
     return pl.pallas_call(
@@ -548,7 +570,6 @@
         in_specs=[VMEM_SPEC, VMEM_SPEC, VMEM_SPEC, HBM_SPEC],
         out_specs=(HBM_SPEC, VMEM_SPEC),
         scratch_shapes=[
-            pltpu.VMEM((bands, 256), F32),
             pltpu.VMEM((rows, bands, cols), F32),
             pltpu.VMEM((slabs, bands, 16, cols), BF16),
             pltpu.SemaphoreType.DMA((groups,)),
@@ -557,7 +578,7 @@
         compiler_params=params(36),
         cost_estimate=cost(2 * bands * bands * rows * cols, 6 * bands * rows * cols),
         name="finish",
-    )(noise, signal, weight, in_hbm(smooth))
+    )(inverse, signal, weight, in_hbm(smooth))
 
 
 def line(count):
@@ -578,7 +599,9 @@
     low = lax.ppermute(to_high, "group", forward)
     high = lax.ppermute(to_low, "group", backward)
     smooth, signal = signal_moments(xt, up, down, low, high, valid_mask)
-    whitened, whitened_cov = finish(total_of(noise), total_of(signal), valid_mask, smooth)
+    noise_total, _ = total_of(noise)
+    signal_total, inverse = total_of(signal, inverse_factor(noise_total))
+    whitened, whitened_cov = finish(inverse, signal_total, valid_mask, smooth)
     return (whitened, whitened_cov)
 
 

time: 94.3 us -> 91.9 us (0.975)
  starting transfers between devices: 55.9 us -> 54.2 us
  waiting for transfers between devices: 3.45 us -> 2.11 us
    pallas_call x0 -> x1, Pallas kernels: none -> 6.71 us  [inverse_factor(): pl.pallas_call(factor_kernel, out_shape=jax.ShapeDtypeStruct((size, size)...]
    pallas_call x1, Pallas kernels: 14.3 us -> 8.16 us  [finish(): pl.pallas_call(finish_kernel, out_shape=(pltpu.HBM((bands, rows, cols), B...]
    ppermute x20, starting transfers between devices: 34.9 us -> 33.1 us  [total_of(): parts = [lax.ppermute(own, AXES, pairs) for pairs in stage]]
    ppermute x20, waiting for transfers between devices: 2.52 us -> 1.2 us  [total_of(): parts = [lax.ppermute(own, AXES, pairs) for pairs in stage]]
  transfers between devices with their start and end apart: 28 -> 28, of which waited for: 4 -> 3; matrix products, arithmetic and copies ran while one was open for 0% -> 0% of each run, Pallas kernels for 16% -> 23%
where the time goes in v4:
time: 91.9 us; the launch traced here: 91.6 us
  starting transfers between devices  54.2 us (59%)
  Pallas kernels  31.5 us (34%)
  local copies, waits for them, and re-layouts  2.56 us (3%)
  waiting for transfers between devices  2.11 us (2%)
  between operations  1.12 us (1%)
    ppermute x20, starting transfers between devices, total_of(): parts = [lax.ppermute(own, AXES, pairs) for pairs in stage]  33.1 us
    ppermute x2, starting transfers between devices, total_of(): other = lax.ppermute(own, AXES, CORE_SWAP)  9.7 us
    pallas_call x1, Pallas kernels, finish(): pl.pallas_call(finish_kernel, out_shape=(pltpu.HBM((bands, rows, cols), B...  8.16 us
    pallas_call x1, Pallas kernels, rows_first(): pl.pallas_call(rows_first_kernel, out_shape=(pltpu.HBM((rows, bands, cols...  7.99 us
    pallas_call x1, Pallas kernels, inverse_factor(): pl.pallas_call(factor_kernel, out_shape=jax.ShapeDtypeStruct((size, size)...  6.71 us
    pallas_call x1, Pallas kernels, signal_moments(): pl.pallas_call(signal_kernel, out_shape=(pltpu.HBM((rows, bands, cols), F...  6.62 us
    ppermute x1, starting transfers between devices, body(): up = lax.ppermute(last, 'tile', forward)  3.95 us
    ppermute x1, starting transfers between devices, body(): low = lax.ppermute(to_high, 'group', forward)  3.1 us
  transfers between devices with their start and end apart: 28, of which 3 were waited for; matrix products, arithmetic and copies ran while one was open for 0% of the time, Pallas kernels for 23%

profile of v4, /device:TPU:1, one launch (start us, length us, event | category | flops | bytes accessed | tf_op | source)
XLA Modules:
  0.0 91.6 jit_solution(4290808659470950364)
XLA Ops:
  0.6 1.6 %edge_rows.1 = (bf16[2,224,128]{2,1,0:T(8,128)(2,1)S(1)}, bf16[2,224,128]{2,1,0:T(8,128)(2,1)S(1)}) custom-call(bf16[224,96,128]{2,1,0:T(8,128)(2,1)} %x_ref.3), custom_call_target="tpu_custom_call" | custom-call | bytes 1835008 | tf_op jit(solution)/shard_map/edge_rows/pallas_call | solution.py:100
  2.2 4.0 %collective-permute-start = (bf16[2,224,128]{2,1,0:T(8,128)(2,1)S(1)}, bf16[2,224,128]{2,1,0:T(8,128)(2,1)S(1)}, u32[]{:S(2)}, u32[]{:S(2)}) collective-permute-start(bf16[2,224,128]{2,1,0:T(8,128)(2,1)S(1)} %get-tuple-element.16.bottom_ref), channel_id=1, source_target_pairs={{0,1},{1,2},{2,3},{3,4},{4,5},{5,6},{6,7},{7,8},{8,9},{9,10},{10,1... | collective-permute-start | bytes 344072 | tf_op jit(solution)/shard_map/ppermute | solution.py:592
  6.2 1.3 %collective-permute-start.1 = (bf16[2,224,128]{2,1,0:T(8,128)(2,1)S(1)}, bf16[2,224,128]{2,1,0:T(8,128)(2,1)S(1)}, u32[]{:S(2)}, u32[]{:S(2)}) collective-permute-start(bf16[2,224,128]{2,1,0:T(8,128)(2,1)S(1)} %get-tuple-element.17.top_ref), channel_id=1, source_target_pairs={{1,0},{2,1},{3,2},{4,3},{5,4},{6,5},{7,6},{8,7},{9,8},{10,9},{11,1... | collective-permute-start | bytes 344072 | tf_op jit(solution)/shard_map/ppermute | solution.py:593
  7.5 8.0 %rows_first.1 = (bf16[96,224,128]{2,1,0:T(8,128)(2,1)}, bf16[2,224,256]{2,1,0:T(8,128)(2,1)S(1)}, f32[224,224]{1,0:T(8,128)S(1)}, f32[224,128]{1,0:T(8,128)S(1)}) custom-call(bf16[224,96,128]{2,1,0:T(8,128)(2,1)} %x_ref.3, s32[96,128]{1,0:T(8,128)S(1)} %copy-done), custom_call_target="tpu_custom_call" | custom-call | flops 1233125376 | bytes 11010048 | tf_op jit(solution)/shard_map/rows_first/pallas_call | solution.py:201
  15.5 0.4 side_columns.1
  16.0 1.0 %collective-permute-start.15 = (f32[112,128]{1,0:T(8,128)S(1)}, f32[112,128]{1,0:T(8,128)S(1)}, u32[]{:S(2)}, u32[]{:S(2)}) collective-permute-start(f32[112,128]{1,0:T(8,128)S(1)} %select_bitcast_fusion.4), channel_id=1, source_target_pairs={{0,32},{1,33},{2,34},{3,35},{4,36},{5,37},{6,38},{7,39},{8,40},{9,... | collective-permute-start | bytes 172040 | tf_op jit(solution)/shard_map/ppermute | solution.py:47
  17.0 3.1 %collective-permute-start.2 = (bf16[224,256]{1,0:T(8,128)(2,1)S(1)}, bf16[224,256]{1,0:T(8,128)(2,1)S(1)}, u32[]{:S(2)}, u32[]{:S(2)}) collective-permute-start(bf16[224,256]{1,0:T(8,128)(2,1)S(1)} %get-tuple-element.21), channel_id=1, source_target_pairs={{0,32},{32,64},{64,96},{96,128},{128,160},{160,192},{192,224},{1,3... | collective-permute-start | bytes 344072 | tf_op jit(solution)/shard_map/ppermute | solution.py:599
  20.1 1.9 %collective-permute-start.3 = (bf16[224,256]{1,0:T(8,128)(2,1)S(1)}, bf16[224,256]{1,0:T(8,128)(2,1)S(1)}, u32[]{:S(2)}, u32[]{:S(2)}) collective-permute-start(bf16[224,256]{1,0:T(8,128)(2,1)S(1)} %get-tuple-element.22), channel_id=1, source_target_pairs={{32,0},{64,32},{96,64},{128,96},{160,128},{192,160},{224,192},{33,... | collective-permute-start | bytes 344072 | tf_op jit(solution)/shard_map/ppermute | solution.py:600
  22.1 4.0 %collective-permute-start.17 = (f32[112,128]{1,0:T(8,128)S(1)}, f32[112,128]{1,0:T(8,128)S(1)}, u32[]{:S(2)}, u32[]{:S(2)}) collective-permute-start(f32[112,128]{1,0:T(8,128)S(1)} %bitcast_add_fusion), channel_id=1, source_target_pairs={{0,2},{1,3},{2,0},{3,1},{4,6},{5,7},{6,4},{7,5},{8,10},{9,11},{10,... | collective-permute-start | bytes 172040 | tf_op jit(solution)/shard_map/ppermute | solution.py:49
  26.1 0.9 collective-permute-start.18
  27.0 2.6 %copy-done.1 = bf16[96,224,128]{2,1,0:T(8,128)(2,1)S(1)} copy-done((bf16[96,224,128]{2,1,0:T(8,128)(2,1)S(1)}, bf16[96,224,128]{2,1,0:T(8,128)(2,1)}, u32[]{:S(2)}) %copy-start.1) | copy-done | bytes 5505048
  29.5 6.6 %signal_moments.1 = (f32[96,224,128]{2,1,0:T(8,128)}, f32[2,112,128]{2,1,0:T(8,128)S(1)}) custom-call(bf16[96,224,128]{2,1,0:T(8,128)(2,1)S(1)} %copy-done.1, bf16[2,224,128]{2,1,0:T(8,128)(2,1)S(1)} %collective-permute-done.up_ref, bf16[2,224,128]{2,1,0:T(8,128)(2,1)S(1)} %collective-permute-done.1.down_ref, ...), custom_call_target="tpu_custom_call" | custom-call | flops 2466250752 | bytes 16515072 | tf_op jit(solution)/shard_map/signal_moments/pallas_call | solution.py:412
  36.3 4.1 %collective-permute-start.20 = (f32[112,128]{1,0:T(8,128)S(1)}, f32[112,128]{1,0:T(8,128)S(1)}, u32[]{:S(2)}, u32[]{:S(2)}) collective-permute-start(f32[112,128]{1,0:T(8,128)S(1)} %add_add_fusion.2), channel_id=1, source_target_pairs={{0,128},{1,129},{2,130},{3,131},{4,132},{5,133},{6,134},{7,135},{8... | collective-permute-start | bytes 172040 | tf_op jit(solution)/shard_map/ppermute | solution.py:49
  40.4 0.8 collective-permute-start.21
  41.2 3.4 %collective-permute-start.6 = (f32[112,128]{1,0:T(8,128)S(1)}, f32[112,128]{1,0:T(8,128)S(1)}, u32[]{:S(2)}, u32[]{:S(2)}) collective-permute-start(f32[112,128]{1,0:T(8,128)S(1)} %bitcast_add_fusion.1), channel_id=1, source_target_pairs={{0,2},{1,3},{2,0},{3,1},{4,6},{5,7},{6,4},{7,5},{8,10},{9,11},{10,... | collective-permute-start | bytes 172040 | tf_op jit(solution)/shard_map/ppermute | solution.py:49
  44.5 0.9 collective-permute-start.7
  45.4 3.7 %collective-permute-start.23 = (f32[112,128]{1,0:T(8,128)S(1)}, f32[112,128]{1,0:T(8,128)S(1)}, u32[]{:S(2)}, u32[]{:S(2)}) collective-permute-start(f32[112,128]{1,0:T(8,128)S(1)} %add_add_fusion.1), channel_id=1, source_target_pairs={{0,8},{1,9},{2,10},{3,11},{4,12},{5,13},{6,14},{7,15},{8,0},{9,1},... | collective-permute-start | bytes 172040 | tf_op jit(solution)/shard_map/ppermute | solution.py:49
  49.1 1.4 %collective-permute-start.24 = (f32[112,128]{1,0:T(8,128)S(1)}, f32[112,128]{1,0:T(8,128)S(1)}, u32[]{:S(2)}, u32[]{:S(2)}) collective-permute-start(f32[112,128]{1,0:T(8,128)S(1)} %add_add_fusion.1), channel_id=1, source_target_pairs={{0,12},{1,13},{2,14},{3,15},{4,8},{5,9},{6,10},{7,11},{8,4},{9,5},... | collective-permute-start | bytes 172040 | tf_op jit(solution)/shard_map/ppermute | solution.py:49
  50.6 0.2 collective-permute-start.22
  50.8 2.5 %collective-permute-start.9 = (f32[112,128]{1,0:T(8,128)S(1)}, f32[112,128]{1,0:T(8,128)S(1)}, u32[]{:S(2)}, u32[]{:S(2)}) collective-permute-start(f32[112,128]{1,0:T(8,128)S(1)} %add_add_fusion.5), channel_id=1, source_target_pairs={{0,128},{1,129},{2,130},{3,131},{4,132},{5,133},{6,134},{7,135},{8... | collective-permute-start | bytes 172040 | tf_op jit(solution)/shard_map/ppermute | solution.py:49
  53.3 0.8 collective-permute-start.10
  54.1 0.5 collective-permute-done.24
  54.6 4.4 %collective-permute-start.25 = (f32[112,128]{1,0:T(8,128)S(1)}, f32[112,128]{1,0:T(8,128)S(1)}, u32[]{:S(2)}, u32[]{:S(2)}) collective-permute-start(f32[112,128]{1,0:T(8,128)S(1)} %add_add_fusion), channel_id=1, source_target_pairs={{0,28},{1,29},{2,30},{3,31},{4,24},{5,25},{6,26},{7,27},{8,20},{9,... | collective-permute-start | bytes 172040 | tf_op jit(solution)/shard_map/ppermute | solution.py:49
  59.1 2.2 %collective-permute-start.12 = (f32[112,128]{1,0:T(8,128)S(1)}, f32[112,128]{1,0:T(8,128)S(1)}, u32[]{:S(2)}, u32[]{:S(2)}) collective-permute-start(f32[112,128]{1,0:T(8,128)S(1)} %add_add_fusion.4), channel_id=1, source_target_pairs={{0,8},{1,9},{2,10},{3,11},{4,12},{5,13},{6,14},{7,15},{8,0},{9,1},... | collective-permute-start | bytes 172040 | tf_op jit(solution)/shard_map/ppermute | solution.py:49
  61.3 1.6 %collective-permute-start.13 = (f32[112,128]{1,0:T(8,128)S(1)}, f32[112,128]{1,0:T(8,128)S(1)}, u32[]{:S(2)}, u32[]{:S(2)}) collective-permute-start(f32[112,128]{1,0:T(8,128)S(1)} %add_add_fusion.4), channel_id=1, source_target_pairs={{0,12},{1,13},{2,14},{3,15},{4,8},{5,9},{6,10},{7,11},{8,4},{9,5},... | collective-permute-start | bytes 172040 | tf_op jit(solution)/shard_map/ppermute | solution.py:49
  62.9 4.2 %collective-permute-start.26 = (f32[112,128]{1,0:T(8,128)S(1)}, f32[112,128]{1,0:T(8,128)S(1)}, u32[]{:S(2)}, u32[]{:S(2)}) collective-permute-start(f32[112,128]{1,0:T(8,128)S(1)} %add.92), channel_id=1, source_target_pairs={{0,32},{1,33},{2,34},{3,35},{4,36},{5,37},{6,38},{7,39},{8,40},{9,... | collective-permute-start | bytes 172040 | tf_op jit(solution)/shard_map/ppermute | solution.py:57
  67.1 0.7 collective-permute-done.11
  67.8 2.3 %collective-permute-start.14 = (f32[112,128]{1,0:T(8,128)S(1)}, f32[112,128]{1,0:T(8,128)S(1)}, u32[]{:S(2)}, u32[]{:S(2)}) collective-permute-start(f32[112,128]{1,0:T(8,128)S(1)} %add_add_fusion.3), channel_id=1, source_target_pairs={{0,28},{1,29},{2,30},{3,31},{4,24},{5,25},{6,26},{7,27},{8,20},{9,... | collective-permute-start | bytes 172040 | tf_op jit(solution)/shard_map/ppermute | solution.py:49
  70.1 6.7 %inverse_factor.1.inverse_ref = f32[224,224]{1,0:T(8,128)S(1)} custom-call(f32[2,112,128]{2,1,0:T(8,128)S(1)} %pad_maximum_fusion.noise_ref), custom_call_target="tpu_custom_call" | custom-call | flops 4495769600 | bytes 401408 | tf_op jit(solution)/shard_map/inverse_factor/pallas_call | solution.py:504
  76.8 5.5 %collective-permute-start.27 = (f32[112,128]{1,0:T(8,128)S(1)}, f32[112,128]{1,0:T(8,128)S(1)}, u32[]{:S(2)}, u32[]{:S(2)}) collective-permute-start(f32[112,128]{1,0:T(8,128)S(1)} %add.93), channel_id=1, source_target_pairs={{0,32},{1,33},{2,34},{3,35},{4,36},{5,37},{6,38},{7,39},{8,40},{9,... | collective-permute-start | bytes 172040 | tf_op jit(solution)/shard_map/ppermute | solution.py:57
  82.4 0.9 collective-permute-done.27
  83.3 8.2 %finish.1 = (bf16[224,96,128]{2,1,0:T(8,128)(2,1)}, f32[224,224]{1,0:T(8,128)}) custom-call(f32[224,224]{1,0:T(8,128)S(1)} %inverse_factor.1.inverse_ref, f32[2,112,128]{2,1,0:T(8,128)S(1)} %pad_maximum_fusion.1.signal_ref, s32[96,128]{1,0:T(8,128)S(1)} %copy-done, f32[96,224,128]{2,1,0:T(8,128)} %get-tuple-element.27.field_ref), custom_call_target="tpu_custom_call" | custom-call | flops 1233125376 | bytes 16515072 | tf_op jit(solution)/shard_map/finish/pallas_call | solution.py:564
  (50 shorter events, 0.4 us)
Async XLA Ops:
  0.6 6.9 %copy-start = (s32[96,128]{1,0:T(8,128)S(1)}, s32[96,128]{1,0:T(8,128)}, u32[]{:S(2)}) copy-start(s32[96,128]{1,0:T(8,128)} %weight_ref.7) | copy-start | bytes 147460
  2.2 13.3 %collective-permute-start = (bf16[2,224,128]{2,1,0:T(8,128)(2,1)S(1)}, bf16[2,224,128]{2,1,0:T(8,128)(2,1)S(1)}, u32[]{:S(2)}, u32[]{:S(2)}) collective-permute-start(bf16[2,224,128]{2,1,0:T(8,128)(2,1)S(1)} %get-tuple-element.16.bottom_ref), channel_id=1, source_target_pairs={{0,1},{1,2},{2,3},{3,4},{4,5},{5,6},{6,7},{7,8},{8,9},{9,10},{10,1... | collective-permute-start | bytes 344072 | tf_op jit(solution)/shard_map/ppermute | solution.py:592
  6.2 9.3 %collective-permute-start.1 = (bf16[2,224,128]{2,1,0:T(8,128)(2,1)S(1)}, bf16[2,224,128]{2,1,0:T(8,128)(2,1)S(1)}, u32[]{:S(2)}, u32[]{:S(2)}) collective-permute-start(bf16[2,224,128]{2,1,0:T(8,128)(2,1)S(1)} %get-tuple-element.17.top_ref), channel_id=1, source_target_pairs={{1,0},{2,1},{3,2},{4,3},{5,4},{6,5},{7,6},{8,7},{9,8},{10,9},{11,1... | collective-permute-start | bytes 344072 | tf_op jit(solution)/shard_map/ppermute | solution.py:593
  16.0 6.1 %collective-permute-start.15 = (f32[112,128]{1,0:T(8,128)S(1)}, f32[112,128]{1,0:T(8,128)S(1)}, u32[]{:S(2)}, u32[]{:S(2)}) collective-permute-start(f32[112,128]{1,0:T(8,128)S(1)} %select_bitcast_fusion.4), channel_id=1, source_target_pairs={{0,32},{1,33},{2,34},{3,35},{4,36},{5,37},{6,38},{7,39},{8,40},{9,... | collective-permute-start | bytes 172040 | tf_op jit(solution)/shard_map/ppermute | solution.py:47
  17.0 9.9 %collective-permute-start.2 = (bf16[224,256]{1,0:T(8,128)(2,1)S(1)}, bf16[224,256]{1,0:T(8,128)(2,1)S(1)}, u32[]{:S(2)}, u32[]{:S(2)}) collective-permute-start(bf16[224,256]{1,0:T(8,128)(2,1)S(1)} %get-tuple-element.21), channel_id=1, source_target_pairs={{0,32},{32,64},{64,96},{96,128},{128,160},{160,192},{192,224},{1,3... | collective-permute-start | bytes 344072 | tf_op jit(solution)/shard_map/ppermute | solution.py:599
  20.1 6.8 %collective-permute-start.3 = (bf16[224,256]{1,0:T(8,128)(2,1)S(1)}, bf16[224,256]{1,0:T(8,128)(2,1)S(1)}, u32[]{:S(2)}, u32[]{:S(2)}) collective-permute-start(bf16[224,256]{1,0:T(8,128)(2,1)S(1)} %get-tuple-element.22), channel_id=1, source_target_pairs={{32,0},{64,32},{96,64},{128,96},{160,128},{192,160},{224,192},{33,... | collective-permute-start | bytes 344072 | tf_op jit(solution)/shard_map/ppermute | solution.py:600
  22.1 14.2 %collective-permute-start.17 = (f32[112,128]{1,0:T(8,128)S(1)}, f32[112,128]{1,0:T(8,128)S(1)}, u32[]{:S(2)}, u32[]{:S(2)}) collective-permute-start(f32[112,128]{1,0:T(8,128)S(1)} %bitcast_add_fusion), channel_id=1, source_target_pairs={{0,2},{1,3},{2,0},{3,1},{4,6},{5,7},{6,4},{7,5},{8,10},{9,11},{10,... | collective-permute-start | bytes 172040 | tf_op jit(solution)/shard_map/ppermute | solution.py:49
  26.1 10.2 %collective-permute-start.18 = (f32[112,128]{1,0:T(8,128)S(1)}, f32[112,128]{1,0:T(8,128)S(1)}, u32[]{:S(2)}, u32[]{:S(2)}) collective-permute-start(f32[112,128]{1,0:T(8,128)S(1)} %bitcast_add_fusion), channel_id=1, source_target_pairs={{0,3},{1,2},{2,1},{3,0},{4,7},{5,6},{6,5},{7,4},{8,11},{9,10},{10,... | collective-permute-start | bytes 172040 | tf_op jit(solution)/shard_map/ppermute | solution.py:49
  26.9 9.3 %collective-permute-start.16 = (f32[112,128]{1,0:T(8,128)S(1)}, f32[112,128]{1,0:T(8,128)S(1)}, u32[]{:S(2)}, u32[]{:S(2)}) collective-permute-start(f32[112,128]{1,0:T(8,128)S(1)} %bitcast_add_fusion), channel_id=1, source_target_pairs={{0,1},{1,0},{2,3},{3,2},{4,5},{5,4},{6,7},{7,6},{8,9},{9,8},{10,11... | collective-permute-start | bytes 172040 | tf_op jit(solution)/shard_map/ppermute | solution.py:49
  26.9 2.6 %copy-start.1 = (bf16[96,224,128]{2,1,0:T(8,128)(2,1)S(1)}, bf16[96,224,128]{2,1,0:T(8,128)(2,1)}, u32[]{:S(2)}) copy-start(bf16[96,224,128]{2,1,0:T(8,128)(2,1)} %get-tuple-element.15.xt_ref) | copy-start | bytes 16515076
  36.1 5.0 %collective-permute-start.4 = (f32[112,128]{1,0:T(8,128)S(1)}, f32[112,128]{1,0:T(8,128)S(1)}, u32[]{:S(2)}, u32[]{:S(2)}) collective-permute-start(f32[112,128]{1,0:T(8,128)S(1)} %select_bitcast_fusion.5), channel_id=1, source_target_pairs={{0,32},{1,33},{2,34},{3,35},{4,36},{5,37},{6,38},{7,39},{8,40},{9,... | collective-permute-start | bytes 172040 | tf_op jit(solution)/shard_map/ppermute | solution.py:47
  36.3 9.1 %collective-permute-start.20 = (f32[112,128]{1,0:T(8,128)S(1)}, f32[112,128]{1,0:T(8,128)S(1)}, u32[]{:S(2)}, u32[]{:S(2)}) collective-permute-start(f32[112,128]{1,0:T(8,128)S(1)} %add_add_fusion.2), channel_id=1, source_target_pairs={{0,128},{1,129},{2,130},{3,131},{4,132},{5,133},{6,134},{7,135},{8... | collective-permute-start | bytes 172040 | tf_op jit(solution)/shard_map/ppermute | solution.py:49
  40.4 5.0 %collective-permute-start.21 = (f32[112,128]{1,0:T(8,128)S(1)}, f32[112,128]{1,0:T(8,128)S(1)}, u32[]{:S(2)}, u32[]{:S(2)}) collective-permute-start(f32[112,128]{1,0:T(8,128)S(1)} %add_add_fusion.2), channel_id=1, source_target_pairs={{0,192},{1,193},{2,194},{3,195},{4,196},{5,197},{6,198},{7,199},{8... | collective-permute-start | bytes 172040 | tf_op jit(solution)/shard_map/ppermute | solution.py:49
  41.2 4.3 %collective-permute-start.19 = (f32[112,128]{1,0:T(8,128)S(1)}, f32[112,128]{1,0:T(8,128)S(1)}, u32[]{:S(2)}, u32[]{:S(2)}) collective-permute-start(f32[112,128]{1,0:T(8,128)S(1)} %add_add_fusion.2), channel_id=1, source_target_pairs={{0,64},{1,65},{2,66},{3,67},{4,68},{5,69},{6,70},{7,71},{8,72},{9,... | collective-permute-start | bytes 172040 | tf_op jit(solution)/shard_map/ppermute | solution.py:49
  41.2 9.4 %collective-permute-start.6 = (f32[112,128]{1,0:T(8,128)S(1)}, f32[112,128]{1,0:T(8,128)S(1)}, u32[]{:S(2)}, u32[]{:S(2)}) collective-permute-start(f32[112,128]{1,0:T(8,128)S(1)} %bitcast_add_fusion.1), channel_id=1, source_target_pairs={{0,2},{1,3},{2,0},{3,1},{4,6},{5,7},{6,4},{7,5},{8,10},{9,11},{10,... | collective-permute-start | bytes 172040 | tf_op jit(solution)/shard_map/ppermute | solution.py:49
  44.5 6.3 %collective-permute-start.7 = (f32[112,128]{1,0:T(8,128)S(1)}, f32[112,128]{1,0:T(8,128)S(1)}, u32[]{:S(2)}, u32[]{:S(2)}) collective-permute-start(f32[112,128]{1,0:T(8,128)S(1)} %bitcast_add_fusion.1), channel_id=1, source_target_pairs={{0,3},{1,2},{2,1},{3,0},{4,7},{5,6},{6,5},{7,4},{8,11},{9,10},{10,... | collective-permute-start | bytes 172040 | tf_op jit(solution)/shard_map/ppermute | solution.py:49
  45.4 5.4 %collective-permute-start.5 = (f32[112,128]{1,0:T(8,128)S(1)}, f32[112,128]{1,0:T(8,128)S(1)}, u32[]{:S(2)}, u32[]{:S(2)}) collective-permute-start(f32[112,128]{1,0:T(8,128)S(1)} %bitcast_add_fusion.1), channel_id=1, source_target_pairs={{0,1},{1,0},{2,3},{3,2},{4,5},{5,4},{6,7},{7,6},{8,9},{9,8},{10,11... | collective-permute-start | bytes 172040 | tf_op jit(solution)/shard_map/ppermute | solution.py:49
  45.4 8.7 %collective-permute-start.23 = (f32[112,128]{1,0:T(8,128)S(1)}, f32[112,128]{1,0:T(8,128)S(1)}, u32[]{:S(2)}, u32[]{:S(2)}) collective-permute-start(f32[112,128]{1,0:T(8,128)S(1)} %add_add_fusion.1), channel_id=1, source_target_pairs={{0,8},{1,9},{2,10},{3,11},{4,12},{5,13},{6,14},{7,15},{8,0},{9,1},... | collective-permute-start | bytes 172040 | tf_op jit(solution)/shard_map/ppermute | solution.py:49
  49.1 5.5 %collective-permute-start.24 = (f32[112,128]{1,0:T(8,128)S(1)}, f32[112,128]{1,0:T(8,128)S(1)}, u32[]{:S(2)}, u32[]{:S(2)}) collective-permute-start(f32[112,128]{1,0:T(8,128)S(1)} %add_add_fusion.1), channel_id=1, source_target_pairs={{0,12},{1,13},{2,14},{3,15},{4,8},{5,9},{6,10},{7,11},{8,4},{9,5},... | collective-permute-start | bytes 172040 | tf_op jit(solution)/shard_map/ppermute | solution.py:49
  50.6 4.0 %collective-permute-start.22 = (f32[112,128]{1,0:T(8,128)S(1)}, f32[112,128]{1,0:T(8,128)S(1)}, u32[]{:S(2)}, u32[]{:S(2)}) collective-permute-start(f32[112,128]{1,0:T(8,128)S(1)} %add_add_fusion.1), channel_id=1, source_target_pairs={{0,4},{1,5},{2,6},{3,7},{4,0},{5,1},{6,2},{7,3},{8,12},{9,13},{10,... | collective-permute-start | bytes 172040 | tf_op jit(solution)/shard_map/ppermute | solution.py:49
  50.8 8.2 %collective-permute-start.9 = (f32[112,128]{1,0:T(8,128)S(1)}, f32[112,128]{1,0:T(8,128)S(1)}, u32[]{:S(2)}, u32[]{:S(2)}) collective-permute-start(f32[112,128]{1,0:T(8,128)S(1)} %add_add_fusion.5), channel_id=1, source_target_pairs={{0,128},{1,129},{2,130},{3,131},{4,132},{5,133},{6,134},{7,135},{8... | collective-permute-start | bytes 172040 | tf_op jit(solution)/shard_map/ppermute | solution.py:49
  53.3 5.7 %collective-permute-start.10 = (f32[112,128]{1,0:T(8,128)S(1)}, f32[112,128]{1,0:T(8,128)S(1)}, u32[]{:S(2)}, u32[]{:S(2)}) collective-permute-start(f32[112,128]{1,0:T(8,128)S(1)} %add_add_fusion.5), channel_id=1, source_target_pairs={{0,192},{1,193},{2,194},{3,195},{4,196},{5,197},{6,198},{7,199},{8... | collective-permute-start | bytes 172040 | tf_op jit(solution)/shard_map/ppermute | solution.py:49
  54.1 4.9 %collective-permute-start.8 = (f32[112,128]{1,0:T(8,128)S(1)}, f32[112,128]{1,0:T(8,128)S(1)}, u32[]{:S(2)}, u32[]{:S(2)}) collective-permute-start(f32[112,128]{1,0:T(8,128)S(1)} %add_add_fusion.5), channel_id=1, source_target_pairs={{0,64},{1,65},{2,66},{3,67},{4,68},{5,69},{6,70},{7,71},{8,72},{9,... | collective-permute-start | bytes 172040 | tf_op jit(solution)/shard_map/ppermute | solution.py:49
  54.6 8.3 %collective-permute-start.25 = (f32[112,128]{1,0:T(8,128)S(1)}, f32[112,128]{1,0:T(8,128)S(1)}, u32[]{:S(2)}, u32[]{:S(2)}) collective-permute-start(f32[112,128]{1,0:T(8,128)S(1)} %add_add_fusion), channel_id=1, source_target_pairs={{0,28},{1,29},{2,30},{3,31},{4,24},{5,25},{6,26},{7,27},{8,20},{9,... | collective-permute-start | bytes 172040 | tf_op jit(solution)/shard_map/ppermute | solution.py:49
  59.1 8.0 %collective-permute-start.12 = (f32[112,128]{1,0:T(8,128)S(1)}, f32[112,128]{1,0:T(8,128)S(1)}, u32[]{:S(2)}, u32[]{:S(2)}) collective-permute-start(f32[112,128]{1,0:T(8,128)S(1)} %add_add_fusion.4), channel_id=1, source_target_pairs={{0,8},{1,9},{2,10},{3,11},{4,12},{5,13},{6,14},{7,15},{8,0},{9,1},... | collective-permute-start | bytes 172040 | tf_op jit(solution)/shard_map/ppermute | solution.py:49
  61.3 5.8 %collective-permute-start.13 = (f32[112,128]{1,0:T(8,128)S(1)}, f32[112,128]{1,0:T(8,128)S(1)}, u32[]{:S(2)}, u32[]{:S(2)}) collective-permute-start(f32[112,128]{1,0:T(8,128)S(1)} %add_add_fusion.4), channel_id=1, source_target_pairs={{0,12},{1,13},{2,14},{3,15},{4,8},{5,9},{6,10},{7,11},{8,4},{9,5},... | collective-permute-start | bytes 172040 | tf_op jit(solution)/shard_map/ppermute | solution.py:49
  62.9 4.8 %collective-permute-start.11 = (f32[112,128]{1,0:T(8,128)S(1)}, f32[112,128]{1,0:T(8,128)S(1)}, u32[]{:S(2)}, u32[]{:S(2)}) collective-permute-start(f32[112,128]{1,0:T(8,128)S(1)} %add_add_fusion.4), channel_id=1, source_target_pairs={{0,4},{1,5},{2,6},{3,7},{4,0},{5,1},{6,2},{7,3},{8,12},{9,13},{10,... | collective-permute-start | bytes 172040 | tf_op jit(solution)/shard_map/ppermute | solution.py:49
  62.9 7.1 %collective-permute-start.26 = (f32[112,128]{1,0:T(8,128)S(1)}, f32[112,128]{1,0:T(8,128)S(1)}, u32[]{:S(2)}, u32[]{:S(2)}) collective-permute-start(f32[112,128]{1,0:T(8,128)S(1)} %add.92), channel_id=1, source_target_pairs={{0,32},{1,33},{2,34},{3,35},{4,36},{5,37},{6,38},{7,39},{8,40},{9,... | collective-permute-start | bytes 172040 | tf_op jit(solution)/shard_map/ppermute | solution.py:57
  67.8 9.0 %collective-permute-start.14 = (f32[112,128]{1,0:T(8,128)S(1)}, f32[112,128]{1,0:T(8,128)S(1)}, u32[]{:S(2)}, u32[]{:S(2)}) collective-permute-start(f32[112,128]{1,0:T(8,128)S(1)} %add_add_fusion.3), channel_id=1, source_target_pairs={{0,28},{1,29},{2,30},{3,31},{4,24},{5,25},{6,26},{7,27},{8,20},{9,... | collective-permute-start | bytes 172040 | tf_op jit(solution)/shard_map/ppermute | solution.py:49
  76.8 6.4 %collective-permute-start.27 = (f32[112,128]{1,0:T(8,128)S(1)}, f32[112,128]{1,0:T(8,128)S(1)}, u32[]{:S(2)}, u32[]{:S(2)}) collective-permute-start(f32[112,128]{1,0:T(8,128)S(1)} %add.93), channel_id=1, source_target_pairs={{0,32},{1,33},{2,34},{3,35},{4,36},{5,37},{6,38},{7,39},{8,40},{9,... | collective-permute-start | bytes 172040 | tf_op jit(solution)/shard_map/ppermute | solution.py:57

commit v5 on v4

--- a/solution.py
+++ b/solution.py
@@ -538,11 +538,11 @@
 
     for s in range(slabs):
         base = 16 * s
+        for g in (2 * s, 2 * s + 1):
+            group_copy(field_ref, smooth_ref, in_sems, g).wait()
         weights = weight_ref[base : base + 16, :].astype(F32)
         parts = []
         for pair in range(8):
-            if pair % 4 == 0:
-                group_copy(field_ref, smooth_ref, in_sems, 2 * s + pair // 4).wait()
             pieces = []
             for i in (2 * pair, 2 * pair + 1):
                 pieces.append((weights[i : i + 1, :] * (smooth_ref[base + i] - mean)).astype(BF16))

time: 91.9 us -> 91.9 us (level)
  no operation moved by 1% of the time
where the time goes in v5:
time: 91.9 us; the launch traced here: 91.7 us
  starting transfers between devices  54.2 us (59%)
  Pallas kernels  31.5 us (34%)
  local copies, waits for them, and re-layouts  2.56 us (3%)
  waiting for transfers between devices  2.11 us (2%)
  between operations  1.12 us (1%)
    ppermute x20, starting transfers between devices, total_of(): parts = [lax.ppermute(own, AXES, pairs) for pairs in stage]  33.1 us
    ppermute x2, starting transfers between devices, total_of(): other = lax.ppermute(own, AXES, CORE_SWAP)  9.7 us
    pallas_call x1, Pallas kernels, finish(): pl.pallas_call(finish_kernel, out_shape=(pltpu.HBM((bands, rows, cols), B...  8.21 us
    pallas_call x1, Pallas kernels, rows_first(): pl.pallas_call(rows_first_kernel, out_shape=(pltpu.HBM((rows, bands, cols...  7.99 us
    pallas_call x1, Pallas kernels, inverse_factor(): pl.pallas_call(factor_kernel, out_shape=jax.ShapeDtypeStruct((size, size)...  6.71 us
    pallas_call x1, Pallas kernels, signal_moments(): pl.pallas_call(signal_kernel, out_shape=(pltpu.HBM((rows, bands, cols), F...  6.62 us
    ppermute x1, starting transfers between devices, body(): up = lax.ppermute(last, 'tile', forward)  3.95 us
    ppermute x1, starting transfers between devices, body(): low = lax.ppermute(to_high, 'group', forward)  3.1 us
  transfers between devices with their start and end apart: 28, of which 3 were waited for; matrix products, arithmetic and copies ran while one was open for 0% of the time, Pallas kernels for 23%

profile of v5, /device:TPU:1, one launch (start us, length us, event | category | flops | bytes accessed | tf_op | source)
XLA Modules:
  0.0 91.7 jit_solution(10017964317446884053)
XLA Ops:
  0.6 1.6 %edge_rows.1 = (bf16[2,224,128]{2,1,0:T(8,128)(2,1)S(1)}, bf16[2,224,128]{2,1,0:T(8,128)(2,1)S(1)}) custom-call(bf16[224,96,128]{2,1,0:T(8,128)(2,1)} %x_ref.3), custom_call_target="tpu_custom_call" | custom-call | bytes 1835008 | tf_op jit(solution)/shard_map/edge_rows/pallas_call | solution.py:100
  2.2 4.0 %collective-permute-start = (bf16[2,224,128]{2,1,0:T(8,128)(2,1)S(1)}, bf16[2,224,128]{2,1,0:T(8,128)(2,1)S(1)}, u32[]{:S(2)}, u32[]{:S(2)}) collective-permute-start(bf16[2,224,128]{2,1,0:T(8,128)(2,1)S(1)} %get-tuple-element.16.bottom_ref), channel_id=1, source_target_pairs={{0,1},{1,2},{2,3},{3,4},{4,5},{5,6},{6,7},{7,8},{8,9},{9,10},{10,1... | collective-permute-start | bytes 344072 | tf_op jit(solution)/shard_map/ppermute | solution.py:592
  6.2 1.3 %collective-permute-start.1 = (bf16[2,224,128]{2,1,0:T(8,128)(2,1)S(1)}, bf16[2,224,128]{2,1,0:T(8,128)(2,1)S(1)}, u32[]{:S(2)}, u32[]{:S(2)}) collective-permute-start(bf16[2,224,128]{2,1,0:T(8,128)(2,1)S(1)} %get-tuple-element.17.top_ref), channel_id=1, source_target_pairs={{1,0},{2,1},{3,2},{4,3},{5,4},{6,5},{7,6},{8,7},{9,8},{10,9},{11,1... | collective-permute-start | bytes 344072 | tf_op jit(solution)/shard_map/ppermute | solution.py:593
  7.5 8.0 %rows_first.1 = (bf16[96,224,128]{2,1,0:T(8,128)(2,1)}, bf16[2,224,256]{2,1,0:T(8,128)(2,1)S(1)}, f32[224,224]{1,0:T(8,128)S(1)}, f32[224,128]{1,0:T(8,128)S(1)}) custom-call(bf16[224,96,128]{2,1,0:T(8,128)(2,1)} %x_ref.3, s32[96,128]{1,0:T(8,128)S(1)} %copy-done), custom_call_target="tpu_custom_call" | custom-call | flops 1233125376 | bytes 11010048 | tf_op jit(solution)/shard_map/rows_first/pallas_call | solution.py:201
  15.5 0.4 side_columns.1
  16.0 1.0 %collective-permute-start.15 = (f32[112,128]{1,0:T(8,128)S(1)}, f32[112,128]{1,0:T(8,128)S(1)}, u32[]{:S(2)}, u32[]{:S(2)}) collective-permute-start(f32[112,128]{1,0:T(8,128)S(1)} %select_bitcast_fusion.4), channel_id=1, source_target_pairs={{0,32},{1,33},{2,34},{3,35},{4,36},{5,37},{6,38},{7,39},{8,40},{9,... | collective-permute-start | bytes 172040 | tf_op jit(solution)/shard_map/ppermute | solution.py:47
  17.0 3.1 %collective-permute-start.2 = (bf16[224,256]{1,0:T(8,128)(2,1)S(1)}, bf16[224,256]{1,0:T(8,128)(2,1)S(1)}, u32[]{:S(2)}, u32[]{:S(2)}) collective-permute-start(bf16[224,256]{1,0:T(8,128)(2,1)S(1)} %get-tuple-element.21), channel_id=1, source_target_pairs={{0,32},{32,64},{64,96},{96,128},{128,160},{160,192},{192,224},{1,3... | collective-permute-start | bytes 344072 | tf_op jit(solution)/shard_map/ppermute | solution.py:599
  20.1 1.9 %collective-permute-start.3 = (bf16[224,256]{1,0:T(8,128)(2,1)S(1)}, bf16[224,256]{1,0:T(8,128)(2,1)S(1)}, u32[]{:S(2)}, u32[]{:S(2)}) collective-permute-start(bf16[224,256]{1,0:T(8,128)(2,1)S(1)} %get-tuple-element.22), channel_id=1, source_target_pairs={{32,0},{64,32},{96,64},{128,96},{160,128},{192,160},{224,192},{33,... | collective-permute-start | bytes 344072 | tf_op jit(solution)/shard_map/ppermute | solution.py:600
  22.1 4.0 %collective-permute-start.17 = (f32[112,128]{1,0:T(8,128)S(1)}, f32[112,128]{1,0:T(8,128)S(1)}, u32[]{:S(2)}, u32[]{:S(2)}) collective-permute-start(f32[112,128]{1,0:T(8,128)S(1)} %bitcast_add_fusion), channel_id=1, source_target_pairs={{0,2},{1,3},{2,0},{3,1},{4,6},{5,7},{6,4},{7,5},{8,10},{9,11},{10,... | collective-permute-start | bytes 172040 | tf_op jit(solution)/shard_map/ppermute | solution.py:49
  26.1 0.9 collective-permute-start.18
  27.0 2.6 %copy-done.1 = bf16[96,224,128]{2,1,0:T(8,128)(2,1)S(1)} copy-done((bf16[96,224,128]{2,1,0:T(8,128)(2,1)S(1)}, bf16[96,224,128]{2,1,0:T(8,128)(2,1)}, u32[]{:S(2)}) %copy-start.1) | copy-done | bytes 5505048
  29.5 6.6 %signal_moments.1 = (f32[96,224,128]{2,1,0:T(8,128)}, f32[2,112,128]{2,1,0:T(8,128)S(1)}) custom-call(bf16[96,224,128]{2,1,0:T(8,128)(2,1)S(1)} %copy-done.1, bf16[2,224,128]{2,1,0:T(8,128)(2,1)S(1)} %collective-permute-done.up_ref, bf16[2,224,128]{2,1,0:T(8,128)(2,1)S(1)} %collective-permute-done.1.down_ref, ...), custom_call_target="tpu_custom_call" | custom-call | flops 2466250752 | bytes 16515072 | tf_op jit(solution)/shard_map/signal_moments/pallas_call | solution.py:412
  36.3 4.1 %collective-permute-start.20 = (f32[112,128]{1,0:T(8,128)S(1)}, f32[112,128]{1,0:T(8,128)S(1)}, u32[]{:S(2)}, u32[]{:S(2)}) collective-permute-start(f32[112,128]{1,0:T(8,128)S(1)} %add_add_fusion.2), channel_id=1, source_target_pairs={{0,128},{1,129},{2,130},{3,131},{4,132},{5,133},{6,134},{7,135},{8... | collective-permute-start | bytes 172040 | tf_op jit(solution)/shard_map/ppermute | solution.py:49
  40.4 0.8 collective-permute-start.21
  41.2 3.4 %collective-permute-start.6 = (f32[112,128]{1,0:T(8,128)S(1)}, f32[112,128]{1,0:T(8,128)S(1)}, u32[]{:S(2)}, u32[]{:S(2)}) collective-permute-start(f32[112,128]{1,0:T(8,128)S(1)} %bitcast_add_fusion.1), channel_id=1, source_target_pairs={{0,2},{1,3},{2,0},{3,1},{4,6},{5,7},{6,4},{7,5},{8,10},{9,11},{10,... | collective-permute-start | bytes 172040 | tf_op jit(solution)/shard_map/ppermute | solution.py:49
  44.5 0.9 collective-permute-start.7
  45.4 3.7 %collective-permute-start.23 = (f32[112,128]{1,0:T(8,128)S(1)}, f32[112,128]{1,0:T(8,128)S(1)}, u32[]{:S(2)}, u32[]{:S(2)}) collective-permute-start(f32[112,128]{1,0:T(8,128)S(1)} %add_add_fusion.1), channel_id=1, source_target_pairs={{0,8},{1,9},{2,10},{3,11},{4,12},{5,13},{6,14},{7,15},{8,0},{9,1},... | collective-permute-start | bytes 172040 | tf_op jit(solution)/shard_map/ppermute | solution.py:49
  49.1 1.4 %collective-permute-start.24 = (f32[112,128]{1,0:T(8,128)S(1)}, f32[112,128]{1,0:T(8,128)S(1)}, u32[]{:S(2)}, u32[]{:S(2)}) collective-permute-start(f32[112,128]{1,0:T(8,128)S(1)} %add_add_fusion.1), channel_id=1, source_target_pairs={{0,12},{1,13},{2,14},{3,15},{4,8},{5,9},{6,10},{7,11},{8,4},{9,5},... | collective-permute-start | bytes 172040 | tf_op jit(solution)/shard_map/ppermute | solution.py:49
  50.6 0.2 collective-permute-start.22
  50.8 2.5 %collective-permute-start.9 = (f32[112,128]{1,0:T(8,128)S(1)}, f32[112,128]{1,0:T(8,128)S(1)}, u32[]{:S(2)}, u32[]{:S(2)}) collective-permute-start(f32[112,128]{1,0:T(8,128)S(1)} %add_add_fusion.5), channel_id=1, source_target_pairs={{0,128},{1,129},{2,130},{3,131},{4,132},{5,133},{6,134},{7,135},{8... | collective-permute-start | bytes 172040 | tf_op jit(solution)/shard_map/ppermute | solution.py:49
  53.3 0.8 collective-permute-start.10
  54.1 0.5 collective-permute-done.24
  54.6 4.4 %collective-permute-start.25 = (f32[112,128]{1,0:T(8,128)S(1)}, f32[112,128]{1,0:T(8,128)S(1)}, u32[]{:S(2)}, u32[]{:S(2)}) collective-permute-start(f32[112,128]{1,0:T(8,128)S(1)} %add_add_fusion), channel_id=1, source_target_pairs={{0,28},{1,29},{2,30},{3,31},{4,24},{5,25},{6,26},{7,27},{8,20},{9,... | collective-permute-start | bytes 172040 | tf_op jit(solution)/shard_map/ppermute | solution.py:49
  59.1 2.2 %collective-permute-start.12 = (f32[112,128]{1,0:T(8,128)S(1)}, f32[112,128]{1,0:T(8,128)S(1)}, u32[]{:S(2)}, u32[]{:S(2)}) collective-permute-start(f32[112,128]{1,0:T(8,128)S(1)} %add_add_fusion.4), channel_id=1, source_target_pairs={{0,8},{1,9},{2,10},{3,11},{4,12},{5,13},{6,14},{7,15},{8,0},{9,1},... | collective-permute-start | bytes 172040 | tf_op jit(solution)/shard_map/ppermute | solution.py:49
  61.3 1.6 %collective-permute-start.13 = (f32[112,128]{1,0:T(8,128)S(1)}, f32[112,128]{1,0:T(8,128)S(1)}, u32[]{:S(2)}, u32[]{:S(2)}) collective-permute-start(f32[112,128]{1,0:T(8,128)S(1)} %add_add_fusion.4), channel_id=1, source_target_pairs={{0,12},{1,13},{2,14},{3,15},{4,8},{5,9},{6,10},{7,11},{8,4},{9,5},... | collective-permute-start | bytes 172040 | tf_op jit(solution)/shard_map/ppermute | solution.py:49
  62.9 4.2 %collective-permute-start.26 = (f32[112,128]{1,0:T(8,128)S(1)}, f32[112,128]{1,0:T(8,128)S(1)}, u32[]{:S(2)}, u32[]{:S(2)}) collective-permute-start(f32[112,128]{1,0:T(8,128)S(1)} %add.92), channel_id=1, source_target_pairs={{0,32},{1,33},{2,34},{3,35},{4,36},{5,37},{6,38},{7,39},{8,40},{9,... | collective-permute-start | bytes 172040 | tf_op jit(solution)/shard_map/ppermute | solution.py:57
  67.1 0.7 collective-permute-done.11
  67.8 2.3 %collective-permute-start.14 = (f32[112,128]{1,0:T(8,128)S(1)}, f32[112,128]{1,0:T(8,128)S(1)}, u32[]{:S(2)}, u32[]{:S(2)}) collective-permute-start(f32[112,128]{1,0:T(8,128)S(1)} %add_add_fusion.3), channel_id=1, source_target_pairs={{0,28},{1,29},{2,30},{3,31},{4,24},{5,25},{6,26},{7,27},{8,20},{9,... | collective-permute-start | bytes 172040 | tf_op jit(solution)/shard_map/ppermute | solution.py:49
  70.1 6.7 %inverse_factor.1.inverse_ref = f32[224,224]{1,0:T(8,128)S(1)} custom-call(f32[2,112,128]{2,1,0:T(8,128)S(1)} %pad_maximum_fusion.noise_ref), custom_call_target="tpu_custom_call" | custom-call | flops 4495769600 | bytes 401408 | tf_op jit(solution)/shard_map/inverse_factor/pallas_call | solution.py:504
  76.8 5.5 %collective-permute-start.27 = (f32[112,128]{1,0:T(8,128)S(1)}, f32[112,128]{1,0:T(8,128)S(1)}, u32[]{:S(2)}, u32[]{:S(2)}) collective-permute-start(f32[112,128]{1,0:T(8,128)S(1)} %add.93), channel_id=1, source_target_pairs={{0,32},{1,33},{2,34},{3,35},{4,36},{5,37},{6,38},{7,39},{8,40},{9,... | collective-permute-start | bytes 172040 | tf_op jit(solution)/shard_map/ppermute | solution.py:57
  82.4 0.9 collective-permute-done.27
  83.3 8.2 %finish.1 = (bf16[224,96,128]{2,1,0:T(8,128)(2,1)}, f32[224,224]{1,0:T(8,128)}) custom-call(f32[224,224]{1,0:T(8,128)S(1)} %inverse_factor.1.inverse_ref, f32[2,112,128]{2,1,0:T(8,128)S(1)} %pad_maximum_fusion.1.signal_ref, s32[96,128]{1,0:T(8,128)S(1)} %copy-done, f32[96,224,128]{2,1,0:T(8,128)} %get-tuple-element.27.field_ref), custom_call_target="tpu_custom_call" | custom-call | flops 1233125376 | bytes 16515072 | tf_op jit(solution)/shard_map/finish/pallas_call | solution.py:564
  (50 shorter events, 0.4 us)
Async XLA Ops:
  0.6 6.9 %copy-start = (s32[96,128]{1,0:T(8,128)S(1)}, s32[96,128]{1,0:T(8,128)}, u32[]{:S(2)}) copy-start(s32[96,128]{1,0:T(8,128)} %weight_ref.7) | copy-start | bytes 147460
  2.2 13.3 %collective-permute-start = (bf16[2,224,128]{2,1,0:T(8,128)(2,1)S(1)}, bf16[2,224,128]{2,1,0:T(8,128)(2,1)S(1)}, u32[]{:S(2)}, u32[]{:S(2)}) collective-permute-start(bf16[2,224,128]{2,1,0:T(8,128)(2,1)S(1)} %get-tuple-element.16.bottom_ref), channel_id=1, source_target_pairs={{0,1},{1,2},{2,3},{3,4},{4,5},{5,6},{6,7},{7,8},{8,9},{9,10},{10,1... | collective-permute-start | bytes 344072 | tf_op jit(solution)/shard_map/ppermute | solution.py:592
  6.2 9.3 %collective-permute-start.1 = (bf16[2,224,128]{2,1,0:T(8,128)(2,1)S(1)}, bf16[2,224,128]{2,1,0:T(8,128)(2,1)S(1)}, u32[]{:S(2)}, u32[]{:S(2)}) collective-permute-start(bf16[2,224,128]{2,1,0:T(8,128)(2,1)S(1)} %get-tuple-element.17.top_ref), channel_id=1, source_target_pairs={{1,0},{2,1},{3,2},{4,3},{5,4},{6,5},{7,6},{8,7},{9,8},{10,9},{11,1... | collective-permute-start | bytes 344072 | tf_op jit(solution)/shard_map/ppermute | solution.py:593
  16.0 6.1 %collective-permute-start.15 = (f32[112,128]{1,0:T(8,128)S(1)}, f32[112,128]{1,0:T(8,128)S(1)}, u32[]{:S(2)}, u32[]{:S(2)}) collective-permute-start(f32[112,128]{1,0:T(8,128)S(1)} %select_bitcast_fusion.4), channel_id=1, source_target_pairs={{0,32},{1,33},{2,34},{3,35},{4,36},{5,37},{6,38},{7,39},{8,40},{9,... | collective-permute-start | bytes 172040 | tf_op jit(solution)/shard_map/ppermute | solution.py:47
  17.0 9.9 %collective-permute-start.2 = (bf16[224,256]{1,0:T(8,128)(2,1)S(1)}, bf16[224,256]{1,0:T(8,128)(2,1)S(1)}, u32[]{:S(2)}, u32[]{:S(2)}) collective-permute-start(bf16[224,256]{1,0:T(8,128)(2,1)S(1)} %get-tuple-element.21), channel_id=1, source_target_pairs={{0,32},{32,64},{64,96},{96,128},{128,160},{160,192},{192,224},{1,3... | collective-permute-start | bytes 344072 | tf_op jit(solution)/shard_map/ppermute | solution.py:599
  20.1 6.8 %collective-permute-start.3 = (bf16[224,256]{1,0:T(8,128)(2,1)S(1)}, bf16[224,256]{1,0:T(8,128)(2,1)S(1)}, u32[]{:S(2)}, u32[]{:S(2)}) collective-permute-start(bf16[224,256]{1,0:T(8,128)(2,1)S(1)} %get-tuple-element.22), channel_id=1, source_target_pairs={{32,0},{64,32},{96,64},{128,96},{160,128},{192,160},{224,192},{33,... | collective-permute-start | bytes 344072 | tf_op jit(solution)/shard_map/ppermute | solution.py:600
  22.1 14.2 %collective-permute-start.17 = (f32[112,128]{1,0:T(8,128)S(1)}, f32[112,128]{1,0:T(8,128)S(1)}, u32[]{:S(2)}, u32[]{:S(2)}) collective-permute-start(f32[112,128]{1,0:T(8,128)S(1)} %bitcast_add_fusion), channel_id=1, source_target_pairs={{0,2},{1,3},{2,0},{3,1},{4,6},{5,7},{6,4},{7,5},{8,10},{9,11},{10,... | collective-permute-start | bytes 172040 | tf_op jit(solution)/shard_map/ppermute | solution.py:49
  26.1 10.2 %collective-permute-start.18 = (f32[112,128]{1,0:T(8,128)S(1)}, f32[112,128]{1,0:T(8,128)S(1)}, u32[]{:S(2)}, u32[]{:S(2)}) collective-permute-start(f32[112,128]{1,0:T(8,128)S(1)} %bitcast_add_fusion), channel_id=1, source_target_pairs={{0,3},{1,2},{2,1},{3,0},{4,7},{5,6},{6,5},{7,4},{8,11},{9,10},{10,... | collective-permute-start | bytes 172040 | tf_op jit(solution)/shard_map/ppermute | solution.py:49
  26.9 9.3 %collective-permute-start.16 = (f32[112,128]{1,0:T(8,128)S(1)}, f32[112,128]{1,0:T(8,128)S(1)}, u32[]{:S(2)}, u32[]{:S(2)}) collective-permute-start(f32[112,128]{1,0:T(8,128)S(1)} %bitcast_add_fusion), channel_id=1, source_target_pairs={{0,1},{1,0},{2,3},{3,2},{4,5},{5,4},{6,7},{7,6},{8,9},{9,8},{10,11... | collective-permute-start | bytes 172040 | tf_op jit(solution)/shard_map/ppermute | solution.py:49
  26.9 2.6 %copy-start.1 = (bf16[96,224,128]{2,1,0:T(8,128)(2,1)S(1)}, bf16[96,224,128]{2,1,0:T(8,128)(2,1)}, u32[]{:S(2)}) copy-start(bf16[96,224,128]{2,1,0:T(8,128)(2,1)} %get-tuple-element.15.xt_ref) | copy-start | bytes 16515076
  36.1 5.0 %collective-permute-start.4 = (f32[112,128]{1,0:T(8,128)S(1)}, f32[112,128]{1,0:T(8,128)S(1)}, u32[]{:S(2)}, u32[]{:S(2)}) collective-permute-start(f32[112,128]{1,0:T(8,128)S(1)} %select_bitcast_fusion.5), channel_id=1, source_target_pairs={{0,32},{1,33},{2,34},{3,35},{4,36},{5,37},{6,38},{7,39},{8,40},{9,... | collective-permute-start | bytes 172040 | tf_op jit(solution)/shard_map/ppermute | solution.py:47
  36.3 9.1 %collective-permute-start.20 = (f32[112,128]{1,0:T(8,128)S(1)}, f32[112,128]{1,0:T(8,128)S(1)}, u32[]{:S(2)}, u32[]{:S(2)}) collective-permute-start(f32[112,128]{1,0:T(8,128)S(1)} %add_add_fusion.2), channel_id=1, source_target_pairs={{0,128},{1,129},{2,130},{3,131},{4,132},{5,133},{6,134},{7,135},{8... | collective-permute-start | bytes 172040 | tf_op jit(solution)/shard_map/ppermute | solution.py:49
  40.4 5.0 %collective-permute-start.21 = (f32[112,128]{1,0:T(8,128)S(1)}, f32[112,128]{1,0:T(8,128)S(1)}, u32[]{:S(2)}, u32[]{:S(2)}) collective-permute-start(f32[112,128]{1,0:T(8,128)S(1)} %add_add_fusion.2), channel_id=1, source_target_pairs={{0,192},{1,193},{2,194},{3,195},{4,196},{5,197},{6,198},{7,199},{8... | collective-permute-start | bytes 172040 | tf_op jit(solution)/shard_map/ppermute | solution.py:49
  41.2 4.3 %collective-permute-start.19 = (f32[112,128]{1,0:T(8,128)S(1)}, f32[112,128]{1,0:T(8,128)S(1)}, u32[]{:S(2)}, u32[]{:S(2)}) collective-permute-start(f32[112,128]{1,0:T(8,128)S(1)} %add_add_fusion.2), channel_id=1, source_target_pairs={{0,64},{1,65},{2,66},{3,67},{4,68},{5,69},{6,70},{7,71},{8,72},{9,... | collective-permute-start | bytes 172040 | tf_op jit(solution)/shard_map/ppermute | solution.py:49
  41.2 9.4 %collective-permute-start.6 = (f32[112,128]{1,0:T(8,128)S(1)}, f32[112,128]{1,0:T(8,128)S(1)}, u32[]{:S(2)}, u32[]{:S(2)}) collective-permute-start(f32[112,128]{1,0:T(8,128)S(1)} %bitcast_add_fusion.1), channel_id=1, source_target_pairs={{0,2},{1,3},{2,0},{3,1},{4,6},{5,7},{6,4},{7,5},{8,10},{9,11},{10,... | collective-permute-start | bytes 172040 | tf_op jit(solution)/shard_map/ppermute | solution.py:49
  44.5 6.3 %collective-permute-start.7 = (f32[112,128]{1,0:T(8,128)S(1)}, f32[112,128]{1,0:T(8,128)S(1)}, u32[]{:S(2)}, u32[]{:S(2)}) collective-permute-start(f32[112,128]{1,0:T(8,128)S(1)} %bitcast_add_fusion.1), channel_id=1, source_target_pairs={{0,3},{1,2},{2,1},{3,0},{4,7},{5,6},{6,5},{7,4},{8,11},{9,10},{10,... | collective-permute-start | bytes 172040 | tf_op jit(solution)/shard_map/ppermute | solution.py:49
  45.4 5.4 %collective-permute-start.5 = (f32[112,128]{1,0:T(8,128)S(1)}, f32[112,128]{1,0:T(8,128)S(1)}, u32[]{:S(2)}, u32[]{:S(2)}) collective-permute-start(f32[112,128]{1,0:T(8,128)S(1)} %bitcast_add_fusion.1), channel_id=1, source_target_pairs={{0,1},{1,0},{2,3},{3,2},{4,5},{5,4},{6,7},{7,6},{8,9},{9,8},{10,11... | collective-permute-start | bytes 172040 | tf_op jit(solution)/shard_map/ppermute | solution.py:49
  45.4 8.7 %collective-permute-start.23 = (f32[112,128]{1,0:T(8,128)S(1)}, f32[112,128]{1,0:T(8,128)S(1)}, u32[]{:S(2)}, u32[]{:S(2)}) collective-permute-start(f32[112,128]{1,0:T(8,128)S(1)} %add_add_fusion.1), channel_id=1, source_target_pairs={{0,8},{1,9},{2,10},{3,11},{4,12},{5,13},{6,14},{7,15},{8,0},{9,1},... | collective-permute-start | bytes 172040 | tf_op jit(solution)/shard_map/ppermute | solution.py:49
  49.1 5.5 %collective-permute-start.24 = (f32[112,128]{1,0:T(8,128)S(1)}, f32[112,128]{1,0:T(8,128)S(1)}, u32[]{:S(2)}, u32[]{:S(2)}) collective-permute-start(f32[112,128]{1,0:T(8,128)S(1)} %add_add_fusion.1), channel_id=1, source_target_pairs={{0,12},{1,13},{2,14},{3,15},{4,8},{5,9},{6,10},{7,11},{8,4},{9,5},... | collective-permute-start | bytes 172040 | tf_op jit(solution)/shard_map/ppermute | solution.py:49
  50.6 4.0 %collective-permute-start.22 = (f32[112,128]{1,0:T(8,128)S(1)}, f32[112,128]{1,0:T(8,128)S(1)}, u32[]{:S(2)}, u32[]{:S(2)}) collective-permute-start(f32[112,128]{1,0:T(8,128)S(1)} %add_add_fusion.1), channel_id=1, source_target_pairs={{0,4},{1,5},{2,6},{3,7},{4,0},{5,1},{6,2},{7,3},{8,12},{9,13},{10,... | collective-permute-start | bytes 172040 | tf_op jit(solution)/shard_map/ppermute | solution.py:49
  50.8 8.2 %collective-permute-start.9 = (f32[112,128]{1,0:T(8,128)S(1)}, f32[112,128]{1,0:T(8,128)S(1)}, u32[]{:S(2)}, u32[]{:S(2)}) collective-permute-start(f32[112,128]{1,0:T(8,128)S(1)} %add_add_fusion.5), channel_id=1, source_target_pairs={{0,128},{1,129},{2,130},{3,131},{4,132},{5,133},{6,134},{7,135},{8... | collective-permute-start | bytes 172040 | tf_op jit(solution)/shard_map/ppermute | solution.py:49
  53.3 5.7 %collective-permute-start.10 = (f32[112,128]{1,0:T(8,128)S(1)}, f32[112,128]{1,0:T(8,128)S(1)}, u32[]{:S(2)}, u32[]{:S(2)}) collective-permute-start(f32[112,128]{1,0:T(8,128)S(1)} %add_add_fusion.5), channel_id=1, source_target_pairs={{0,192},{1,193},{2,194},{3,195},{4,196},{5,197},{6,198},{7,199},{8... | collective-permute-start | bytes 172040 | tf_op jit(solution)/shard_map/ppermute | solution.py:49
  54.1 4.9 %collective-permute-start.8 = (f32[112,128]{1,0:T(8,128)S(1)}, f32[112,128]{1,0:T(8,128)S(1)}, u32[]{:S(2)}, u32[]{:S(2)}) collective-permute-start(f32[112,128]{1,0:T(8,128)S(1)} %add_add_fusion.5), channel_id=1, source_target_pairs={{0,64},{1,65},{2,66},{3,67},{4,68},{5,69},{6,70},{7,71},{8,72},{9,... | collective-permute-start | bytes 172040 | tf_op jit(solution)/shard_map/ppermute | solution.py:49
  54.6 8.3 %collective-permute-start.25 = (f32[112,128]{1,0:T(8,128)S(1)}, f32[112,128]{1,0:T(8,128)S(1)}, u32[]{:S(2)}, u32[]{:S(2)}) collective-permute-start(f32[112,128]{1,0:T(8,128)S(1)} %add_add_fusion), channel_id=1, source_target_pairs={{0,28},{1,29},{2,30},{3,31},{4,24},{5,25},{6,26},{7,27},{8,20},{9,... | collective-permute-start | bytes 172040 | tf_op jit(solution)/shard_map/ppermute | solution.py:49
  59.1 8.0 %collective-permute-start.12 = (f32[112,128]{1,0:T(8,128)S(1)}, f32[112,128]{1,0:T(8,128)S(1)}, u32[]{:S(2)}, u32[]{:S(2)}) collective-permute-start(f32[112,128]{1,0:T(8,128)S(1)} %add_add_fusion.4), channel_id=1, source_target_pairs={{0,8},{1,9},{2,10},{3,11},{4,12},{5,13},{6,14},{7,15},{8,0},{9,1},... | collective-permute-start | bytes 172040 | tf_op jit(solution)/shard_map/ppermute | solution.py:49
  61.3 5.8 %collective-permute-start.13 = (f32[112,128]{1,0:T(8,128)S(1)}, f32[112,128]{1,0:T(8,128)S(1)}, u32[]{:S(2)}, u32[]{:S(2)}) collective-permute-start(f32[112,128]{1,0:T(8,128)S(1)} %add_add_fusion.4), channel_id=1, source_target_pairs={{0,12},{1,13},{2,14},{3,15},{4,8},{5,9},{6,10},{7,11},{8,4},{9,5},... | collective-permute-start | bytes 172040 | tf_op jit(solution)/shard_map/ppermute | solution.py:49
  62.9 4.8 %collective-permute-start.11 = (f32[112,128]{1,0:T(8,128)S(1)}, f32[112,128]{1,0:T(8,128)S(1)}, u32[]{:S(2)}, u32[]{:S(2)}) collective-permute-start(f32[112,128]{1,0:T(8,128)S(1)} %add_add_fusion.4), channel_id=1, source_target_pairs={{0,4},{1,5},{2,6},{3,7},{4,0},{5,1},{6,2},{7,3},{8,12},{9,13},{10,... | collective-permute-start | bytes 172040 | tf_op jit(solution)/shard_map/ppermute | solution.py:49
  62.9 7.1 %collective-permute-start.26 = (f32[112,128]{1,0:T(8,128)S(1)}, f32[112,128]{1,0:T(8,128)S(1)}, u32[]{:S(2)}, u32[]{:S(2)}) collective-permute-start(f32[112,128]{1,0:T(8,128)S(1)} %add.92), channel_id=1, source_target_pairs={{0,32},{1,33},{2,34},{3,35},{4,36},{5,37},{6,38},{7,39},{8,40},{9,... | collective-permute-start | bytes 172040 | tf_op jit(solution)/shard_map/ppermute | solution.py:57
  67.8 9.0 %collective-permute-start.14 = (f32[112,128]{1,0:T(8,128)S(1)}, f32[112,128]{1,0:T(8,128)S(1)}, u32[]{:S(2)}, u32[]{:S(2)}) collective-permute-start(f32[112,128]{1,0:T(8,128)S(1)} %add_add_fusion.3), channel_id=1, source_target_pairs={{0,28},{1,29},{2,30},{3,31},{4,24},{5,25},{6,26},{7,27},{8,20},{9,... | collective-permute-start | bytes 172040 | tf_op jit(solution)/shard_map/ppermute | solution.py:49
  76.8 6.4 %collective-permute-start.27 = (f32[112,128]{1,0:T(8,128)S(1)}, f32[112,128]{1,0:T(8,128)S(1)}, u32[]{:S(2)}, u32[]{:S(2)}) collective-permute-start(f32[112,128]{1,0:T(8,128)S(1)} %add.93), channel_id=1, source_target_pairs={{0,32},{1,33},{2,34},{3,35},{4,36},{5,37},{6,38},{7,39},{8,40},{9,... | collective-permute-start | bytes 172040 | tf_op jit(solution)/shard_map/ppermute | solution.py:57
